TPU v7x, 256 devices: a whole 4x4x8 slice. The times are simulated.
256 devices in a mesh: pipe: 4 (over z_lo), expert: 64 (over x, z_hi, y, core).
Axes of the slice: x: 4, y: 4, z: 8 (z_hi: 2, z_lo: 4; z = z_hi * 4 + z_lo), core: 2. Of those that a mesh axis runs over, the one named last changes fastest.
Arguments:
- forward_input: bfloat16 [4, 8192, 2048], P('pipe', 'expert'), may hold values from -6 to 6
- queries: bfloat16 [4, 8192, 2048], P('pipe', 'expert'), may hold values from -100 to 100
- new_keys: bfloat16 [4, 8192, 256], P('pipe', 'expert'), may hold values from -6 to 6
- new_values: bfloat16 [4, 8192, 256], P('pipe', 'expert'), may hold values from -6 to 6
- cache_keys: bfloat16 [4, 8192, 256], P('pipe', 'expert'), may hold values from -6 to 6
- cache_values: bfloat16 [4, 8192, 256], P('pipe', 'expert'), may hold values from -6 to 6
- context_lengths: int32 [4, 64], P('pipe', 'expert'), may hold values from 1 to 128
- norm_gain: float32 [4, 2048], P('pipe'), may hold values from 0.5 to 1.5
- router: bfloat16 [4, 2048, 64], P('pipe'), may hold values from -0.125 to 0.125
- gate_weight: bfloat16 [4, 64, 2048, 768], P('pipe', 'expert'), may hold values from -0.125 to 0.125
- up_weight: bfloat16 [4, 64, 2048, 768], P('pipe', 'expert'), may hold values from -0.125 to 0.125
- down_weight: bfloat16 [4, 64, 768, 2048], P('pipe', 'expert'), may hold values from -0.21875 to 0.21875
- forward_ids: int32 [4, 8192, 4], P('pipe', 'expert'), may hold values from 0 to 63, all different within a row; in each aligned block of 128 rows (0 to 127, 128 to 255, ..., all dimensions but the last counted through in order) at most 9 rows name the same one
- backward_input: bfloat16 [4, 8192, 2048], P('pipe', 'expert'), may hold values from -6 to 6
- backward_ids: int32 [4, 8192, 4], P('pipe', 'expert'), may hold values from 0 to 63, all different within a row; in each aligned block of 128 rows (0 to 127, 128 to 255, ..., all dimensions but the last counted through in order) at most 9 rows name the same one
- output_grad: bfloat16 [4, 8192, 2048], P('pipe', 'expert'), may hold values from -16 to 16
Outputs:
- forward_output: bfloat16 [4, 8192, 2048], P('pipe', 'expert')
- input_grad: bfloat16 [4, 8192, 2048], P('pipe', 'expert')
- router_grad: float32 [4, 2048, 64], P('pipe', 'expert')
- gain_grad: float32 [4, 2048], P('pipe', 'expert')
Inputs may be any that keep to these rules, and one draw needn't show every extreme that they name: `forward_ids`: each row names 4 different experts; in the 128 rows of one device no expert is named more than 9 times, and on some devices one is named exactly 9 times. `backward_ids`: each row names 4 different experts; in the 128 rows of one device no expert is named more than 9 times, and on some devices one is named exactly 9 times.
All inputs are finite; a program needn't handle non-finite values.
Results may differ from a plain program's by a relative error of at most 0.012.
Values may be sent and summed in bfloat16 or wider, within the bound.
No kernel may reach another device: no remote copies, remote signals or barrier semaphores. Data moves between devices by JAX's collectives and lax.ppermute only.
A program may use at most 128 MiB of HBM per device.

v0:
```python
import jax
import jax.numpy as jnp
from jax import lax
from jax.experimental import pallas as pl
from jax.experimental.pallas import tpu as pltpu
from jax.sharding import Mesh, PartitionSpec as P


HEADS = 16
KV_HEADS = 2
HEAD_DIM = 128
D = 2048
FF = 768
EXPERTS = 64
MOST = 9
TOK = 128
PEERS = 32
SLOTS = PEERS * MOST
ROWS = MOST * 8
AREA = SLOTS * 8
XY = ("x", "y", "core")
ALL = ("x", "zh", "y", "core")

epsilon = 1e-06
far_below = -1e30
factor = 8192 ** (-0.5)
bf16 = jnp.bfloat16
f32 = jnp.float32
ACROSS = (((1,), (1,)), ((), ()))
DOWN = (((0,), (0,)), ((), ()))
VMEM = pl.BlockSpec(memory_space=pltpu.VMEM)
SMEM = pl.BlockSpec(memory_space=pltpu.SMEM)
HBM = pl.BlockSpec(memory_space=pltpu.HBM)


def spread_out(x):
    return lax.all_to_all(x, XY, 0, 0, tiled=True)


def swapped(x):
    return lax.ppermute(x, "zh", [(0, 1), (1, 0)])


def moved(x, same, step):
    pairs = []
    for pipe in range(4):
        for zh in range(2):
            to = ((pipe + step) % 4) * 2 + (zh if same else 1 - zh)
            pairs.append((pipe * 2 + zh, to))
    return lax.ppermute(x, ("pipe", "zh"), pairs)


def shape(dims, dtype=bf16):
    return jax.ShapeDtypeStruct(dims, dtype)


def call(kernel, outs, ins, scratch, args, flops, mib):
    return pl.pallas_call(
        kernel,
        out_shape=outs,
        in_specs=ins,
        out_specs=tuple(VMEM for _ in outs),
        scratch_shapes=scratch,
        compiler_params=pltpu.CompilerParams(vmem_limit_bytes=63 * 2**20),
        cost_estimate=pl.CostEstimate(
            flops=flops, transcendentals=0, bytes_accessed=mib * 2**20
        ),
    )(*args)


def dot(a, b, dims=None):
    if dims is None:
        return jnp.dot(a, b, preferred_element_type=f32)
    return lax.dot_general(a, b, dims, preferred_element_type=f32)


def iota(dims, dim):
    return lax.broadcasted_iota(jnp.int32, dims, dim)


def marks(cond):
    return cond.astype(f32).astype(bf16)


def unit_rows(x):
    wide = x.astype(f32)
    inv_rms = lax.rsqrt(jnp.mean(wide * wide, axis=-1, keepdims=True) + epsilon)
    return inv_rms, wide * inv_rms


def hits(ids):
    expert = iota((EXPERTS, ids.shape[1]), 0)
    hit = ids[0:1, :] == expert
    for k in range(1, 4):
        hit = hit | (ids[k : k + 1, :] == expert)
    return hit


def choice(normed, table, hit):
    logits = jnp.where(hit, dot(table, normed, ACROSS), far_below)
    lifted = jnp.where(hit, jnp.exp(logits - jnp.max(logits, axis=0, keepdims=True)), 0.0)
    return lifted / jnp.sum(lifted, axis=0, keepdims=True)


def ranked(hit):
    tokens = hit.shape[1]
    earlier, later = iota((tokens, tokens), 0), iota((tokens, tokens), 1)
    before = marks((earlier < later) & (earlier // TOK == later // TOK))
    hit = hit.astype(f32)
    return (hit * (dot(hit.astype(bf16), before) + 1.0)).astype(bf16)


def picks(peer, zh):
    owner = (peer // 8) * 16 + zh * 8 + peer % 8
    return marks(owner == iota(peer.shape, 1))


def each_peer(step):
    def turn(d, carry):
        step(d, pl.ds(pl.multiple_of(d * ROWS, 8), ROWS))
        return carry

    lax.fori_loop(0, PEERS, turn, 0)


def area_rows(d, area):
    return pl.ds(pl.multiple_of(d * ROWS + area * AREA, 8), ROWS)


LANES = (pl.ds(0, 128), pl.ds(128, 128))


def put_rows(wide_ref, j, rows, start=0):
    for lane in range(rows.shape[1] // 128):
        wide_ref[lane, pl.ds(start + j, rows.shape[0], stride=8), :] = rows[
            :, lane * 128 : lane * 128 + 128
        ]


def get_rows(wide_ref, j, count, start=0):
    return jnp.concatenate(
        [
            wide_ref[lane, pl.ds(start + j, count, stride=8), :].astype(bf16)
            for lane in range(wide_ref.shape[0])
        ],
        axis=1,
    )


def routed(ids, x, zh, gain, table):
    hit = hits(ids)
    _, unit = unit_rows(x)
    normed = (unit * gain).astype(bf16)
    probs = choice(normed, table, hit)
    pick = picks(iota((SLOTS, EXPERTS), 0) // MOST, zh)
    slot = (iota((SLOTS, TOK), 0) % MOST + 1).astype(f32)
    return normed, probs, pick, marks(dot(pick, ranked(hit)) == slot)


def mixed_by(onehot, pick, probs):
    return onehot * dot(pick, probs.astype(bf16)).astype(bf16)


def loop(count, step):
    def turn(i, carry):
        step(i)
        return carry

    lax.fori_loop(0, count, turn, 0)


def columns(j, width):
    return pl.ds(pl.multiple_of(j * width, width), width)


def fill_looped(wide_ref, area, onehot_ref, rows_ref):
    def step(j):
        put_rows(wide_ref, j, dot(onehot_ref[...], rows_ref[:, columns(j, 256)]), area * AREA)

    loop(8, step)


def fill(wide_ref, area, onehot, rows_ref):
    for j in range(8):
        put_rows(wide_ref, j, dot(onehot, rows_ref[:, pl.ds(j * 256, 256)]), area * AREA)


def give(wide_ref, sent_ref, areas):
    def step(d, rows):
        for area in range(areas):
            for lane in range(2):
                sent_ref[d, pl.ds(area * ROWS, ROWS), LANES[lane]] = wide_ref[lane, area_rows(d, area), :].astype(bf16)

    each_peer(step)


def near_pack(
    zh_ref, ids_ref, ahead_ids_ref, x_ref, g_ref, resid_ref, gain_ref, table_ref,
    sent_ref, normed_ref, onehot_ref, probs_ref, mix_ref, wide_ref, rows_ref
):
    zh, gain, table = zh_ref[0], gain_ref[...], table_ref[...]
    normed_ref[...], probs_ref[...], _, onehot_ref[...] = routed(ids_ref[...], x_ref[...], zh, gain, table)
    fill(wide_ref, 0, onehot_ref[...], normed_ref)
    fill(wide_ref, 1, onehot_ref[...], g_ref)
    rows_ref[...], probs, pick, onehot = routed(ahead_ids_ref[...], resid_ref[...], zh, gain, table)
    mix_ref[...] = mixed_by(onehot, pick, probs)
    fill(wide_ref, 2, onehot, rows_ref)
    give(wide_ref, sent_ref, 3)


def run_near_pack(*args):
    return call(
        near_pack,
        (
            shape((PEERS, 3 * ROWS, 256)),
            shape((TOK, D)),
            shape((SLOTS, TOK)),
            shape((EXPERTS, TOK), f32),
            shape((SLOTS, TOK)),
        ),
        [SMEM] + [VMEM] * 7,
        [pltpu.VMEM((2, 3 * AREA, 128), f32), pltpu.VMEM((TOK, D), bf16)],
        args,
        2 * 10**9,
        8,
    )


def far_pack(
    zh_ref, ids_ref, x_ref, g_ref, gain_ref, table_ref, sent_ref, normed_ref, onehot_ref, probs_ref, wide_ref
):
    normed_ref[...], probs_ref[...], _, onehot_ref[...] = routed(
        ids_ref[...], x_ref[...], zh_ref[0], gain_ref[...], table_ref[...]
    )
    fill_looped(wide_ref, 0, onehot_ref, normed_ref)
    fill_looped(wide_ref, 1, onehot_ref, g_ref)
    give(wide_ref, sent_ref, 2)


def run_far_pack(*args):
    return call(
        far_pack,
        (shape((PEERS, 2 * ROWS, 256)), shape((TOK, D)), shape((SLOTS, TOK)), shape((EXPERTS, TOK), f32)),
        [SMEM] + [VMEM] * 5,
        [pltpu.VMEM((2, 2 * AREA, 128), f32)],
        args,
        10**9,
        6,
    )


def ahead_pack(zh_ref, ids_ref, x_ref, gain_ref, table_ref, sent_ref, mix_ref, wide_ref, rows_ref, onehot_ref):
    rows_ref[...], probs, pick, onehot = routed(ids_ref[...], x_ref[...], zh_ref[0], gain_ref[...], table_ref[...])
    mix_ref[...] = mixed_by(onehot, pick, probs)
    onehot_ref[...] = onehot
    fill_looped(wide_ref, 0, onehot_ref, rows_ref)
    give(wide_ref, sent_ref, 1)


def run_ahead_pack(*args):
    return call(
        ahead_pack,
        (shape((PEERS, ROWS, 256)), shape((SLOTS, TOK))),
        [SMEM] + [VMEM] * 4,
        [pltpu.VMEM((2, AREA, 128), f32), pltpu.VMEM((TOK, D), bf16), pltpu.VMEM((SLOTS, TOK), bf16)],
        args,
        10**9,
        4,
    )


def fetched(pairs, sems):
    copies = [pltpu.make_async_copy(a, b, sems.at[i]) for i, (a, b) in enumerate(pairs)]
    for copy in copies:
        copy.start()
    return copies


def behind_half(got_ref, weights, place, wide_ref, sems):
    (gate_hbm, gate_ref), (up_hbm, up_ref), (down_hbm, down_ref) = weights
    copies = fetched(weights, sems)

    def take(d, rows):
        for lane in range(2):
            for kind in range(2):
                wide_ref[lane, area_rows(d, kind), :] = got_ref[d, pl.ds(kind * ROWS, ROWS), LANES[lane]].astype(f32)

    each_peer(take)
    copies[0].wait()
    copies[1].wait()
    gate_pre, up_pre = jnp.zeros((SLOTS, FF), f32), jnp.zeros((SLOTS, FF), f32)
    for j in range(4):
        rows = jnp.concatenate([get_rows(wide_ref, 2 * j + i, SLOTS) for i in range(2)], axis=1)
        gate_pre = gate_pre + dot(rows, gate_ref[pl.ds(j * 512, 512), :])
        up_pre = up_pre + dot(rows, up_ref[pl.ds(j * 512, 512), :])
    copies[2].wait()
    down_grad = jnp.zeros((SLOTS, FF), f32)
    for j in range(4):
        rows = jnp.concatenate([get_rows(wide_ref, 2 * j + i, SLOTS, AREA) for i in range(2)], axis=1)
        down_grad = down_grad + dot(rows, down_ref[:, pl.ds(j * 512, 512)], ACROSS)
    sig = 1.0 / (1.0 + jnp.exp(-gate_pre))
    act = gate_pre * sig
    hidden = (act * up_pre).astype(bf16).astype(f32)
    grads = jnp.sum(hidden * down_grad, axis=-1, keepdims=True).astype(bf16).astype(f32)
    gate_grad = (down_grad * up_pre * sig * (1.0 + gate_pre * (1.0 - sig))).astype(bf16)
    up_grad = (down_grad * act).astype(bf16)
    for j in range(8):
        part = pl.ds(j * 256, 256)
        put_rows(wide_ref, j, dot(gate_grad, gate_ref[part, :], ACROSS) + dot(up_grad, up_ref[part, :], ACROSS))
    p, lane = iota((SLOTS, 128), 0), iota((SLOTS, 128), 1)
    gather = marks(iota((PEERS * 8, SLOTS), 1) // MOST == iota((PEERS * 8, SLOTS), 0) // 8)
    spread = jnp.where(lane == p % MOST + place * MOST, grads, 0.0)
    return dot(gather, spread.astype(bf16))


def near_experts(
    got_ref, gate_hbm, up_hbm, down_hbm, back_ref, small_ref, wide_ref, gate_ref, up_ref, down_ref, sems
):
    weights = ((gate_hbm, gate_ref), (up_hbm, up_ref), (down_hbm, down_ref))
    small_ref[...] = behind_half(got_ref, weights, 0, wide_ref, sems)

    def put(d, rows):
        for lane in range(2):
            back_ref[d, :, LANES[lane]] = wide_ref[lane, rows, :].astype(bf16)

    each_peer(put)


def far_experts(
    got_ref, near_ref, near_small_ref, gate_hbm, up_hbm, down_hbm, back_ref, wide_ref, gate_ref, up_ref, down_ref, sems
):
    weights = ((gate_hbm, gate_ref), (up_hbm, up_ref), (down_hbm, down_ref))
    small = behind_half(got_ref, weights, 1, wide_ref, sems) + near_small_ref[...]
    wide_ref[0, pl.ds(AREA, PEERS * 8), :] = small

    def put(d, rows):
        for lane in range(2):
            back_ref[d, pl.ds(0, ROWS), LANES[lane]] = near_ref[d, :, LANES[lane]]
            back_ref[d, pl.ds(ROWS, ROWS), LANES[lane]] = wide_ref[lane, rows, :].astype(bf16)
        extra = wide_ref[0, pl.ds(pl.multiple_of(AREA + d * 8, 8), 8), :].astype(bf16)
        back_ref[d, pl.ds(2 * ROWS, 8), LANES[0]] = extra
        back_ref[d, pl.ds(2 * ROWS, 8), LANES[1]] = extra

    each_peer(put)


WEIGHTS = [
    pltpu.VMEM((D, FF), bf16),
    pltpu.VMEM((D, FF), bf16),
    pltpu.VMEM((FF, D), bf16),
    pltpu.SemaphoreType.DMA((3,)),
]


def run_near_experts(*args):
    return call(
        near_experts,
        (shape((PEERS, ROWS, 256)), shape((PEERS * 8, 128), f32)),
        [VMEM] + [HBM] * 3,
        [pltpu.VMEM((2, 2 * AREA, 128), f32)] + WEIGHTS,
        args,
        5 * 10**9,
        13,
    )


def run_far_experts(*args):
    return call(
        far_experts,
        (shape((PEERS, 2 * ROWS + 8, 256)),),
        [VMEM] * 3 + [HBM] * 3,
        [pltpu.VMEM((2, 2 * AREA, 128), f32)] + WEIGHTS,
        args,
        5 * 10**9,
        15,
    )[0]


def ahead_experts(
    near_ref, far_ref, gate_hbm, up_hbm, down_hbm, first_ref, second_ref, wide_ref, gate_ref, up_ref, down_ref, sems,
    gate_sum, up_sum, hidden_ref
):
    copies = fetched(((gate_hbm, gate_ref), (up_hbm, up_ref), (down_hbm, down_ref)), sems)
    count = 2 * SLOTS

    def take(d, rows):
        for lane in range(2):
            wide_ref[lane, area_rows(d, 0), :] = near_ref[d, pl.ds(2 * ROWS, ROWS), LANES[lane]].astype(f32)
            wide_ref[lane, area_rows(d, 1), :] = far_ref[d, :, LANES[lane]].astype(f32)

    each_peer(take)
    copies[0].wait()
    copies[1].wait()
    gate_sum[...] = jnp.zeros((count, FF), f32)
    up_sum[...] = jnp.zeros((count, FF), f32)

    def inward(j):
        rows = jnp.concatenate([get_rows(wide_ref, 2 * j, count), get_rows(wide_ref, 2 * j + 1, count)], axis=1)
        gate_sum[...] += dot(rows, gate_ref[columns(j, 512), :])
        up_sum[...] += dot(rows, up_ref[columns(j, 512), :])

    loop(4, inward)
    gate_pre = gate_sum[...]
    hidden_ref[...] = (gate_pre / (1.0 + jnp.exp(-gate_pre)) * up_sum[...]).astype(bf16)
    copies[2].wait()

    def outward(c):
        for part in range(2):
            made = dot(hidden_ref[...], down_ref[:, columns(part * 4 + c, 256)])
            for i in range(2):
                wide_ref[part, pl.ds(2 * c + i, count, stride=8), :] = made[:, i * 128 : i * 128 + 128]

    loop(4, outward)

    def put(d, rows):
        for half in range(2):
            first_ref[d, pl.ds(half * ROWS, ROWS), :] = wide_ref[0, area_rows(d, half), :].astype(bf16)
            second_ref[d, pl.ds(half * ROWS, ROWS), :] = wide_ref[1, area_rows(d, half), :].astype(bf16)

    each_peer(put)


def run_ahead_experts(*args):
    return call(
        ahead_experts,
        (shape((PEERS, 2 * ROWS, 128)), shape((PEERS, 2 * ROWS, 128))),
        [VMEM] * 2 + [HBM] * 3,
        [pltpu.VMEM((2, 2 * AREA, 128), f32)]
        + WEIGHTS
        + [pltpu.VMEM((2 * SLOTS, FF), f32), pltpu.VMEM((2 * SLOTS, FF), f32), pltpu.VMEM((2 * SLOTS, FF), bf16)],
        args,
        6 * 10**9,
        14,
    )


def attend(length_ref, x_ref, q_ref, kc_ref, kn_ref, vc_ref, vn_ref, resid_ref):
    length = length_ref[0, 0]
    row, col = iota((TOK, 2 * TOK), 0), iota((TOK, 2 * TOK), 1)
    visible = ((col < TOK) & (col < length)) | ((col >= TOK) & (col - TOK <= row))
    for kv in range(KV_HEADS):
        part = pl.ds(kv * HEAD_DIM, HEAD_DIM)
        keys = jnp.concatenate([kc_ref[:, part], kn_ref[:, part]], axis=0)
        values = jnp.concatenate([vc_ref[:, part], vn_ref[:, part]], axis=0)
        for h in range(HEADS // KV_HEADS):
            cols = pl.ds((kv * (HEADS // KV_HEADS) + h) * HEAD_DIM, HEAD_DIM)
            scores = dot(q_ref[:, cols], keys, ACROSS) * HEAD_DIM ** (-0.5)
            scores = jnp.where(visible, scores, far_below)
            lifted = jnp.exp(scores - jnp.max(scores, axis=-1, keepdims=True))
            weights = (lifted * (1.0 / jnp.sum(lifted, axis=-1, keepdims=True))).astype(bf16)
            mixed = dot(weights, values).astype(bf16)
            resid_ref[:, cols] = (x_ref[:, cols].astype(f32) + mixed.astype(f32)).astype(bf16)


def run_attend(length, x, q, kc, kn, vc, vn):
    return call(
        attend,
        (shape((TOK, D)),),
        [SMEM] + [VMEM] * 6,
        [],
        (length, x, q, kc, kn, vc, vn),
        3 * 10**9,
        8,
    )[0]


def through_norm(sums, gain, inv, unit):
    scaled = sums * gain
    return inv * (scaled - unit * jnp.mean(scaled * unit, axis=-1, keepdims=True))


def behind_sums(
    zh_ref, home_ref, near_hot_ref, far_hot_ref, near_probs_ref, far_probs_ref, near_x_ref, far_x_ref, gain_ref,
    sums_ref, sent_ref, note_ref, mine_ref, wide_ref, line_ref, mix_ref
):
    zh = zh_ref[0]

    def take(d, rows):
        for half in range(2):
            for lane in range(2):
                wide_ref[lane, area_rows(d, half), :] = home_ref[d, pl.ds(half * ROWS, ROWS), LANES[lane]].astype(f32)
        wide_ref[0, pl.ds(pl.multiple_of(2 * AREA + d * 8, 8), 8), :] = home_ref[
            d, pl.ds(2 * ROWS, 8), LANES[0]
        ].astype(f32)

    each_peer(take)
    pick = picks(iota((SLOTS, EXPERTS), 0) // MOST, zh)
    near_mix = near_hot_ref[...] * dot(pick, near_probs_ref[...].astype(bf16)).astype(bf16)
    far_mix = far_hot_ref[...] * dot(pick, far_probs_ref[...].astype(bf16)).astype(bf16)
    small = wide_ref[0, pl.ds(2 * AREA, PEERS * 8), :].astype(bf16)
    share = marks(iota((SLOTS, PEERS * 8), 0) // MOST * 8 == iota((SLOTS, PEERS * 8), 1))
    small = dot(share, small)
    p, lane = iota((SLOTS, 128), 0) % MOST, iota((SLOTS, 128), 1)
    for half, hot in enumerate((near_hot_ref, far_hot_ref)):
        grads = jnp.sum(jnp.where(lane == p + half * MOST, small, 0.0), axis=-1, keepdims=True)
        note_ref[pl.ds(0, EXPERTS), pl.ds(half * TOK, TOK)] = dot(
            (pick.astype(f32) * grads).astype(bf16), hot[...], DOWN
        )
    mix_ref[0] = near_mix
    mix_ref[1] = far_mix

    def gather(j):
        cols = columns(j, 256)
        sums_ref[:, cols] = dot(mix_ref[0], get_rows(wide_ref, j, SLOTS), DOWN)
        line_ref[:, cols] = dot(mix_ref[1], get_rows(wide_ref, j, SLOTS, AREA), DOWN)

    loop(8, gather)
    inv, unit = unit_rows(far_x_ref[...])
    sums = line_ref[...]
    sent_ref[...] = through_norm(sums, gain_ref[...], inv, unit).astype(bf16)
    total = jnp.sum(sums * unit, axis=0, keepdims=True)
    _, unit = unit_rows(near_x_ref[...])
    total = total + jnp.sum(sums_ref[...] * unit, axis=0, keepdims=True)
    note_ref[pl.ds(EXPERTS, 8), :] = jnp.zeros((8, 256), f32)
    mine_ref[...] = jnp.zeros((8, 256), f32)
    for x in range(4):
        first, second = total[:, x * 512 : x * 512 + 256], total[:, x * 512 + 256 : x * 512 + 512]
        mine_ref[pl.ds(x, 1), :] = jnp.where(zh == 0, first, second)
        note_ref[pl.ds(EXPERTS + x, 1), :] = jnp.where(zh == 0, second, first)


def run_behind_sums(*args):
    return call(
        behind_sums,
        (shape((TOK, D), f32), shape((TOK, D)), shape((EXPERTS + 8, 256), f32), shape((8, 256), f32)),
        [SMEM] + [VMEM] * 8,
        [pltpu.VMEM((2, 2 * AREA + PEERS * 8, 128), f32), pltpu.VMEM((TOK, D), f32), pltpu.VMEM((2, SLOTS, TOK), bf16)],
        args,
        10**9,
        6,
    )


def behind_end(
    zh_ref, near_note_ref, far_note_ref, mine_ref, sums_ref, near_probs_ref, far_probs_ref, near_normed_ref,
    far_normed_ref, near_x_ref, far_x_ref, g_ref, gain_ref, table_ref, sent_ref, shares_ref
):
    zh = zh_ref[0]
    near_tok, far_tok = pl.ds(0, TOK), pl.ds(TOK, TOK)
    rows = pl.ds(0, EXPERTS)

    def logit_grads(probs, grads):
        return (probs * (grads - jnp.sum(probs * grads, axis=0, keepdims=True))).astype(bf16)

    near_logit = logit_grads(near_probs_ref[...], near_note_ref[rows, near_tok] + far_note_ref[rows, far_tok])
    far_logit = logit_grads(far_probs_ref[...], near_note_ref[rows, far_tok] + far_note_ref[rows, near_tok])
    inv, near_unit = unit_rows(near_x_ref[...])
    _, far_unit = unit_rows(far_x_ref[...])
    near_term = dot(near_logit, table_ref[...], DOWN)
    sums = sums_ref[...] + near_term
    sent_ref[...] = (g_ref[...].astype(f32) + through_norm(sums, gain_ref[...], inv, near_unit)).astype(bf16)
    far_term = dot(far_logit, table_ref[...], DOWN)
    total = jnp.sum(near_term * near_unit + far_term * far_unit, axis=0, keepdims=True)
    row = iota((128 - EXPERTS, 256), 0)
    for x in range(4):
        first, second = total[:, x * 512 : x * 512 + 256], total[:, x * 512 + 256 : x * 512 + 512]
        gains = (
            jnp.where(zh == 0, first, second)
            + mine_ref[pl.ds(x, 1), :]
            + far_note_ref[pl.ds(EXPERTS + x, 1), :]
        )
        cols = pl.ds(pl.multiple_of(x * 512 + zh * 256, 256), 256)
        part = dot(near_logit, near_normed_ref[:, cols]) + dot(far_logit, far_normed_ref[:, cols])
        both = jnp.concatenate([part, jnp.where(row == 0, gains, 0.0)], axis=0)
        shares_ref[pl.ds(x * 256, 256), :] = both.T


def run_behind_end(*args):
    return call(
        behind_end,
        (shape((TOK, D)), shape((D // 2, 128), f32)),
        [SMEM] + [VMEM] * 13,
        [],
        args,
        10**9,
        6,
    )


def ahead_end(home_ref, near_mix_ref, far_mix_ref, resid_ref, near_ref, far_ref, wide_ref):
    def take(d, rows):
        for half in range(2):
            wide_ref[0, area_rows(d, half), :] = home_ref[d, pl.ds(half * ROWS, ROWS), :].astype(f32)

    each_peer(take)
    for c in range(4):
        cols = pl.ds(c * 256, 256)
        for half, (mix_ref, out_ref) in enumerate(((near_mix_ref, near_ref), (far_mix_ref, far_ref))):
            rows = jnp.concatenate([get_rows(wide_ref, 2 * c + i, SLOTS, half * AREA) for i in range(2)], axis=1)
            sums = dot(mix_ref[...], rows, DOWN)
            if half == 0:
                sums = sums + resid_ref[:, cols].astype(f32)
            out_ref[:, cols] = sums.astype(bf16)


def run_ahead_end(home, near_mix, far_mix, resid, part):
    columns = pl.BlockSpec((TOK, D // 2), lambda i: (0, part))
    whole = [pl.BlockSpec(a.shape, lambda i, n=a.ndim: (0,) * n) for a in (home, near_mix, far_mix)]
    half = pl.BlockSpec((TOK, D // 2), lambda i: (0, 0))
    return pl.pallas_call(
        ahead_end,
        grid=(1,),
        out_shape=(shape((TOK, D // 2)), shape((TOK, D // 2))),
        in_specs=whole + [columns],
        out_specs=(half, half),
        scratch_shapes=[pltpu.VMEM((1, 2 * AREA, 128), f32)],
        compiler_params=pltpu.CompilerParams(vmem_limit_bytes=63 * 2**20),
        cost_estimate=pl.CostEstimate(flops=10**9, transcendentals=0, bytes_accessed=3 * 2**20),
    )(home, near_mix, far_mix, resid)


def final_add(a_ref, b_ref, c_ref, d_ref, out_ref):
    half = D // 2
    out_ref[:, pl.ds(0, half)] = (a_ref[...].astype(f32) + b_ref[...].astype(f32)).astype(bf16)
    out_ref[:, pl.ds(half, half)] = (c_ref[...].astype(f32) + d_ref[...].astype(f32)).astype(bf16)


def run_final_add(*args):
    return call(final_add, (shape((TOK, D)),), [VMEM] * 4, [], args, 10**6, 2)[0]


def body(
    forward_input,
    queries,
    new_keys,
    new_values,
    cache_keys,
    cache_values,
    context_lengths,
    norm_gain,
    router,
    gate_weight,
    up_weight,
    down_weight,
    forward_ids,
    backward_input,
    backward_ids,
    output_grad,
):
    zh = lax.axis_index("zh").astype(jnp.int32).reshape(1)
    gain = norm_gain
    table = router[0].T
    weights = (gate_weight[0, 0], up_weight[0, 0], down_weight[0, 0])
    back_x, back_g = backward_input[0], output_grad[0]
    ids_b, ids_f = backward_ids[0].T, forward_ids[0].T
    ids_far = swapped(jnp.concatenate([ids_b, ids_f], axis=0))
    x_far = swapped(back_x)
    g_far = swapped(back_g)
    resid = run_attend(
        context_lengths,
        forward_input[0],
        queries[0],
        cache_keys[0],
        new_keys[0],
        cache_values[0],
        new_values[0],
    )
    resid_far = swapped(resid)
    sent_1, normed_b, hot_b, probs_b, mix_f = run_near_pack(
        zh, ids_b, ids_f, back_x, back_g, resid, gain, table
    )
    got_1 = spread_out(sent_1)
    sent_2, normed_c, hot_c, probs_c = run_far_pack(zh, ids_far[:4], x_far, g_far, gain, table)
    sent_2, _ = lax.optimization_barrier((sent_2, got_1))
    got_2 = spread_out(sent_2)
    sent_3, mix_h = run_ahead_pack(zh, ids_far[4:], resid_far, gain, table)
    sent_3, got_2 = lax.optimization_barrier((sent_3, got_2))
    got_3 = spread_out(sent_3)
    back_b, small_b = run_near_experts(got_1, *weights)
    back = run_far_experts(got_2, back_b, small_b, *weights)
    back, got_3 = lax.optimization_barrier((back, got_3))
    home_b = spread_out(back)
    made_1, made_2 = run_ahead_experts(got_1, got_3, *weights)
    made_1, home_b = lax.optimization_barrier((made_1, home_b))
    home_1 = spread_out(made_1)
    sums_b, own_c, note, mine = run_behind_sums(
        zh, home_b, hot_b, hot_c, probs_b, probs_c, back_x, x_far, gain
    )
    far_note = swapped(note)
    moved_c = moved(own_c, False, -1)
    own_b, shares = run_behind_end(
        zh, note, far_note, mine, sums_b, probs_b, probs_c, normed_b, normed_c, back_x, x_far, back_g, gain, table
    )
    moved_b = moved(own_b, True, -1)
    made_2, home_1 = lax.optimization_barrier((made_2, home_1))
    home_2 = spread_out(made_2)
    own_f1, own_h1 = run_ahead_end(home_1, mix_f, mix_h, resid, 0)
    moved_h1 = moved(own_h1, False, 1)
    moved_f1 = moved(own_f1, True, 1)
    own_f2, own_h2 = run_ahead_end(home_2, mix_f, mix_h, resid, 1)
    moved_h2 = moved(own_h2, False, 1)
    moved_f2 = moved(own_f2, True, 1)
    shares, own_f2 = lax.optimization_barrier((shares, own_f2))
    total = jnp.sum(spread_out(shares.reshape(PEERS, PEERS, 128)), axis=0) * factor
    input_grad = (moved_b.astype(f32) + moved_c.astype(f32)).astype(bf16)
    forward_output = run_final_add(moved_f1, moved_h1, moved_f2, moved_h2)
    return (
        forward_output[None],
        input_grad[None],
        total[None, :, :EXPERTS],
        total[:, EXPERTS][None],
    )


def solution(mesh):
    grid = Mesh(mesh.devices.reshape(4, 4, 2, 4, 2), ("pipe", "x", "zh", "y", "core"))
    rows = P("pipe", ALL, None)
    placed = (
        rows,
        rows,
        rows,
        rows,
        rows,
        rows,
        P("pipe", ALL),
        P("pipe", None),
        P("pipe", None, None),
        P("pipe", ALL, None, None),
        P("pipe", ALL, None, None),
        P("pipe", ALL, None, None),
        rows,
        rows,
        rows,
        rows,
    )
    return jax.shard_map(
        body,
        mesh=grid,
        in_specs=placed,
        out_specs=(rows, rows, rows, P("pipe", ALL)),
        check_vma=False,
    )
```

profile of v0, /device:TPU:1, one launch (start us, length us, event | category | flops | bytes accessed | tf_op | source)
XLA Modules:
  0.0 316.0 jit_solution(17823490154422790604)
XLA Ops:
  4.9 6.6 %shard_map.184 = (bf16[32,216,256]{2,1,0:T(8,128)(2,1)}, bf16[128,2048]{1,0:T(8,128)(2,1)}, bf16[288,128]{1,0:T(8,128)(2,1)}, f32[64,128]{1,0:T(8,128)}, bf16[288,128]{1,0:T(8,128)(2,1)}) custom-call(s32[1]{0:T(128)} %bitcast.zh_ref, s32[4,128]{1,0:T(4,128)} %bitcast.41, s32[4,128]{1,0:T(4,128)} %bitcast.43, bf16[128,2048]{1,0:T(8,128)(2,1)} %bitcast.28, ...), custom_call_target="tpu_custom_call" | custom-call | flops 2000000000 | bytes 8388608 | tf_op jit(solution)/shard_map/pallas_call | solution.py:58
  11.6 8.8 %all-to-all-start = ((bf16[32,216,256]{2,1,0:T(8,128)(2,1)}), bf16[32,216,256]{2,1,0:T(8,128)(2,1)}, u32[]{:S(2)}, u32[]{:S(2)}) async-start(bf16[32,216,256]{2,1,0:T(8,128)(2,1)} %get-tuple-element.39), calls=%async_computation | async-start | bytes 7077888 | tf_op jit(solution)/shard_map/all_to_all | solution.py:37
  20.4 7.0 %collective-permute-start.2 = (bf16[128,2048]{1,0:T(8,128)(2,1)S(1)}, bf16[128,2048]{1,0:T(8,128)(2,1)S(1)}, u32[]{:S(2)}, u32[]{:S(2)}) collective-permute-start(bf16[128,2048]{1,0:T(8,128)(2,1)S(1)} %bitcast.31), channel_id=1, source_target_pairs={{0,8},{8,0},{1,9},{9,1},{2,10},{10,2},{3,11},{11,3},{4,12},{12,4},... | collective-permute-start | bytes 1572872 | tf_op jit(solution)/shard_map/ppermute | solution.py:41
  27.5 5.4 %collective-permute-start = (s32[8,128]{1,0:T(8,128)S(1)}, s32[8,128]{1,0:T(8,128)S(1)}, u32[]{:S(2)}, u32[]{:S(2)}) collective-permute-start(s32[8,128]{1,0:T(8,128)S(1)} %pad_add_fusion), channel_id=1, source_target_pairs={{0,8},{8,0},{1,9},{9,1},{2,10},{10,2},{3,11},{11,3},{4,12},{12,4},... | collective-permute-start | bytes 12296 | tf_op jit(solution)/shard_map/ppermute | solution.py:41
  32.8 23.8 %collective-permute-done = s32[8,128]{1,0:T(8,128)S(1)} collective-permute-done((s32[8,128]{1,0:T(8,128)S(1)}, s32[8,128]{1,0:T(8,128)S(1)}, u32[]{:S(2)}, u32[]{:S(2)}) %collective-permute-start) | collective-permute-done | bytes 4128 | tf_op jit(solution)/shard_map/ppermute | solution.py:41
  58.8 7.5 %shard_map.186 = (bf16[32,144,256]{2,1,0:T(8,128)(2,1)}, bf16[128,2048]{1,0:T(8,128)(2,1)}, bf16[288,128]{1,0:T(8,128)(2,1)}, f32[64,128]{1,0:T(8,128)}) custom-call(s32[1]{0:T(128)} %bitcast.zh_ref, s32[4,128]{1,0:T(4,128)} %get-tuple-element.74.ids_ref, bf16[128,2048]{1,0:T(8,128)(2,1)} %copy-done.1, bf16[128,2048]{1,0:T(8,128)(2,1)} %copy-done.8, ...), custom_call_target="tpu_custom_call" | custom-call | flops 1000000000 | bytes 6291456 | tf_op jit(solution)/shard_map/pallas_call | solution.py:58
  66.3 23.4 %all-to-all-start.1 = ((bf16[32,144,256]{2,1,0:T(8,128)(2,1)}), bf16[32,144,256]{2,1,0:T(8,128)(2,1)}, u32[]{:S(2)}, u32[]{:S(2)}) async-start(bf16[32,144,256]{2,1,0:T(8,128)(2,1)} %get-tuple-element.42), calls=%async_computation.1 | async-start | bytes 4718592 | tf_op jit(solution)/shard_map/all_to_all | solution.py:37
  89.7 6.2 %collective-permute-start.1 = (bf16[128,2048]{1,0:T(8,128)(2,1)S(1)}, bf16[128,2048]{1,0:T(8,128)(2,1)S(1)}, u32[]{:S(2)}, u32[]{:S(2)}) collective-permute-start(bf16[128,2048]{1,0:T(8,128)(2,1)S(1)} %copy-done.7), channel_id=1, source_target_pairs={{0,8},{8,0},{1,9},{9,1},{2,10},{10,2},{3,11},{11,3},{4,12},{12,4},... | collective-permute-start | bytes 1572872 | tf_op jit(solution)/shard_map/ppermute | solution.py:41
  96.0 13.8 %collective-permute-done.1.x_ref = bf16[128,2048]{1,0:T(8,128)(2,1)S(1)} collective-permute-done((bf16[128,2048]{1,0:T(8,128)(2,1)S(1)}, bf16[128,2048]{1,0:T(8,128)(2,1)S(1)}, u32[]{:S(2)}, u32[]{:S(2)}) %collective-permute-start.1) | collective-permute-done | bytes 524320 | tf_op jit(solution)/shard_map/ppermute | solution.py:41
  110.5 5.0 %shard_map.185 = (bf16[32,72,256]{2,1,0:T(8,128)(2,1)}, bf16[288,128]{1,0:T(8,128)(2,1)}) custom-call(s32[1]{0:T(128)} %bitcast.zh_ref, s32[4,128]{1,0:T(4,128)} %get-tuple-element.75.ids_ref, bf16[128,2048]{1,0:T(8,128)(2,1)} %copy-done.9, f32[1,2048]{1,0:T(1,128)} %gain_ref.9, bf16[64,2048]{1,0:T(8,128)(2,1)} %bitcast.39), custom_call_target="tpu_custom_call" | custom-call | flops 1000000000 | bytes 4194304 | tf_op jit(solution)/shard_map/pallas_call | solution.py:58
  115.5 5.4 %all-to-all-done.1.got_ref = bf16[32,144,256]{2,1,0:T(8,128)(2,1)} async-done(((bf16[32,144,256]{2,1,0:T(8,128)(2,1)}), bf16[32,144,256]{2,1,0:T(8,128)(2,1)}, u32[]{:S(2)}, u32[]{:S(2)}) %all-to-all-start.1) | async-done | bytes 2359328 | tf_op jit(solution)/shard_map/all_to_all | solution.py:37
  121.0 11.3 %all-to-all-start.2 = ((bf16[32,72,256]{2,1,0:T(8,128)(2,1)}), bf16[32,72,256]{2,1,0:T(8,128)(2,1)}, u32[]{:S(2)}, u32[]{:S(2)}) async-start(bf16[32,72,256]{2,1,0:T(8,128)(2,1)} %get-tuple-element.46), calls=%async_computation.2 | async-start | bytes 2359296 | tf_op jit(solution)/shard_map/all_to_all | solution.py:37
  132.2 12.2 %shard_map.187 = (bf16[32,72,256]{2,1,0:T(8,128)(2,1)}, f32[256,128]{1,0:T(8,128)}) custom-call(bf16[32,216,256]{2,1,0:T(8,128)(2,1)} %all-to-all-done.got_ref.near_ref, bf16[2048,768]{1,0:T(8,128)(2,1)} %bitcast.46, bf16[2048,768]{1,0:T(8,128)(2,1)} %bitcast.49, bf16[768,2048]{1,0:T(8,128)(2,1)} %bitcast.52), custom_call_target="tpu_custom_call" | custom-call | flops 5000000000 | bytes 13631488 | tf_op jit(solution)/shard_map/pallas_call | solution.py:58
  144.4 12.7 %shard_map.188 = bf16[32,152,256]{2,1,0:T(8,128)(2,1)} custom-call(bf16[32,144,256]{2,1,0:T(8,128)(2,1)} %all-to-all-done.1.got_ref, bf16[32,72,256]{2,1,0:T(8,128)(2,1)} %get-tuple-element.44.near_ref, f32[256,128]{1,0:T(8,128)} %get-tuple-element.45.near_small_ref, bf16[2048,768]{1,0:T(8,128)(2,1)} %bitcast.47, bf16[2048,768]{1,0:T(8,128)(2,1)} %bitcast.50, ...), custom_call_target="tpu_custom_call" | custom-call | flops 5000000000 | bytes 15728640 | tf_op jit(solution)/shard_map/pallas_call | solution.py:58
  157.2 7.5 %all-to-all-start.3 = ((bf16[32,152,256]{2,1,0:T(8,128)(2,1)}), bf16[32,152,256]{2,1,0:T(8,128)(2,1)}, u32[]{:S(2)}, u32[]{:S(2)}) async-start(bf16[32,152,256]{2,1,0:T(8,128)(2,1)} %shard_map.188), calls=%async_computation.3 | async-start | bytes 4980736 | tf_op jit(solution)/shard_map/all_to_all | solution.py:37
  164.6 15.0 %shard_map.189 = (bf16[32,144,128]{2,1,0:T(8,128)(2,1)}, bf16[32,144,128]{2,1,0:T(8,128)(2,1)}) custom-call(bf16[32,216,256]{2,1,0:T(8,128)(2,1)} %all-to-all-done.got_ref.near_ref, bf16[32,72,256]{2,1,0:T(8,128)(2,1)} %all-to-all-done.2.far_ref, bf16[2048,768]{1,0:T(8,128)(2,1)} %bitcast.48, bf16[2048,768]{1,0:T(8,128)(2,1)} %bitcast.51, ...), custom_call_target="tpu_custom_call" | custom-call | flops 6000000000 | bytes 14680064 | tf_op jit(solution)/shard_map/pallas_call | solution.py:58
  179.6 17.6 %all-to-all-done.3.home_ref = bf16[32,152,256]{2,1,0:T(8,128)(2,1)} async-done(((bf16[32,152,256]{2,1,0:T(8,128)(2,1)}), bf16[32,152,256]{2,1,0:T(8,128)(2,1)}, u32[]{:S(2)}, u32[]{:S(2)}) %all-to-all-start.3) | async-done | bytes 2490400 | tf_op jit(solution)/shard_map/all_to_all | solution.py:37
  197.2 24.2 %all_to_all.35.home_ref = bf16[32,144,128]{2,1,0:T(8,128)(2,1)} all-to-all(bf16[32,144,128]{2,1,0:T(8,128)(2,1)} %get-tuple-element.51), channel_id=1, replica_groups=mesh['pipe'=4,'x'=4,'zh'=2,'y'=4,'core'=2] {'x','y','core'}, dimensions={0} | all-to-all | bytes 2359296 | tf_op jit(solution)/shard_map/all_to_all | solution.py:37
  226.1 7.5 %shard_map.193 = (f32[128,2048]{1,0:T(8,128)}, bf16[128,2048]{1,0:T(8,128)(2,1)}, f32[72,256]{1,0:T(8,128)}, f32[8,256]{1,0:T(8,128)}) custom-call(s32[1]{0:T(128)} %bitcast.zh_ref, bf16[32,152,256]{2,1,0:T(8,128)(2,1)} %all-to-all-done.3.home_ref, bf16[288,128]{1,0:T(8,128)(2,1)} %get-tuple-element.61.near_hot_ref, ...), custom_call_target="tpu_custom_call" | custom-call | flops 1000000000 | bytes 6291456 | tf_op jit(solution)/shard_map/pallas_call | solution.py:58
  233.6 6.1 %collective-permute-start.8 = (f32[72,256]{1,0:T(8,128)}, f32[72,256]{1,0:T(8,128)S(1)}, u32[]{:S(2)}, u32[]{:S(2)}) collective-permute-start(f32[72,256]{1,0:T(8,128)} %get-tuple-element.65.near_note_ref), channel_id=1, source_target_pairs={{0,8},{8,0},{1,9},{9,1},{2,10},{10,2},{3,11},{11,3},{4,12},{12,4},... | collective-permute-start | bytes 221192 | tf_op jit(solution)/shard_map/ppermute | solution.py:41
  250.0 10.6 %all-to-all-start.6 = ((f32[32,32,128]{2,1,0:T(8,128)}), f32[32,32,128]{2,1,0:T(8,128)S(1)}, u32[]{:S(2)}, u32[]{:S(2)}) async-start(f32[32,32,128]{2,1,0:T(8,128)} %bitcast.36), calls=%async_computation.6 | async-start | bytes 1048576 | tf_op jit(solution)/shard_map/all_to_all | solution.py:37
  265.3 13.6 %collective-permute-start.5 = (bf16[128,1024]{1,0:T(8,128)(2,1)}, bf16[128,1024]{1,0:T(8,128)(2,1)}, u32[]{:S(2)}, u32[]{:S(2)}) collective-permute-start(bf16[128,1024]{1,0:T(8,128)(2,1)} %get-tuple-element.56), channel_id=1, source_target_pairs={{0,72},{8,64},{64,136},{72,128},{128,200},{136,192},{192,8},{200,0... | collective-permute-start | bytes 786440 | tf_op jit(solution)/shard_map/ppermute | solution.py:50
  282.8 10.3 %collective-permute-done.5.b_ref = bf16[128,1024]{1,0:T(8,128)(2,1)} collective-permute-done((bf16[128,1024]{1,0:T(8,128)(2,1)}, bf16[128,1024]{1,0:T(8,128)(2,1)}, u32[]{:S(2)}, u32[]{:S(2)}) %collective-permute-start.5) | collective-permute-done | bytes 262176 | tf_op jit(solution)/shard_map/ppermute | solution.py:50
  293.1 19.4 %collective-permute-done.7.d_ref = bf16[128,1024]{1,0:T(8,128)(2,1)} collective-permute-done((bf16[128,1024]{1,0:T(8,128)(2,1)}, bf16[128,1024]{1,0:T(8,128)(2,1)}, u32[]{:S(2)}, u32[]{:S(2)}) %collective-permute-start.7) | collective-permute-done | bytes 262176 | tf_op jit(solution)/shard_map/ppermute | solution.py:50
  (50 shorter events, 33.7 us)
Async XLA Ops:
  11.5 8.8 %copy-start = (bf16[1,128,2048]{2,1,0:T(8,128)(2,1)S(1)}, bf16[1,128,2048]{2,1,0:T(8,128)(2,1)}, u32[]{:S(2)}) copy-start(bf16[1,128,2048]{2,1,0:T(8,128)(2,1)} %param.29) | copy-start | bytes 1572868
  11.5 15.8 %copy-start.2 = (bf16[1,128,2048]{2,1,0:T(8,128)(2,1)S(1)}, bf16[1,128,2048]{2,1,0:T(8,128)(2,1)}, u32[]{:S(2)}) copy-start(bf16[1,128,2048]{2,1,0:T(8,128)(2,1)} %param.31) | copy-start | bytes 1572868
  11.5 15.9 %copy-start.5 = (s32[1,128,4]{1,2,0:T(4,128)S(1)}, s32[1,128,4]{1,2,0:T(4,128)}, u32[]{:S(2)}) copy-start(s32[1,128,4]{1,2,0:T(4,128)} %param.30) | copy-start | bytes 6148
  11.6 15.9 %copy-start.6 = (s32[1,128,4]{1,2,0:T(4,128)S(1)}, s32[1,128,4]{1,2,0:T(4,128)}, u32[]{:S(2)}) copy-start(s32[1,128,4]{1,2,0:T(4,128)} %param.28) | copy-start | bytes 6148
  11.6 54.7 %all-to-all-start = ((bf16[32,216,256]{2,1,0:T(8,128)(2,1)}), bf16[32,216,256]{2,1,0:T(8,128)(2,1)}, u32[]{:S(2)}, u32[]{:S(2)}) async-start(bf16[32,216,256]{2,1,0:T(8,128)(2,1)} %get-tuple-element.39), calls=%async_computation | async-start | bytes 7077888 | tf_op jit(solution)/shard_map/all_to_all | solution.py:37
  20.4 36.9 %collective-permute-start.2 = (bf16[128,2048]{1,0:T(8,128)(2,1)S(1)}, bf16[128,2048]{1,0:T(8,128)(2,1)S(1)}, u32[]{:S(2)}, u32[]{:S(2)}) collective-permute-start(bf16[128,2048]{1,0:T(8,128)(2,1)S(1)} %bitcast.31), channel_id=1, source_target_pairs={{0,8},{8,0},{1,9},{9,1},{2,10},{10,2},{3,11},{11,3},{4,12},{12,4},... | collective-permute-start | bytes 1572872 | tf_op jit(solution)/shard_map/ppermute | solution.py:41
  27.4 30.7 %collective-permute-start.3 = (bf16[128,2048]{1,0:T(8,128)(2,1)S(1)}, bf16[128,2048]{1,0:T(8,128)(2,1)S(1)}, u32[]{:S(2)}, u32[]{:S(2)}) collective-permute-start(bf16[128,2048]{1,0:T(8,128)(2,1)S(1)} %bitcast.34), channel_id=1, source_target_pairs={{0,8},{8,0},{1,9},{9,1},{2,10},{10,2},{3,11},{11,3},{4,12},{12,4},... | collective-permute-start | bytes 1572872 | tf_op jit(solution)/shard_map/ppermute | solution.py:41
  27.5 29.2 %collective-permute-start = (s32[8,128]{1,0:T(8,128)S(1)}, s32[8,128]{1,0:T(8,128)S(1)}, u32[]{:S(2)}, u32[]{:S(2)}) collective-permute-start(s32[8,128]{1,0:T(8,128)S(1)} %pad_add_fusion), channel_id=1, source_target_pairs={{0,8},{8,0},{1,9},{9,1},{2,10},{10,2},{3,11},{11,3},{4,12},{12,4},... | collective-permute-start | bytes 12296 | tf_op jit(solution)/shard_map/ppermute | solution.py:41
  57.2 0.8 copy-start.1
  66.3 23.5 %copy-start.7 = (bf16[128,2048]{1,0:T(8,128)(2,1)S(1)}, bf16[128,2048]{1,0:T(8,128)(2,1)}, u32[]{:S(2)}) copy-start(bf16[128,2048]{1,0:T(8,128)(2,1)} %shard_map.183.resid_ref) | copy-start | bytes 1572868
  66.3 54.7 %all-to-all-start.1 = ((bf16[32,144,256]{2,1,0:T(8,128)(2,1)}), bf16[32,144,256]{2,1,0:T(8,128)(2,1)}, u32[]{:S(2)}, u32[]{:S(2)}) async-start(bf16[32,144,256]{2,1,0:T(8,128)(2,1)} %get-tuple-element.42), calls=%async_computation.1 | async-start | bytes 4718592 | tf_op jit(solution)/shard_map/all_to_all | solution.py:37
  89.7 20.0 %collective-permute-start.1 = (bf16[128,2048]{1,0:T(8,128)(2,1)S(1)}, bf16[128,2048]{1,0:T(8,128)(2,1)S(1)}, u32[]{:S(2)}, u32[]{:S(2)}) collective-permute-start(bf16[128,2048]{1,0:T(8,128)(2,1)S(1)} %copy-done.7), channel_id=1, source_target_pairs={{0,8},{8,0},{1,9},{9,1},{2,10},{10,2},{3,11},{11,3},{4,12},{12,4},... | collective-permute-start | bytes 1572872 | tf_op jit(solution)/shard_map/ppermute | solution.py:41
  121.0 36.2 %all-to-all-start.2 = ((bf16[32,72,256]{2,1,0:T(8,128)(2,1)}), bf16[32,72,256]{2,1,0:T(8,128)(2,1)}, u32[]{:S(2)}, u32[]{:S(2)}) async-start(bf16[32,72,256]{2,1,0:T(8,128)(2,1)} %get-tuple-element.46), calls=%async_computation.2 | async-start | bytes 2359296 | tf_op jit(solution)/shard_map/all_to_all | solution.py:37
  157.2 40.1 %all-to-all-start.3 = ((bf16[32,152,256]{2,1,0:T(8,128)(2,1)}), bf16[32,152,256]{2,1,0:T(8,128)(2,1)}, u32[]{:S(2)}, u32[]{:S(2)}) async-start(bf16[32,152,256]{2,1,0:T(8,128)(2,1)} %shard_map.188), calls=%async_computation.3 | async-start | bytes 4980736 | tf_op jit(solution)/shard_map/all_to_all | solution.py:37
  221.4 25.6 %all-to-all-start.5 = ((bf16[32,144,128]{2,1,0:T(8,128)(2,1)}), bf16[32,144,128]{2,1,0:T(8,128)(2,1)}, u32[]{:S(2)}, u32[]{:S(2)}) async-start(bf16[32,144,128]{2,1,0:T(8,128)(2,1)} %get-tuple-element.57), calls=%async_computation.5 | async-start | bytes 2359296 | tf_op jit(solution)/shard_map/all_to_all | solution.py:37
  233.6 8.6 %collective-permute-start.8 = (f32[72,256]{1,0:T(8,128)}, f32[72,256]{1,0:T(8,128)S(1)}, u32[]{:S(2)}, u32[]{:S(2)}) collective-permute-start(f32[72,256]{1,0:T(8,128)} %get-tuple-element.65.near_note_ref), channel_id=1, source_target_pairs={{0,8},{8,0},{1,9},{9,1},{2,10},{10,2},{3,11},{11,3},{4,12},{12,4},... | collective-permute-start | bytes 221192 | tf_op jit(solution)/shard_map/ppermute | solution.py:41
  239.7 40.9 %collective-permute-start.10 = (bf16[128,2048]{1,0:T(8,128)(2,1)}, bf16[128,2048]{1,0:T(8,128)(2,1)}, u32[]{:S(2)}, u32[]{:S(2)}) collective-permute-start(bf16[128,2048]{1,0:T(8,128)(2,1)} %get-tuple-element.71), channel_id=1, source_target_pairs={{0,200},{8,192},{64,8},{72,0},{128,72},{136,64},{192,136},{200,128... | collective-permute-start | bytes 1572872 | tf_op jit(solution)/shard_map/ppermute | solution.py:50
  247.0 33.6 %collective-permute-start.9 = (bf16[128,2048]{1,0:T(8,128)(2,1)}, bf16[128,2048]{1,0:T(8,128)(2,1)}, u32[]{:S(2)}, u32[]{:S(2)}) collective-permute-start(bf16[128,2048]{1,0:T(8,128)(2,1)} %get-tuple-element.70), channel_id=1, source_target_pairs={{0,192},{8,200},{64,0},{72,8},{128,64},{136,72},{192,128},{200,136... | collective-permute-start | bytes 1572872 | tf_op jit(solution)/shard_map/ppermute | solution.py:50
  250.0 64.6 %all-to-all-start.6 = ((f32[32,32,128]{2,1,0:T(8,128)}), f32[32,32,128]{2,1,0:T(8,128)S(1)}, u32[]{:S(2)}, u32[]{:S(2)}) async-start(f32[32,32,128]{2,1,0:T(8,128)} %bitcast.36), calls=%async_computation.6 | async-start | bytes 1048576 | tf_op jit(solution)/shard_map/all_to_all | solution.py:37
  263.6 19.2 %collective-permute-start.4 = (bf16[128,1024]{1,0:T(8,128)(2,1)}, bf16[128,1024]{1,0:T(8,128)(2,1)S(1)}, u32[]{:S(2)}, u32[]{:S(2)}) collective-permute-start(bf16[128,1024]{1,0:T(8,128)(2,1)} %get-tuple-element.55), channel_id=1, source_target_pairs={{0,64},{8,72},{64,128},{72,136},{128,192},{136,200},{192,0},{200,8... | collective-permute-start | bytes 786440 | tf_op jit(solution)/shard_map/ppermute | solution.py:50
  265.3 27.8 %collective-permute-start.5 = (bf16[128,1024]{1,0:T(8,128)(2,1)}, bf16[128,1024]{1,0:T(8,128)(2,1)}, u32[]{:S(2)}, u32[]{:S(2)}) collective-permute-start(bf16[128,1024]{1,0:T(8,128)(2,1)} %get-tuple-element.56), channel_id=1, source_target_pairs={{0,72},{8,64},{64,136},{72,128},{128,200},{136,192},{192,8},{200,0... | collective-permute-start | bytes 786440 | tf_op jit(solution)/shard_map/ppermute | solution.py:50
  278.9 33.6 %collective-permute-start.6 = (bf16[128,1024]{1,0:T(8,128)(2,1)}, bf16[128,1024]{1,0:T(8,128)(2,1)}, u32[]{:S(2)}, u32[]{:S(2)}) collective-permute-start(bf16[128,1024]{1,0:T(8,128)(2,1)} %get-tuple-element.58), channel_id=1, source_target_pairs={{0,64},{8,72},{64,128},{72,136},{128,192},{136,200},{192,0},{200,8... | collective-permute-start | bytes 786440 | tf_op jit(solution)/shard_map/ppermute | solution.py:50
  280.7 31.9 %collective-permute-start.7 = (bf16[128,1024]{1,0:T(8,128)(2,1)}, bf16[128,1024]{1,0:T(8,128)(2,1)}, u32[]{:S(2)}, u32[]{:S(2)}) collective-permute-start(bf16[128,1024]{1,0:T(8,128)(2,1)} %get-tuple-element.59), channel_id=1, source_target_pairs={{0,72},{8,64},{64,136},{72,128},{128,200},{136,192},{192,8},{200,0... | collective-permute-start | bytes 786440 | tf_op jit(solution)/shard_map/ppermute | solution.py:50
  282.8 29.7 %copy-start.3 = (bf16[128,1024]{1,0:T(8,128)(2,1)}, bf16[128,1024]{1,0:T(8,128)(2,1)S(1)}, u32[]{:S(2)}) copy-start(bf16[128,1024]{1,0:T(8,128)(2,1)S(1)} %collective-permute-done.4.a_ref) | copy-start | bytes 786436
  (3 other events, 2.2 us)
where the time goes:
time: 317 us; the launch traced here: 316 us
  starting transfers between devices  108 us (34%)
  waiting for transfers between devices  92.8 us (29%)
  Pallas kernels  82.3 us (26%)
  blocking collectives  24.2 us (8%)
  local copies, waits for them, and re-layouts  4.94 us (2%)
    pallas_call x10, Pallas kernels, call(): pl.pallas_call(kernel, out_shape=outs, in_specs=ins, out_specs=tuple((VME...  76.4 us
    all_to_all x6, starting transfers between devices, spread_out(): return lax.all_to_all(x, XY, 0, 0, tiled=True)  66.2 us
    ppermute x5, waiting for transfers between devices, swapped(): return lax.ppermute(x, 'zh', [(0, 1), (1, 0)])  40 us
    ppermute x6, waiting for transfers between devices, moved(): return lax.ppermute(x, ('pipe', 'zh'), pairs)  29.7 us
    ppermute x5, starting transfers between devices, swapped(): return lax.ppermute(x, 'zh', [(0, 1), (1, 0)])  24.8 us
    all_to_all x1, blocking collectives, spread_out(): return lax.all_to_all(x, XY, 0, 0, tiled=True)  24.2 us
    all_to_all x6, waiting for transfers between devices, spread_out(): return lax.all_to_all(x, XY, 0, 0, tiled=True)  23.1 us
    ppermute x6, starting transfers between devices, moved(): return lax.ppermute(x, ('pipe', 'zh'), pairs)  17.1 us
  transfers between devices with their start and end apart: 17, of which 7 were waited for; matrix products, arithmetic and copies ran while one was open for 1% of the time, Pallas kernels for 23%

commit v1 on v0

--- a/solution.py
+++ b/solution.py
@@ -232,8 +232,8 @@
     normed_ref[...], probs_ref[...], _, onehot_ref[...] = routed(
         ids_ref[...], x_ref[...], zh_ref[0], gain_ref[...], table_ref[...]
     )
-    fill_looped(wide_ref, 0, onehot_ref, normed_ref)
-    fill_looped(wide_ref, 1, onehot_ref, g_ref)
+    fill(wide_ref, 0, onehot_ref[...], normed_ref)
+    fill(wide_ref, 1, onehot_ref[...], g_ref)
     give(wide_ref, sent_ref, 2)
 
 
@@ -276,7 +276,23 @@
     return copies
 
 
-def behind_half(got_ref, weights, place, wide_ref, sems):
+def expert_slopes(gate_pre, up_pre, down_grad, gate_grad, up_grad):
+    sig = 1.0 / (1.0 + jnp.exp(-gate_pre))
+    act = gate_pre * sig
+    hidden = (act * up_pre).astype(bf16).astype(f32)
+    gate_grad[...] = (down_grad * up_pre * sig * (1.0 + gate_pre * (1.0 - sig))).astype(bf16)
+    up_grad[...] = (down_grad * act).astype(bf16)
+    return jnp.sum(hidden * down_grad, axis=-1, keepdims=True).astype(bf16).astype(f32)
+
+
+def small_grads(grads, place):
+    p, lane = iota((SLOTS, 128), 0), iota((SLOTS, 128), 1)
+    gather = marks(iota((PEERS * 8, SLOTS), 1) // MOST == iota((PEERS * 8, SLOTS), 0) // 8)
+    spread = jnp.where(lane == p % MOST + place * MOST, grads, 0.0)
+    return dot(gather, spread.astype(bf16))
+
+
+def behind_half(got_ref, weights, place, wide_ref, sems, gate_grad, up_grad):
     (gate_hbm, gate_ref), (up_hbm, up_ref), (down_hbm, down_ref) = weights
     copies = fetched(weights, sems)
 
@@ -298,26 +314,48 @@
     for j in range(4):
         rows = jnp.concatenate([get_rows(wide_ref, 2 * j + i, SLOTS, AREA) for i in range(2)], axis=1)
         down_grad = down_grad + dot(rows, down_ref[:, pl.ds(j * 512, 512)], ACROSS)
-    sig = 1.0 / (1.0 + jnp.exp(-gate_pre))
-    act = gate_pre * sig
-    hidden = (act * up_pre).astype(bf16).astype(f32)
-    grads = jnp.sum(hidden * down_grad, axis=-1, keepdims=True).astype(bf16).astype(f32)
-    gate_grad = (down_grad * up_pre * sig * (1.0 + gate_pre * (1.0 - sig))).astype(bf16)
-    up_grad = (down_grad * act).astype(bf16)
+    grads = expert_slopes(gate_pre, up_pre, down_grad, gate_grad, up_grad)
     for j in range(8):
         part = pl.ds(j * 256, 256)
-        put_rows(wide_ref, j, dot(gate_grad, gate_ref[part, :], ACROSS) + dot(up_grad, up_ref[part, :], ACROSS))
-    p, lane = iota((SLOTS, 128), 0), iota((SLOTS, 128), 1)
-    gather = marks(iota((PEERS * 8, SLOTS), 1) // MOST == iota((PEERS * 8, SLOTS), 0) // 8)
-    spread = jnp.where(lane == p % MOST + place * MOST, grads, 0.0)
-    return dot(gather, spread.astype(bf16))
+        rows = dot(gate_grad[...], gate_ref[part, :], ACROSS) + dot(up_grad[...], up_ref[part, :], ACROSS)
+        put_rows(wide_ref, j, rows)
+    return small_grads(grads, place)
 
 
 def near_experts(
-    got_ref, gate_hbm, up_hbm, down_hbm, back_ref, small_ref, wide_ref, gate_ref, up_ref, down_ref, sems
-):
-    weights = ((gate_hbm, gate_ref), (up_hbm, up_ref), (down_hbm, down_ref))
-    small_ref[...] = behind_half(got_ref, weights, 0, wide_ref, sems)
+    got_ref, gate_hbm, up_hbm, down_hbm, back_ref, small_ref, wide_ref, gate_ref, up_ref, down_ref, sems,
+    gate_sum, up_sum, down_sum, gate_grad, up_grad
+):
+    copies = fetched(((gate_hbm, gate_ref), (up_hbm, up_ref), (down_hbm, down_ref)), sems)
+
+    def take(d, rows):
+        for lane in range(2):
+            for kind in range(2):
+                wide_ref[lane, area_rows(d, kind), :] = got_ref[d, pl.ds(kind * ROWS, ROWS), LANES[lane]].astype(f32)
+
+    each_peer(take)
+    for ref in (gate_sum, up_sum, down_sum):
+        ref[...] = jnp.zeros((SLOTS, FF), f32)
+    for copy in copies:
+        copy.wait()
+
+    def inward(j):
+        rows = jnp.concatenate([get_rows(wide_ref, 2 * j + i, SLOTS) for i in range(2)], axis=1)
+        gate_sum[...] += dot(rows, gate_ref[columns(j, 512), :])
+        up_sum[...] += dot(rows, up_ref[columns(j, 512), :])
+        rows = jnp.concatenate([get_rows(wide_ref, 2 * j + i, SLOTS, AREA) for i in range(2)], axis=1)
+        down_sum[...] += dot(rows, down_ref[:, columns(j, 512)], ACROSS)
+
+    loop(4, inward)
+    grads = expert_slopes(gate_sum[...], up_sum[...], down_sum[...], gate_grad, up_grad)
+
+    def outward(j):
+        part = columns(j, 256)
+        rows = dot(gate_grad[...], gate_ref[part, :], ACROSS) + dot(up_grad[...], up_ref[part, :], ACROSS)
+        put_rows(wide_ref, j, rows)
+
+    loop(8, outward)
+    small_ref[...] = small_grads(grads, 0)
 
     def put(d, rows):
         for lane in range(2):
@@ -327,10 +365,11 @@
 
 
 def far_experts(
-    got_ref, near_ref, near_small_ref, gate_hbm, up_hbm, down_hbm, back_ref, wide_ref, gate_ref, up_ref, down_ref, sems
+    got_ref, near_ref, near_small_ref, gate_hbm, up_hbm, down_hbm, back_ref, wide_ref, gate_ref, up_ref, down_ref, sems,
+    gate_grad, up_grad
 ):
     weights = ((gate_hbm, gate_ref), (up_hbm, up_ref), (down_hbm, down_ref))
-    small = behind_half(got_ref, weights, 1, wide_ref, sems) + near_small_ref[...]
+    small = behind_half(got_ref, weights, 1, wide_ref, sems, gate_grad, up_grad) + near_small_ref[...]
     wide_ref[0, pl.ds(AREA, PEERS * 8), :] = small
 
     def put(d, rows):
@@ -344,6 +383,7 @@
     each_peer(put)
 
 
+GRADS = [pltpu.VMEM((SLOTS, FF), bf16)] * 2
 WEIGHTS = [
     pltpu.VMEM((D, FF), bf16),
     pltpu.VMEM((D, FF), bf16),
@@ -357,7 +397,7 @@
         near_experts,
         (shape((PEERS, ROWS, 256)), shape((PEERS * 8, 128), f32)),
         [VMEM] + [HBM] * 3,
-        [pltpu.VMEM((2, 2 * AREA, 128), f32)] + WEIGHTS,
+        [pltpu.VMEM((2, 2 * AREA, 128), f32)] + WEIGHTS + [pltpu.VMEM((SLOTS, FF), f32)] * 3 + GRADS,
         args,
         5 * 10**9,
         13,
@@ -369,7 +409,7 @@
         far_experts,
         (shape((PEERS, 2 * ROWS + 8, 256)),),
         [VMEM] * 3 + [HBM] * 3,
-        [pltpu.VMEM((2, 2 * AREA, 128), f32)] + WEIGHTS,
+        [pltpu.VMEM((2, 2 * AREA, 128), f32)] + WEIGHTS + GRADS,
         args,
         5 * 10**9,
         15,
@@ -404,18 +444,15 @@
     hidden_ref[...] = (gate_pre / (1.0 + jnp.exp(-gate_pre)) * up_sum[...]).astype(bf16)
     copies[2].wait()
 
-    def outward(c):
-        for part in range(2):
-            made = dot(hidden_ref[...], down_ref[:, columns(part * 4 + c, 256)])
-            for i in range(2):
-                wide_ref[part, pl.ds(2 * c + i, count, stride=8), :] = made[:, i * 128 : i * 128 + 128]
-
-    loop(4, outward)
+    def outward(j):
+        put_rows(wide_ref, j, dot(hidden_ref[...], down_ref[:, columns(j, 256)]))
+
+    loop(8, outward)
 
     def put(d, rows):
-        for half in range(2):
-            first_ref[d, pl.ds(half * ROWS, ROWS), :] = wide_ref[0, area_rows(d, half), :].astype(bf16)
-            second_ref[d, pl.ds(half * ROWS, ROWS), :] = wide_ref[1, area_rows(d, half), :].astype(bf16)
+        for lane in range(2):
+            first_ref[d, :, LANES[lane]] = wide_ref[lane, area_rows(d, 1), :].astype(bf16)
+            second_ref[d, :, LANES[lane]] = wide_ref[lane, area_rows(d, 0), :].astype(bf16)
 
     each_peer(put)
 
@@ -423,7 +460,7 @@
 def run_ahead_experts(*args):
     return call(
         ahead_experts,
-        (shape((PEERS, 2 * ROWS, 128)), shape((PEERS, 2 * ROWS, 128))),
+        (shape((PEERS, ROWS, 256)), shape((PEERS, ROWS, 256))),
         [VMEM] * 2 + [HBM] * 3,
         [pltpu.VMEM((2, 2 * AREA, 128), f32)]
         + WEIGHTS
@@ -469,62 +506,78 @@
     return inv * (scaled - unit * jnp.mean(scaled * unit, axis=-1, keepdims=True))
 
 
-def behind_sums(
-    zh_ref, home_ref, near_hot_ref, far_hot_ref, near_probs_ref, far_probs_ref, near_x_ref, far_x_ref, gain_ref,
-    sums_ref, sent_ref, note_ref, mine_ref, wide_ref, line_ref, mix_ref
-):
-    zh = zh_ref[0]
-
-    def take(d, rows):
-        for half in range(2):
-            for lane in range(2):
-                wide_ref[lane, area_rows(d, half), :] = home_ref[d, pl.ds(half * ROWS, ROWS), LANES[lane]].astype(f32)
-        wide_ref[0, pl.ds(pl.multiple_of(2 * AREA + d * 8, 8), 8), :] = home_ref[
-            d, pl.ds(2 * ROWS, 8), LANES[0]
-        ].astype(f32)
-
-    each_peer(take)
-    pick = picks(iota((SLOTS, EXPERTS), 0) // MOST, zh)
-    near_mix = near_hot_ref[...] * dot(pick, near_probs_ref[...].astype(bf16)).astype(bf16)
-    far_mix = far_hot_ref[...] * dot(pick, far_probs_ref[...].astype(bf16)).astype(bf16)
-    small = wide_ref[0, pl.ds(2 * AREA, PEERS * 8), :].astype(bf16)
+def behind_note(zh_ref, home_ref, near_hot_ref, far_hot_ref, note_ref):
+    pick = picks(iota((SLOTS, EXPERTS), 0) // MOST, zh_ref[0]).astype(f32)
+    small = jnp.concatenate([home_ref[d].astype(f32) for d in range(PEERS)], axis=0)[:, :128].astype(bf16)
     share = marks(iota((SLOTS, PEERS * 8), 0) // MOST * 8 == iota((SLOTS, PEERS * 8), 1))
     small = dot(share, small)
     p, lane = iota((SLOTS, 128), 0) % MOST, iota((SLOTS, 128), 1)
     for half, hot in enumerate((near_hot_ref, far_hot_ref)):
         grads = jnp.sum(jnp.where(lane == p + half * MOST, small, 0.0), axis=-1, keepdims=True)
-        note_ref[pl.ds(0, EXPERTS), pl.ds(half * TOK, TOK)] = dot(
-            (pick.astype(f32) * grads).astype(bf16), hot[...], DOWN
-        )
-    mix_ref[0] = near_mix
-    mix_ref[1] = far_mix
-
-    def gather(j):
-        cols = columns(j, 256)
+        note_ref[:, pl.ds(half * TOK, TOK)] = dot((pick * grads).astype(bf16), hot[...], DOWN)
+
+
+def whole(a):
+    return pl.BlockSpec(a.shape, lambda i, n=a.ndim: (0,) * n)
+
+
+def run_behind_note(zh, home, near_hot, far_hot):
+    tail = pl.BlockSpec((PEERS, 8, 256), lambda i: (0, 2 * ROWS // 8, 0))
+    return pl.pallas_call(
+        behind_note,
+        grid=(1,),
+        out_shape=shape((EXPERTS, 2 * TOK), f32),
+        in_specs=[SMEM, tail, whole(near_hot), whole(far_hot)],
+        out_specs=pl.BlockSpec((EXPERTS, 2 * TOK), lambda i: (0, 0)),
+        compiler_params=pltpu.CompilerParams(vmem_limit_bytes=63 * 2**20),
+        cost_estimate=pl.CostEstimate(flops=10**7, transcendentals=0, bytes_accessed=2**18),
+    )(zh, home, near_hot, far_hot)
+
+
+def behind_sums(
+    zh_ref, home_ref, near_hot_ref, far_hot_ref, near_probs_ref, far_probs_ref, near_x_ref, far_x_ref, gain_ref,
+    sums_ref, sent_ref, theirs_ref, mine_ref, wide_ref, line_ref, mix_ref
+):
+    zh = zh_ref[0]
+
+    def take(d, rows):
+        for half in range(2):
+            for lane in range(2):
+                wide_ref[lane, area_rows(d, half), :] = home_ref[d, pl.ds(half * ROWS, ROWS), LANES[lane]].astype(f32)
+
+    each_peer(take)
+    pick = picks(iota((SLOTS, EXPERTS), 0) // MOST, zh)
+    mix_ref[0] = mixed_by(near_hot_ref[...], pick, near_probs_ref[...])
+    mix_ref[1] = mixed_by(far_hot_ref[...], pick, far_probs_ref[...])
+
+    for j in range(8):
+        cols = pl.ds(j * 256, 256)
         sums_ref[:, cols] = dot(mix_ref[0], get_rows(wide_ref, j, SLOTS), DOWN)
         line_ref[:, cols] = dot(mix_ref[1], get_rows(wide_ref, j, SLOTS, AREA), DOWN)
-
-    loop(8, gather)
     inv, unit = unit_rows(far_x_ref[...])
     sums = line_ref[...]
     sent_ref[...] = through_norm(sums, gain_ref[...], inv, unit).astype(bf16)
     total = jnp.sum(sums * unit, axis=0, keepdims=True)
     _, unit = unit_rows(near_x_ref[...])
     total = total + jnp.sum(sums_ref[...] * unit, axis=0, keepdims=True)
-    note_ref[pl.ds(EXPERTS, 8), :] = jnp.zeros((8, 256), f32)
+    theirs_ref[...] = jnp.zeros((8, 256), f32)
     mine_ref[...] = jnp.zeros((8, 256), f32)
     for x in range(4):
         first, second = total[:, x * 512 : x * 512 + 256], total[:, x * 512 + 256 : x * 512 + 512]
         mine_ref[pl.ds(x, 1), :] = jnp.where(zh == 0, first, second)
-        note_ref[pl.ds(EXPERTS + x, 1), :] = jnp.where(zh == 0, second, first)
+        theirs_ref[pl.ds(x, 1), :] = jnp.where(zh == 0, second, first)
 
 
 def run_behind_sums(*args):
     return call(
         behind_sums,
-        (shape((TOK, D), f32), shape((TOK, D)), shape((EXPERTS + 8, 256), f32), shape((8, 256), f32)),
+        (shape((TOK, D), f32), shape((TOK, D)), shape((8, 256), f32), shape((8, 256), f32)),
         [SMEM] + [VMEM] * 8,
-        [pltpu.VMEM((2, 2 * AREA + PEERS * 8, 128), f32), pltpu.VMEM((TOK, D), f32), pltpu.VMEM((2, SLOTS, TOK), bf16)],
+        [
+            pltpu.VMEM((2, 2 * AREA, 128), f32),
+            pltpu.VMEM((TOK, D), f32),
+            pltpu.VMEM((2, SLOTS, TOK), bf16),
+        ],
         args,
         10**9,
         6,
@@ -532,91 +585,96 @@
 
 
 def behind_end(
-    zh_ref, near_note_ref, far_note_ref, mine_ref, sums_ref, near_probs_ref, far_probs_ref, near_normed_ref,
-    far_normed_ref, near_x_ref, far_x_ref, g_ref, gain_ref, table_ref, sent_ref, shares_ref
-):
-    zh = zh_ref[0]
+    near_note_ref, far_note_ref, sums_ref, near_probs_ref, far_probs_ref, x_ref, g_ref, gain_ref, table_ref,
+    sent_ref, near_logit_ref, far_logit_ref
+):
     near_tok, far_tok = pl.ds(0, TOK), pl.ds(TOK, TOK)
-    rows = pl.ds(0, EXPERTS)
 
     def logit_grads(probs, grads):
         return (probs * (grads - jnp.sum(probs * grads, axis=0, keepdims=True))).astype(bf16)
 
-    near_logit = logit_grads(near_probs_ref[...], near_note_ref[rows, near_tok] + far_note_ref[rows, far_tok])
-    far_logit = logit_grads(far_probs_ref[...], near_note_ref[rows, far_tok] + far_note_ref[rows, near_tok])
-    inv, near_unit = unit_rows(near_x_ref[...])
+    near_logit_ref[...] = logit_grads(near_probs_ref[...], near_note_ref[:, near_tok] + far_note_ref[:, far_tok])
+    far_logit_ref[...] = logit_grads(far_probs_ref[...], near_note_ref[:, far_tok] + far_note_ref[:, near_tok])
+    inv, unit = unit_rows(x_ref[...])
+    sums = sums_ref[...] + dot(near_logit_ref[...], table_ref[...], DOWN)
+    sent_ref[...] = (g_ref[...].astype(f32) + through_norm(sums, gain_ref[...], inv, unit)).astype(bf16)
+
+
+def run_behind_end(*args):
+    return call(
+        behind_end,
+        (shape((TOK, D)), shape((EXPERTS, TOK)), shape((EXPERTS, TOK))),
+        [VMEM] * 9,
+        [],
+        args,
+        10**9,
+        4,
+    )
+
+
+def share_parts(
+    zh_ref, near_logit_ref, far_logit_ref, mine_ref, theirs_ref, near_normed_ref, far_normed_ref, near_x_ref,
+    far_x_ref, table_ref, shares_ref
+):
+    zh = zh_ref[0]
+    near_logit, far_logit = near_logit_ref[...], far_logit_ref[...]
+    _, near_unit = unit_rows(near_x_ref[...])
     _, far_unit = unit_rows(far_x_ref[...])
-    near_term = dot(near_logit, table_ref[...], DOWN)
-    sums = sums_ref[...] + near_term
-    sent_ref[...] = (g_ref[...].astype(f32) + through_norm(sums, gain_ref[...], inv, near_unit)).astype(bf16)
-    far_term = dot(far_logit, table_ref[...], DOWN)
+    near_term, far_term = dot(near_logit, table_ref[...], DOWN), dot(far_logit, table_ref[...], DOWN)
     total = jnp.sum(near_term * near_unit + far_term * far_unit, axis=0, keepdims=True)
     row = iota((128 - EXPERTS, 256), 0)
     for x in range(4):
         first, second = total[:, x * 512 : x * 512 + 256], total[:, x * 512 + 256 : x * 512 + 512]
-        gains = (
-            jnp.where(zh == 0, first, second)
-            + mine_ref[pl.ds(x, 1), :]
-            + far_note_ref[pl.ds(EXPERTS + x, 1), :]
-        )
+        gains = jnp.where(zh == 0, first, second) + mine_ref[pl.ds(x, 1), :] + theirs_ref[pl.ds(x, 1), :]
         cols = pl.ds(pl.multiple_of(x * 512 + zh * 256, 256), 256)
         part = dot(near_logit, near_normed_ref[:, cols]) + dot(far_logit, far_normed_ref[:, cols])
         both = jnp.concatenate([part, jnp.where(row == 0, gains, 0.0)], axis=0)
         shares_ref[pl.ds(x * 256, 256), :] = both.T
 
 
-def run_behind_end(*args):
-    return call(
-        behind_end,
-        (shape((TOK, D)), shape((D // 2, 128), f32)),
-        [SMEM] + [VMEM] * 13,
-        [],
-        args,
-        10**9,
-        6,
-    )
-
-
-def ahead_end(home_ref, near_mix_ref, far_mix_ref, resid_ref, near_ref, far_ref, wide_ref):
+def run_share_parts(*args):
+    return call(share_parts, (shape((D // 2, 128), f32),), [SMEM] + [VMEM] * 9, [], args, 10**9, 3)[0]
+
+
+def ahead_sums(home_ref, mix_ref, wide_ref):
     def take(d, rows):
-        for half in range(2):
-            wide_ref[0, area_rows(d, half), :] = home_ref[d, pl.ds(half * ROWS, ROWS), :].astype(f32)
+        for lane in range(2):
+            wide_ref[lane, rows, :] = home_ref[d, :, LANES[lane]].astype(f32)
 
     each_peer(take)
-    for c in range(4):
-        cols = pl.ds(c * 256, 256)
-        for half, (mix_ref, out_ref) in enumerate(((near_mix_ref, near_ref), (far_mix_ref, far_ref))):
-            rows = jnp.concatenate([get_rows(wide_ref, 2 * c + i, SLOTS, half * AREA) for i in range(2)], axis=1)
-            sums = dot(mix_ref[...], rows, DOWN)
-            if half == 0:
-                sums = sums + resid_ref[:, cols].astype(f32)
-            out_ref[:, cols] = sums.astype(bf16)
-
-
-def run_ahead_end(home, near_mix, far_mix, resid, part):
-    columns = pl.BlockSpec((TOK, D // 2), lambda i: (0, part))
-    whole = [pl.BlockSpec(a.shape, lambda i, n=a.ndim: (0,) * n) for a in (home, near_mix, far_mix)]
-    half = pl.BlockSpec((TOK, D // 2), lambda i: (0, 0))
-    return pl.pallas_call(
-        ahead_end,
-        grid=(1,),
-        out_shape=(shape((TOK, D // 2)), shape((TOK, D // 2))),
-        in_specs=whole + [columns],
-        out_specs=(half, half),
-        scratch_shapes=[pltpu.VMEM((1, 2 * AREA, 128), f32)],
-        compiler_params=pltpu.CompilerParams(vmem_limit_bytes=63 * 2**20),
-        cost_estimate=pl.CostEstimate(flops=10**9, transcendentals=0, bytes_accessed=3 * 2**20),
-    )(home, near_mix, far_mix, resid)
-
-
-def final_add(a_ref, b_ref, c_ref, d_ref, out_ref):
-    half = D // 2
-    out_ref[:, pl.ds(0, half)] = (a_ref[...].astype(f32) + b_ref[...].astype(f32)).astype(bf16)
-    out_ref[:, pl.ds(half, half)] = (c_ref[...].astype(f32) + d_ref[...].astype(f32)).astype(bf16)
-
-
-def run_final_add(*args):
-    return call(final_add, (shape((TOK, D)),), [VMEM] * 4, [], args, 10**6, 2)[0]
+    for j in range(8):
+        yield pl.ds(j * 256, 256), dot(mix_ref[...], get_rows(wide_ref, j, SLOTS), DOWN)
+
+
+def ahead_far(home_ref, mix_ref, out_ref, wide_ref):
+    for cols, sums in ahead_sums(home_ref, mix_ref, wide_ref):
+        out_ref[:, cols] = sums.astype(bf16)
+
+
+def ahead_near(home_ref, mix_ref, resid_ref, out_ref, wide_ref):
+    for cols, sums in ahead_sums(home_ref, mix_ref, wide_ref):
+        out_ref[:, cols] = (resid_ref[:, cols].astype(f32) + sums).astype(bf16)
+
+
+def run_ahead_end(kernel, *args):
+    return call(
+        kernel, (shape((TOK, D)),), [VMEM] * len(args), [pltpu.VMEM((2, AREA, 128), f32)], args, 10**9, 3
+    )[0]
+
+
+def share_sums(got_ref, router_ref, gain_ref):
+    total = got_ref[0]
+    for source in range(1, PEERS):
+        total = total + got_ref[source]
+    total = total * factor
+    router_ref[...] = total[:, :EXPERTS]
+    gain_ref[...] = total.T[EXPERTS : EXPERTS + 1, :]
+
+
+def run_share_sums(got):
+    return call(
+        share_sums, (shape((PEERS, EXPERTS), f32), shape((1, PEERS), f32)), [VMEM], [], (got,), 10**6, 1
+    )
 
 
 def body(
@@ -673,33 +731,32 @@
     made_1, made_2 = run_ahead_experts(got_1, got_3, *weights)
     made_1, home_b = lax.optimization_barrier((made_1, home_b))
     home_1 = spread_out(made_1)
-    sums_b, own_c, note, mine = run_behind_sums(
+    note = run_behind_note(zh, home_b, hot_b, hot_c)
+    far_note = swapped(note)
+    sums_b, own_c, theirs, mine = run_behind_sums(
         zh, home_b, hot_b, hot_c, probs_b, probs_c, back_x, x_far, gain
     )
-    far_note = swapped(note)
     moved_c = moved(own_c, False, -1)
-    own_b, shares = run_behind_end(
-        zh, note, far_note, mine, sums_b, probs_b, probs_c, normed_b, normed_c, back_x, x_far, back_g, gain, table
+    own_b, logit_b, logit_c = run_behind_end(
+        note, far_note, sums_b, probs_b, probs_c, back_x, back_g, gain, table
     )
     moved_b = moved(own_b, True, -1)
     made_2, home_1 = lax.optimization_barrier((made_2, home_1))
     home_2 = spread_out(made_2)
-    own_f1, own_h1 = run_ahead_end(home_1, mix_f, mix_h, resid, 0)
-    moved_h1 = moved(own_h1, False, 1)
-    moved_f1 = moved(own_f1, True, 1)
-    own_f2, own_h2 = run_ahead_end(home_2, mix_f, mix_h, resid, 1)
-    moved_h2 = moved(own_h2, False, 1)
-    moved_f2 = moved(own_f2, True, 1)
-    shares, own_f2 = lax.optimization_barrier((shares, own_f2))
-    total = jnp.sum(spread_out(shares.reshape(PEERS, PEERS, 128)), axis=0) * factor
+    own_h = run_ahead_end(ahead_far, home_1, mix_h)
+    moved_h = moved(own_h, False, 1)
+    theirs = swapped(theirs)
+    shares = run_share_parts(
+        zh, logit_b, logit_c, mine, theirs, normed_b, normed_c, back_x, x_far, table
+    )
+    own_f = run_ahead_end(ahead_near, home_2, mix_f, resid)
+    moved_f = moved(own_f, True, 1)
+    shares, own_f = lax.optimization_barrier((shares, own_f))
+    got_s = spread_out(shares.reshape(PEERS, PEERS, 128))
+    router_grad, gain_grad = run_share_sums(got_s)
     input_grad = (moved_b.astype(f32) + moved_c.astype(f32)).astype(bf16)
-    forward_output = run_final_add(moved_f1, moved_h1, moved_f2, moved_h2)
-    return (
-        forward_output[None],
-        input_grad[None],
-        total[None, :, :EXPERTS],
-        total[:, EXPERTS][None],
-    )
+    forward_output = (moved_f.astype(f32) + moved_h.astype(f32)).astype(bf16)
+    return forward_output[None], input_grad[None], router_grad[None], gain_grad
 
 
 def solution(mesh):

time: 317 us -> 317 us (level)
  starting transfers between devices: 108 us -> 96.3 us
  waiting for transfers between devices: 92.8 us -> 97.7 us
  Pallas kernels: 82.3 us -> 86.7 us
    ppermute x6 -> x4, waiting for transfers between devices: 29.7 us -> 0.01 us  [moved(): return lax.ppermute(x, ('pipe', 'zh'), pairs)]
    ppermute x5 -> x6, waiting for transfers between devices: 40 us -> 65.8 us  [swapped(): return lax.ppermute(x, 'zh', [(0, 1), (1, 0)])]
    ppermute x6 -> x4, starting transfers between devices: 17.1 us -> 2.17 us  [moved(): return lax.ppermute(x, ('pipe', 'zh'), pairs)]
    all_to_all x6, waiting for transfers between devices: 23.1 us -> 31.9 us  [spread_out(): return lax.all_to_all(x, XY, 0, 0, tiled=True)]
    pallas_call x10 -> x13, Pallas kernels: 76.4 us -> 84.5 us  [call(): pl.pallas_call(kernel, out_shape=outs, in_specs=ins, out_specs=tuple((VME...]
    ppermute x5 -> x6, starting transfers between devices: 24.8 us -> 29.2 us  [swapped(): return lax.ppermute(x, 'zh', [(0, 1), (1, 0)])]
    pallas_call x2 -> x1, Pallas kernels: 5.89 us -> 2.18 us  [run_behind_note(): pl.pallas_call(behind_note, grid=(1,), out_shape=shape((EXPERTS, 2 * TOK)...]
  transfers between devices with their start and end apart: 17 -> 16, of which waited for: 7 -> 7; matrix products, arithmetic and copies ran while one was open for 1% -> 1% of each run, Pallas kernels for 23% -> 24%
where the time goes in v1:
time: 317 us; the launch traced here: 316 us
  waiting for transfers between devices  97.7 us (31%)
  starting transfers between devices  96.3 us (30%)
  Pallas kernels  86.7 us (27%)
  blocking collectives  24.2 us (8%)
  local copies, waits for them, and re-layouts  5.04 us (2%)
  other arithmetic  4.25 us (1%)
    pallas_call x13, Pallas kernels, call(): pl.pallas_call(kernel, out_shape=outs, in_specs=ins, out_specs=tuple((VME...  84.5 us
    ppermute x6, waiting for transfers between devices, swapped(): return lax.ppermute(x, 'zh', [(0, 1), (1, 0)])  65.8 us
    all_to_all x6, starting transfers between devices, spread_out(): return lax.all_to_all(x, XY, 0, 0, tiled=True)  65 us
    all_to_all x6, waiting for transfers between devices, spread_out(): return lax.all_to_all(x, XY, 0, 0, tiled=True)  31.9 us
    ppermute x6, starting transfers between devices, swapped(): return lax.ppermute(x, 'zh', [(0, 1), (1, 0)])  29.2 us
    all_to_all x1, blocking collectives, spread_out(): return lax.all_to_all(x, XY, 0, 0, tiled=True)  24.2 us
  transfers between devices with their start and end apart: 16, of which 7 were waited for; matrix products, arithmetic and copies ran while one was open for 1% of the time, Pallas kernels for 24%

profile of v1, /device:TPU:1, one launch (start us, length us, event | category | flops | bytes accessed | tf_op | source)
XLA Modules:
  0.0 315.6 jit_solution(16367174180569164270)
XLA Ops:
  4.9 6.6 %shard_map.184 = (bf16[32,216,256]{2,1,0:T(8,128)(2,1)}, bf16[128,2048]{1,0:T(8,128)(2,1)}, bf16[288,128]{1,0:T(8,128)(2,1)}, f32[64,128]{1,0:T(8,128)}, bf16[288,128]{1,0:T(8,128)(2,1)}) custom-call(s32[1]{0:T(128)} %bitcast.zh_ref, s32[4,128]{1,0:T(4,128)} %bitcast.33, s32[4,128]{1,0:T(4,128)} %bitcast.35, bf16[128,2048]{1,0:T(8,128)(2,1)} %bitcast.28, ...), custom_call_target="tpu_custom_call" | custom-call | flops 2000000000 | bytes 8388608 | tf_op jit(solution)/shard_map/pallas_call | solution.py:58
  11.6 8.8 %all-to-all-start = ((bf16[32,216,256]{2,1,0:T(8,128)(2,1)}), bf16[32,216,256]{2,1,0:T(8,128)(2,1)}, u32[]{:S(2)}, u32[]{:S(2)}) async-start(bf16[32,216,256]{2,1,0:T(8,128)(2,1)} %get-tuple-element.38), calls=%async_computation | async-start | bytes 7077888 | tf_op jit(solution)/shard_map/all_to_all | solution.py:37
  20.4 7.0 %collective-permute-start.2 = (bf16[128,2048]{1,0:T(8,128)(2,1)S(1)}, bf16[128,2048]{1,0:T(8,128)(2,1)S(1)}, u32[]{:S(2)}, u32[]{:S(2)}) collective-permute-start(bf16[128,2048]{1,0:T(8,128)(2,1)S(1)} %bitcast.32), channel_id=1, source_target_pairs={{0,8},{8,0},{1,9},{9,1},{2,10},{10,2},{3,11},{11,3},{4,12},{12,4},... | collective-permute-start | bytes 1572872 | tf_op jit(solution)/shard_map/ppermute | solution.py:41
  27.5 5.4 %collective-permute-start = (s32[8,128]{1,0:T(8,128)S(1)}, s32[8,128]{1,0:T(8,128)S(1)}, u32[]{:S(2)}, u32[]{:S(2)}) collective-permute-start(s32[8,128]{1,0:T(8,128)S(1)} %pad_add_fusion), channel_id=1, source_target_pairs={{0,8},{8,0},{1,9},{9,1},{2,10},{10,2},{3,11},{11,3},{4,12},{12,4},... | collective-permute-start | bytes 12296 | tf_op jit(solution)/shard_map/ppermute | solution.py:41
  32.8 23.8 %collective-permute-done = s32[8,128]{1,0:T(8,128)S(1)} collective-permute-done((s32[8,128]{1,0:T(8,128)S(1)}, s32[8,128]{1,0:T(8,128)S(1)}, u32[]{:S(2)}, u32[]{:S(2)}) %collective-permute-start) | collective-permute-done | bytes 4128 | tf_op jit(solution)/shard_map/ppermute | solution.py:41
  58.8 5.2 %shard_map.186 = (bf16[32,144,256]{2,1,0:T(8,128)(2,1)}, bf16[128,2048]{1,0:T(8,128)(2,1)}, bf16[288,128]{1,0:T(8,128)(2,1)}, f32[64,128]{1,0:T(8,128)}) custom-call(s32[1]{0:T(128)} %bitcast.zh_ref, s32[4,128]{1,0:T(4,128)} %get-tuple-element.72.ids_ref, bf16[128,2048]{1,0:T(8,128)(2,1)} %copy-done.2, bf16[128,2048]{1,0:T(8,128)(2,1)} %copy-done.7, ...), custom_call_target="tpu_custom_call" | custom-call | flops 1000000000 | bytes 6291456 | tf_op jit(solution)/shard_map/pallas_call | solution.py:58
  64.3 23.2 %all-to-all-start.1 = ((bf16[32,144,256]{2,1,0:T(8,128)(2,1)}), bf16[32,144,256]{2,1,0:T(8,128)(2,1)}, u32[]{:S(2)}, u32[]{:S(2)}) async-start(bf16[32,144,256]{2,1,0:T(8,128)(2,1)} %get-tuple-element.41), calls=%async_computation.1 | async-start | bytes 4718592 | tf_op jit(solution)/shard_map/all_to_all | solution.py:37
  87.5 6.2 %collective-permute-start.1 = (bf16[128,2048]{1,0:T(8,128)(2,1)S(1)}, bf16[128,2048]{1,0:T(8,128)(2,1)S(1)}, u32[]{:S(2)}, u32[]{:S(2)}) collective-permute-start(bf16[128,2048]{1,0:T(8,128)(2,1)S(1)} %copy-done.6), channel_id=1, source_target_pairs={{0,8},{8,0},{1,9},{9,1},{2,10},{10,2},{3,11},{11,3},{4,12},{12,4},... | collective-permute-start | bytes 1572872 | tf_op jit(solution)/shard_map/ppermute | solution.py:41
  93.7 13.8 %collective-permute-done.1.x_ref = bf16[128,2048]{1,0:T(8,128)(2,1)S(1)} collective-permute-done((bf16[128,2048]{1,0:T(8,128)(2,1)S(1)}, bf16[128,2048]{1,0:T(8,128)(2,1)S(1)}, u32[]{:S(2)}, u32[]{:S(2)}) %collective-permute-start.1) | collective-permute-done | bytes 524320 | tf_op jit(solution)/shard_map/ppermute | solution.py:41
  108.3 5.0 %shard_map.185 = (bf16[32,72,256]{2,1,0:T(8,128)(2,1)}, bf16[288,128]{1,0:T(8,128)(2,1)}) custom-call(s32[1]{0:T(128)} %bitcast.zh_ref, s32[4,128]{1,0:T(4,128)} %get-tuple-element.73.ids_ref, bf16[128,2048]{1,0:T(8,128)(2,1)} %copy-done.8, f32[1,2048]{1,0:T(1,128)} %gain_ref.9, bf16[64,2048]{1,0:T(8,128)(2,1)} %bitcast.53), custom_call_target="tpu_custom_call" | custom-call | flops 1000000000 | bytes 4194304 | tf_op jit(solution)/shard_map/pallas_call | solution.py:58
  113.3 5.4 %all-to-all-done.1.got_ref = bf16[32,144,256]{2,1,0:T(8,128)(2,1)} async-done(((bf16[32,144,256]{2,1,0:T(8,128)(2,1)}), bf16[32,144,256]{2,1,0:T(8,128)(2,1)}, u32[]{:S(2)}, u32[]{:S(2)}) %all-to-all-start.1) | async-done | bytes 2359328 | tf_op jit(solution)/shard_map/all_to_all | solution.py:37
  118.7 11.3 %all-to-all-start.2 = ((bf16[32,72,256]{2,1,0:T(8,128)(2,1)}), bf16[32,72,256]{2,1,0:T(8,128)(2,1)}, u32[]{:S(2)}, u32[]{:S(2)}) async-start(bf16[32,72,256]{2,1,0:T(8,128)(2,1)} %get-tuple-element.45), calls=%async_computation.2 | async-start | bytes 2359296 | tf_op jit(solution)/shard_map/all_to_all | solution.py:37
  130.0 15.7 %shard_map.187 = (bf16[32,72,256]{2,1,0:T(8,128)(2,1)}, f32[256,128]{1,0:T(8,128)}) custom-call(bf16[32,216,256]{2,1,0:T(8,128)(2,1)} %all-to-all-done.got_ref.near_ref, bf16[2048,768]{1,0:T(8,128)(2,1)} %bitcast.37, bf16[2048,768]{1,0:T(8,128)(2,1)} %bitcast.40, bf16[768,2048]{1,0:T(8,128)(2,1)} %bitcast.43), custom_call_target="tpu_custom_call" | custom-call | flops 5000000000 | bytes 13631488 | tf_op jit(solution)/shard_map/pallas_call | solution.py:58
  145.6 12.7 %shard_map.188 = bf16[32,152,256]{2,1,0:T(8,128)(2,1)} custom-call(bf16[32,144,256]{2,1,0:T(8,128)(2,1)} %all-to-all-done.1.got_ref, bf16[32,72,256]{2,1,0:T(8,128)(2,1)} %get-tuple-element.43.near_ref, f32[256,128]{1,0:T(8,128)} %get-tuple-element.44.near_small_ref, bf16[2048,768]{1,0:T(8,128)(2,1)} %bitcast.38, bf16[2048,768]{1,0:T(8,128)(2,1)} %bitcast.41, ...), custom_call_target="tpu_custom_call" | custom-call | flops 5000000000 | bytes 15728640 | tf_op jit(solution)/shard_map/pallas_call | solution.py:58
  158.4 7.4 %all-to-all-start.3 = ((bf16[32,152,256]{2,1,0:T(8,128)(2,1)}), bf16[32,152,256]{2,1,0:T(8,128)(2,1)}, u32[]{:S(2)}, u32[]{:S(2)}) async-start(bf16[32,152,256]{2,1,0:T(8,128)(2,1)} %shard_map.188), calls=%async_computation.3 | async-start | bytes 4980736 | tf_op jit(solution)/shard_map/all_to_all | solution.py:37
  165.8 15.8 %shard_map.189 = (bf16[32,72,256]{2,1,0:T(8,128)(2,1)}, bf16[32,72,256]{2,1,0:T(8,128)(2,1)}) custom-call(bf16[32,216,256]{2,1,0:T(8,128)(2,1)} %all-to-all-done.got_ref.near_ref, bf16[32,72,256]{2,1,0:T(8,128)(2,1)} %all-to-all-done.2.far_ref, bf16[2048,768]{1,0:T(8,128)(2,1)} %bitcast.39, bf16[2048,768]{1,0:T(8,128)(2,1)} %bitcast.42, ...), custom_call_target="tpu_custom_call" | custom-call | flops 6000000000 | bytes 14680064 | tf_op jit(solution)/shard_map/pallas_call | solution.py:58
  181.7 16.8 %all-to-all-done.3.home_ref = bf16[32,152,256]{2,1,0:T(8,128)(2,1)} async-done(((bf16[32,152,256]{2,1,0:T(8,128)(2,1)}), bf16[32,152,256]{2,1,0:T(8,128)(2,1)}, u32[]{:S(2)}, u32[]{:S(2)}) %all-to-all-start.3) | async-done | bytes 2490400 | tf_op jit(solution)/shard_map/all_to_all | solution.py:37
  198.4 24.2 %all_to_all.35.home_ref = bf16[32,72,256]{2,1,0:T(8,128)(2,1)} all-to-all(bf16[32,72,256]{2,1,0:T(8,128)(2,1)} %get-tuple-element.50), channel_id=1, replica_groups=mesh['pipe'=4,'x'=4,'zh'=2,'y'=4,'core'=2] {'x','y','core'}, dimensions={0} | all-to-all | bytes 2359296 | tf_op jit(solution)/shard_map/all_to_all | solution.py:37
  222.6 4.7 %all-to-all-start.5 = ((bf16[32,72,256]{2,1,0:T(8,128)(2,1)}), bf16[32,72,256]{2,1,0:T(8,128)(2,1)}, u32[]{:S(2)}, u32[]{:S(2)}) async-start(bf16[32,72,256]{2,1,0:T(8,128)(2,1)} %get-tuple-element.51), calls=%async_computation.5 | async-start | bytes 2359296 | tf_op jit(solution)/shard_map/all_to_all | solution.py:37
  229.4 6.1 %collective-permute-start.6 = (f32[64,256]{1,0:T(8,128)}, f32[64,256]{1,0:T(8,128)S(1)}, u32[]{:S(2)}, u32[]{:S(2)}) collective-permute-start(f32[64,256]{1,0:T(8,128)} %shard_map.192.near_note_ref), channel_id=1, source_target_pairs={{0,8},{8,0},{1,9},{9,1},{2,10},{10,2},{3,11},{11,3},{4,12},{12,4},... | collective-permute-start | bytes 196616 | tf_op jit(solution)/shard_map/ppermute | solution.py:41
  235.6 5.7 %shard_map.193 = (f32[128,2048]{1,0:T(8,128)}, bf16[128,2048]{1,0:T(8,128)(2,1)}, f32[8,256]{1,0:T(8,128)}, f32[8,256]{1,0:T(8,128)}) custom-call(s32[1]{0:T(128)} %bitcast.zh_ref, bf16[32,152,256]{2,1,0:T(8,128)(2,1)} %all-to-all-done.3.home_ref, bf16[288,128]{1,0:T(8,128)(2,1)} %get-tuple-element.56.near_hot_ref, ...), custom_call_target="tpu_custom_call" | custom-call | flops 1000000000 | bytes 6291456 | tf_op jit(solution)/shard_map/pallas_call | solution.py:58
  257.7 28.2 %collective-permute-done.9.theirs_ref = f32[8,256]{1,0:T(8,128)S(1)} collective-permute-done((f32[8,256]{1,0:T(8,128)S(1)}, f32[8,256]{1,0:T(8,128)S(1)}, u32[]{:S(2)}, u32[]{:S(2)}) %collective-permute-start.9) | collective-permute-done | bytes 8224 | tf_op jit(solution)/shard_map/ppermute | solution.py:41
  289.8 9.7 %all-to-all-start.6 = ((f32[32,32,128]{2,1,0:T(8,128)}), f32[32,32,128]{2,1,0:T(8,128)S(1)}, u32[]{:S(2)}, u32[]{:S(2)}) async-start(f32[32,32,128]{2,1,0:T(8,128)} %bitcast.27), calls=%async_computation.6 | async-start | bytes 1048576 | tf_op jit(solution)/shard_map/all_to_all | solution.py:37
  301.6 9.4 %all-to-all-done.6.got_ref = f32[32,32,128]{2,1,0:T(8,128)S(1)} async-done(((f32[32,32,128]{2,1,0:T(8,128)}), f32[32,32,128]{2,1,0:T(8,128)S(1)}, u32[]{:S(2)}, u32[]{:S(2)}) %all-to-all-start.6) | async-done | bytes 524320 | tf_op jit(solution)/shard_map/all_to_all | solution.py:37
  (51 shorter events, 36.1 us)
Async XLA Ops:
  11.5 8.8 %copy-start.1 = (bf16[1,128,2048]{2,1,0:T(8,128)(2,1)S(1)}, bf16[1,128,2048]{2,1,0:T(8,128)(2,1)}, u32[]{:S(2)}) copy-start(bf16[1,128,2048]{2,1,0:T(8,128)(2,1)} %param.29) | copy-start | bytes 1572868
  11.5 15.8 %copy-start.5 = (bf16[1,128,2048]{2,1,0:T(8,128)(2,1)S(1)}, bf16[1,128,2048]{2,1,0:T(8,128)(2,1)}, u32[]{:S(2)}) copy-start(bf16[1,128,2048]{2,1,0:T(8,128)(2,1)} %param.31) | copy-start | bytes 1572868
  11.5 15.9 %copy-start.3 = (s32[1,128,4]{1,2,0:T(4,128)S(1)}, s32[1,128,4]{1,2,0:T(4,128)}, u32[]{:S(2)}) copy-start(s32[1,128,4]{1,2,0:T(4,128)} %param.30) | copy-start | bytes 6148
  11.6 15.9 %copy-start.4 = (s32[1,128,4]{1,2,0:T(4,128)S(1)}, s32[1,128,4]{1,2,0:T(4,128)}, u32[]{:S(2)}) copy-start(s32[1,128,4]{1,2,0:T(4,128)} %param.28) | copy-start | bytes 6148
  11.6 52.7 %all-to-all-start = ((bf16[32,216,256]{2,1,0:T(8,128)(2,1)}), bf16[32,216,256]{2,1,0:T(8,128)(2,1)}, u32[]{:S(2)}, u32[]{:S(2)}) async-start(bf16[32,216,256]{2,1,0:T(8,128)(2,1)} %get-tuple-element.38), calls=%async_computation | async-start | bytes 7077888 | tf_op jit(solution)/shard_map/all_to_all | solution.py:37
  20.4 36.9 %collective-permute-start.2 = (bf16[128,2048]{1,0:T(8,128)(2,1)S(1)}, bf16[128,2048]{1,0:T(8,128)(2,1)S(1)}, u32[]{:S(2)}, u32[]{:S(2)}) collective-permute-start(bf16[128,2048]{1,0:T(8,128)(2,1)S(1)} %bitcast.32), channel_id=1, source_target_pairs={{0,8},{8,0},{1,9},{9,1},{2,10},{10,2},{3,11},{11,3},{4,12},{12,4},... | collective-permute-start | bytes 1572872 | tf_op jit(solution)/shard_map/ppermute | solution.py:41
  27.4 30.7 %collective-permute-start.3 = (bf16[128,2048]{1,0:T(8,128)(2,1)S(1)}, bf16[128,2048]{1,0:T(8,128)(2,1)S(1)}, u32[]{:S(2)}, u32[]{:S(2)}) collective-permute-start(bf16[128,2048]{1,0:T(8,128)(2,1)S(1)} %bitcast.50), channel_id=1, source_target_pairs={{0,8},{8,0},{1,9},{9,1},{2,10},{10,2},{3,11},{11,3},{4,12},{12,4},... | collective-permute-start | bytes 1572872 | tf_op jit(solution)/shard_map/ppermute | solution.py:41
  27.5 29.2 %collective-permute-start = (s32[8,128]{1,0:T(8,128)S(1)}, s32[8,128]{1,0:T(8,128)S(1)}, u32[]{:S(2)}, u32[]{:S(2)}) collective-permute-start(s32[8,128]{1,0:T(8,128)S(1)} %pad_add_fusion), channel_id=1, source_target_pairs={{0,8},{8,0},{1,9},{9,1},{2,10},{10,2},{3,11},{11,3},{4,12},{12,4},... | collective-permute-start | bytes 12296 | tf_op jit(solution)/shard_map/ppermute | solution.py:41
  57.2 0.8 copy-start.2
  58.0 0.8 copy-start.7
  64.3 23.2 %copy-start.6 = (bf16[128,2048]{1,0:T(8,128)(2,1)S(1)}, bf16[128,2048]{1,0:T(8,128)(2,1)}, u32[]{:S(2)}) copy-start(bf16[128,2048]{1,0:T(8,128)(2,1)} %shard_map.183.resid_ref) | copy-start | bytes 1572868
  64.3 54.4 %all-to-all-start.1 = ((bf16[32,144,256]{2,1,0:T(8,128)(2,1)}), bf16[32,144,256]{2,1,0:T(8,128)(2,1)}, u32[]{:S(2)}, u32[]{:S(2)}) async-start(bf16[32,144,256]{2,1,0:T(8,128)(2,1)} %get-tuple-element.41), calls=%async_computation.1 | async-start | bytes 4718592 | tf_op jit(solution)/shard_map/all_to_all | solution.py:37
  87.5 20.0 %collective-permute-start.1 = (bf16[128,2048]{1,0:T(8,128)(2,1)S(1)}, bf16[128,2048]{1,0:T(8,128)(2,1)S(1)}, u32[]{:S(2)}, u32[]{:S(2)}) collective-permute-start(bf16[128,2048]{1,0:T(8,128)(2,1)S(1)} %copy-done.6), channel_id=1, source_target_pairs={{0,8},{8,0},{1,9},{9,1},{2,10},{10,2},{3,11},{11,3},{4,12},{12,4},... | collective-permute-start | bytes 1572872 | tf_op jit(solution)/shard_map/ppermute | solution.py:41
  118.7 39.7 %all-to-all-start.2 = ((bf16[32,72,256]{2,1,0:T(8,128)(2,1)}), bf16[32,72,256]{2,1,0:T(8,128)(2,1)}, u32[]{:S(2)}, u32[]{:S(2)}) async-start(bf16[32,72,256]{2,1,0:T(8,128)(2,1)} %get-tuple-element.45), calls=%async_computation.2 | async-start | bytes 2359296 | tf_op jit(solution)/shard_map/all_to_all | solution.py:37
  158.4 40.0 %all-to-all-start.3 = ((bf16[32,152,256]{2,1,0:T(8,128)(2,1)}), bf16[32,152,256]{2,1,0:T(8,128)(2,1)}, u32[]{:S(2)}, u32[]{:S(2)}) async-start(bf16[32,152,256]{2,1,0:T(8,128)(2,1)} %shard_map.188), calls=%async_computation.3 | async-start | bytes 4980736 | tf_op jit(solution)/shard_map/all_to_all | solution.py:37
  222.6 32.0 %all-to-all-start.5 = ((bf16[32,72,256]{2,1,0:T(8,128)(2,1)}), bf16[32,72,256]{2,1,0:T(8,128)(2,1)}, u32[]{:S(2)}, u32[]{:S(2)}) async-start(bf16[32,72,256]{2,1,0:T(8,128)(2,1)} %get-tuple-element.51), calls=%async_computation.5 | async-start | bytes 2359296 | tf_op jit(solution)/shard_map/all_to_all | solution.py:37
  229.4 11.9 %collective-permute-start.6 = (f32[64,256]{1,0:T(8,128)}, f32[64,256]{1,0:T(8,128)S(1)}, u32[]{:S(2)}, u32[]{:S(2)}) collective-permute-start(f32[64,256]{1,0:T(8,128)} %shard_map.192.near_note_ref), channel_id=1, source_target_pairs={{0,8},{8,0},{1,9},{9,1},{2,10},{10,2},{3,11},{11,3},{4,12},{12,4},... | collective-permute-start | bytes 196616 | tf_op jit(solution)/shard_map/ppermute | solution.py:41
  241.3 6.0 %copy-start.10 = (f32[8,256]{1,0:T(8,128)S(1)}, f32[8,256]{1,0:T(8,128)}, u32[]{:S(2)}) copy-start(f32[8,256]{1,0:T(8,128)} %get-tuple-element.66) | copy-start | bytes 24580
  241.3 58.1 %collective-permute-start.8 = (bf16[128,2048]{1,0:T(8,128)(2,1)}, bf16[128,2048]{1,0:T(8,128)(2,1)}, u32[]{:S(2)}, u32[]{:S(2)}) collective-permute-start(bf16[128,2048]{1,0:T(8,128)(2,1)} %get-tuple-element.62), channel_id=1, source_target_pairs={{0,200},{8,192},{64,8},{72,0},{128,72},{136,64},{192,136},{200,128... | collective-permute-start | bytes 1572872 | tf_op jit(solution)/shard_map/ppermute | solution.py:50
  245.1 54.3 %collective-permute-start.7 = (bf16[128,2048]{1,0:T(8,128)(2,1)}, bf16[128,2048]{1,0:T(8,128)(2,1)}, u32[]{:S(2)}, u32[]{:S(2)}) collective-permute-start(bf16[128,2048]{1,0:T(8,128)(2,1)} %get-tuple-element.61), channel_id=1, source_target_pairs={{0,192},{8,200},{64,0},{72,8},{128,64},{136,72},{192,128},{200,136... | collective-permute-start | bytes 1572872 | tf_op jit(solution)/shard_map/ppermute | solution.py:50
  247.3 38.6 %collective-permute-start.9 = (f32[8,256]{1,0:T(8,128)S(1)}, f32[8,256]{1,0:T(8,128)S(1)}, u32[]{:S(2)}, u32[]{:S(2)}) collective-permute-start(f32[8,256]{1,0:T(8,128)S(1)} %copy-done.10), channel_id=1, source_target_pairs={{0,8},{8,0},{1,9},{9,1},{2,10},{10,2},{3,11},{11,3},{4,12},{12,4},... | collective-permute-start | bytes 24584 | tf_op jit(solution)/shard_map/ppermute | solution.py:41
  254.6 58.9 %collective-permute-start.5 = (bf16[128,2048]{1,0:T(8,128)(2,1)}, bf16[128,2048]{1,0:T(8,128)(2,1)}, u32[]{:S(2)}, u32[]{:S(2)}) collective-permute-start(bf16[128,2048]{1,0:T(8,128)(2,1)} %shard_map.191), channel_id=1, source_target_pairs={{0,72},{8,64},{64,136},{72,128},{128,200},{136,192},{192,8},{200,0... | collective-permute-start | bytes 1572872 | tf_op jit(solution)/shard_map/ppermute | solution.py:50
  257.7 55.8 %collective-permute-start.4 = (bf16[128,2048]{1,0:T(8,128)(2,1)}, bf16[128,2048]{1,0:T(8,128)(2,1)}, u32[]{:S(2)}, u32[]{:S(2)}) collective-permute-start(bf16[128,2048]{1,0:T(8,128)(2,1)} %shard_map.190), channel_id=1, source_target_pairs={{0,64},{8,72},{64,128},{72,136},{128,192},{136,200},{192,0},{200,8... | collective-permute-start | bytes 1572872 | tf_op jit(solution)/shard_map/ppermute | solution.py:50
  289.8 21.3 %all-to-all-start.6 = ((f32[32,32,128]{2,1,0:T(8,128)}), f32[32,32,128]{2,1,0:T(8,128)S(1)}, u32[]{:S(2)}, u32[]{:S(2)}) async-start(f32[32,32,128]{2,1,0:T(8,128)} %bitcast.27), calls=%async_computation.6 | async-start | bytes 1048576 | tf_op jit(solution)/shard_map/all_to_all | solution.py:37
  (4 other events, 2.8 us)

commit v2 on v1

--- a/solution.py
+++ b/solution.py
@@ -629,11 +629,11 @@
         cols = pl.ds(pl.multiple_of(x * 512 + zh * 256, 256), 256)
         part = dot(near_logit, near_normed_ref[:, cols]) + dot(far_logit, far_normed_ref[:, cols])
         both = jnp.concatenate([part, jnp.where(row == 0, gains, 0.0)], axis=0)
-        shares_ref[pl.ds(x * 256, 256), :] = both.T
+        shares_ref[pl.ds(x * 256, 256), :] = both.T.astype(bf16)
 
 
 def run_share_parts(*args):
-    return call(share_parts, (shape((D // 2, 128), f32),), [SMEM] + [VMEM] * 9, [], args, 10**9, 3)[0]
+    return call(share_parts, (shape((D // 2, 128)),), [SMEM] + [VMEM] * 9, [], args, 10**9, 3)[0]
 
 
 def ahead_sums(home_ref, mix_ref, wide_ref):
@@ -663,9 +663,9 @@
 
 
 def share_sums(got_ref, router_ref, gain_ref):
-    total = got_ref[0]
+    total = got_ref[0].astype(f32)
     for source in range(1, PEERS):
-        total = total + got_ref[source]
+        total = total + got_ref[source].astype(f32)
     total = total * factor
     router_ref[...] = total[:, :EXPERTS]
     gain_ref[...] = total.T[EXPERTS : EXPERTS + 1, :]

time: 317 us -> 314 us (level)
  no operation moved by 1% of the time
where the time goes in v2:
time: 314 us; the launch traced here: 313 us
  starting transfers between devices  96.3 us (31%)
  waiting for transfers between devices  95.2 us (30%)
  Pallas kernels  86.5 us (28%)
  blocking collectives  24.2 us (8%)
  local copies, waits for them, and re-layouts  4.94 us (2%)
  other arithmetic  4.09 us (1%)
    pallas_call x13, Pallas kernels, call(): pl.pallas_call(kernel, out_shape=outs, in_specs=ins, out_specs=tuple((VME...  84.3 us
    ppermute x6, waiting for transfers between devices, swapped(): return lax.ppermute(x, 'zh', [(0, 1), (1, 0)])  65.8 us
    all_to_all x6, starting transfers between devices, spread_out(): return lax.all_to_all(x, XY, 0, 0, tiled=True)  65 us
    all_to_all x6, waiting for transfers between devices, spread_out(): return lax.all_to_all(x, XY, 0, 0, tiled=True)  29.5 us
    ppermute x6, starting transfers between devices, swapped(): return lax.ppermute(x, 'zh', [(0, 1), (1, 0)])  29.2 us
    all_to_all x1, blocking collectives, spread_out(): return lax.all_to_all(x, XY, 0, 0, tiled=True)  24.2 us
  transfers between devices with their start and end apart: 16, of which 7 were waited for; matrix products, arithmetic and copies ran while one was open for 1% of the time, Pallas kernels for 24%

profile of v2, /device:TPU:1, one launch (start us, length us, event | category | flops | bytes accessed | tf_op | source)
XLA Modules:
  0.0 312.7 jit_solution(3419818788096958232)
XLA Ops:
  4.9 6.6 %shard_map.184 = (bf16[32,216,256]{2,1,0:T(8,128)(2,1)}, bf16[128,2048]{1,0:T(8,128)(2,1)}, bf16[288,128]{1,0:T(8,128)(2,1)}, f32[64,128]{1,0:T(8,128)}, bf16[288,128]{1,0:T(8,128)(2,1)}) custom-call(s32[1]{0:T(128)} %bitcast.zh_ref, s32[4,128]{1,0:T(4,128)} %bitcast.33, s32[4,128]{1,0:T(4,128)} %bitcast.35, bf16[128,2048]{1,0:T(8,128)(2,1)} %bitcast.27, ...), custom_call_target="tpu_custom_call" | custom-call | flops 2000000000 | bytes 8388608 | tf_op jit(solution)/shard_map/pallas_call | solution.py:58
  11.6 8.8 %all-to-all-start = ((bf16[32,216,256]{2,1,0:T(8,128)(2,1)}), bf16[32,216,256]{2,1,0:T(8,128)(2,1)}, u32[]{:S(2)}, u32[]{:S(2)}) async-start(bf16[32,216,256]{2,1,0:T(8,128)(2,1)} %get-tuple-element.38), calls=%async_computation | async-start | bytes 7077888 | tf_op jit(solution)/shard_map/all_to_all | solution.py:37
  20.4 7.0 %collective-permute-start.2 = (bf16[128,2048]{1,0:T(8,128)(2,1)S(1)}, bf16[128,2048]{1,0:T(8,128)(2,1)S(1)}, u32[]{:S(2)}, u32[]{:S(2)}) collective-permute-start(bf16[128,2048]{1,0:T(8,128)(2,1)S(1)} %bitcast.31), channel_id=1, source_target_pairs={{0,8},{8,0},{1,9},{9,1},{2,10},{10,2},{3,11},{11,3},{4,12},{12,4},... | collective-permute-start | bytes 1572872 | tf_op jit(solution)/shard_map/ppermute | solution.py:41
  27.5 5.4 %collective-permute-start = (s32[8,128]{1,0:T(8,128)S(1)}, s32[8,128]{1,0:T(8,128)S(1)}, u32[]{:S(2)}, u32[]{:S(2)}) collective-permute-start(s32[8,128]{1,0:T(8,128)S(1)} %pad_add_fusion), channel_id=1, source_target_pairs={{0,8},{8,0},{1,9},{9,1},{2,10},{10,2},{3,11},{11,3},{4,12},{12,4},... | collective-permute-start | bytes 12296 | tf_op jit(solution)/shard_map/ppermute | solution.py:41
  32.8 23.8 %collective-permute-done = s32[8,128]{1,0:T(8,128)S(1)} collective-permute-done((s32[8,128]{1,0:T(8,128)S(1)}, s32[8,128]{1,0:T(8,128)S(1)}, u32[]{:S(2)}, u32[]{:S(2)}) %collective-permute-start) | collective-permute-done | bytes 4128 | tf_op jit(solution)/shard_map/ppermute | solution.py:41
  58.8 5.2 %shard_map.186 = (bf16[32,144,256]{2,1,0:T(8,128)(2,1)}, bf16[128,2048]{1,0:T(8,128)(2,1)}, bf16[288,128]{1,0:T(8,128)(2,1)}, f32[64,128]{1,0:T(8,128)}) custom-call(s32[1]{0:T(128)} %bitcast.zh_ref, s32[4,128]{1,0:T(4,128)} %get-tuple-element.72.ids_ref, bf16[128,2048]{1,0:T(8,128)(2,1)} %copy-done.2, bf16[128,2048]{1,0:T(8,128)(2,1)} %copy-done.7, ...), custom_call_target="tpu_custom_call" | custom-call | flops 1000000000 | bytes 6291456 | tf_op jit(solution)/shard_map/pallas_call | solution.py:58
  64.3 23.2 %all-to-all-start.1 = ((bf16[32,144,256]{2,1,0:T(8,128)(2,1)}), bf16[32,144,256]{2,1,0:T(8,128)(2,1)}, u32[]{:S(2)}, u32[]{:S(2)}) async-start(bf16[32,144,256]{2,1,0:T(8,128)(2,1)} %get-tuple-element.41), calls=%async_computation.1 | async-start | bytes 4718592 | tf_op jit(solution)/shard_map/all_to_all | solution.py:37
  87.5 6.2 %collective-permute-start.1 = (bf16[128,2048]{1,0:T(8,128)(2,1)S(1)}, bf16[128,2048]{1,0:T(8,128)(2,1)S(1)}, u32[]{:S(2)}, u32[]{:S(2)}) collective-permute-start(bf16[128,2048]{1,0:T(8,128)(2,1)S(1)} %copy-done.6), channel_id=1, source_target_pairs={{0,8},{8,0},{1,9},{9,1},{2,10},{10,2},{3,11},{11,3},{4,12},{12,4},... | collective-permute-start | bytes 1572872 | tf_op jit(solution)/shard_map/ppermute | solution.py:41
  93.7 13.8 %collective-permute-done.1.x_ref = bf16[128,2048]{1,0:T(8,128)(2,1)S(1)} collective-permute-done((bf16[128,2048]{1,0:T(8,128)(2,1)S(1)}, bf16[128,2048]{1,0:T(8,128)(2,1)S(1)}, u32[]{:S(2)}, u32[]{:S(2)}) %collective-permute-start.1) | collective-permute-done | bytes 524320 | tf_op jit(solution)/shard_map/ppermute | solution.py:41
  108.3 5.0 %shard_map.185 = (bf16[32,72,256]{2,1,0:T(8,128)(2,1)}, bf16[288,128]{1,0:T(8,128)(2,1)}) custom-call(s32[1]{0:T(128)} %bitcast.zh_ref, s32[4,128]{1,0:T(4,128)} %get-tuple-element.73.ids_ref, bf16[128,2048]{1,0:T(8,128)(2,1)} %copy-done.8, f32[1,2048]{1,0:T(1,128)} %gain_ref.9, bf16[64,2048]{1,0:T(8,128)(2,1)} %bitcast.53), custom_call_target="tpu_custom_call" | custom-call | flops 1000000000 | bytes 4194304 | tf_op jit(solution)/shard_map/pallas_call | solution.py:58
  113.3 5.4 %all-to-all-done.1.got_ref = bf16[32,144,256]{2,1,0:T(8,128)(2,1)} async-done(((bf16[32,144,256]{2,1,0:T(8,128)(2,1)}), bf16[32,144,256]{2,1,0:T(8,128)(2,1)}, u32[]{:S(2)}, u32[]{:S(2)}) %all-to-all-start.1) | async-done | bytes 2359328 | tf_op jit(solution)/shard_map/all_to_all | solution.py:37
  118.7 11.3 %all-to-all-start.2 = ((bf16[32,72,256]{2,1,0:T(8,128)(2,1)}), bf16[32,72,256]{2,1,0:T(8,128)(2,1)}, u32[]{:S(2)}, u32[]{:S(2)}) async-start(bf16[32,72,256]{2,1,0:T(8,128)(2,1)} %get-tuple-element.45), calls=%async_computation.2 | async-start | bytes 2359296 | tf_op jit(solution)/shard_map/all_to_all | solution.py:37
  130.0 15.7 %shard_map.187 = (bf16[32,72,256]{2,1,0:T(8,128)(2,1)}, f32[256,128]{1,0:T(8,128)}) custom-call(bf16[32,216,256]{2,1,0:T(8,128)(2,1)} %all-to-all-done.got_ref.near_ref, bf16[2048,768]{1,0:T(8,128)(2,1)} %bitcast.37, bf16[2048,768]{1,0:T(8,128)(2,1)} %bitcast.40, bf16[768,2048]{1,0:T(8,128)(2,1)} %bitcast.43), custom_call_target="tpu_custom_call" | custom-call | flops 5000000000 | bytes 13631488 | tf_op jit(solution)/shard_map/pallas_call | solution.py:58
  145.6 12.7 %shard_map.188 = bf16[32,152,256]{2,1,0:T(8,128)(2,1)} custom-call(bf16[32,144,256]{2,1,0:T(8,128)(2,1)} %all-to-all-done.1.got_ref, bf16[32,72,256]{2,1,0:T(8,128)(2,1)} %get-tuple-element.43.near_ref, f32[256,128]{1,0:T(8,128)} %get-tuple-element.44.near_small_ref, bf16[2048,768]{1,0:T(8,128)(2,1)} %bitcast.38, bf16[2048,768]{1,0:T(8,128)(2,1)} %bitcast.41, ...), custom_call_target="tpu_custom_call" | custom-call | flops 5000000000 | bytes 15728640 | tf_op jit(solution)/shard_map/pallas_call | solution.py:58
  158.4 7.4 %all-to-all-start.3 = ((bf16[32,152,256]{2,1,0:T(8,128)(2,1)}), bf16[32,152,256]{2,1,0:T(8,128)(2,1)}, u32[]{:S(2)}, u32[]{:S(2)}) async-start(bf16[32,152,256]{2,1,0:T(8,128)(2,1)} %shard_map.188), calls=%async_computation.3 | async-start | bytes 4980736 | tf_op jit(solution)/shard_map/all_to_all | solution.py:37
  165.8 15.8 %shard_map.189 = (bf16[32,72,256]{2,1,0:T(8,128)(2,1)}, bf16[32,72,256]{2,1,0:T(8,128)(2,1)}) custom-call(bf16[32,216,256]{2,1,0:T(8,128)(2,1)} %all-to-all-done.got_ref.near_ref, bf16[32,72,256]{2,1,0:T(8,128)(2,1)} %all-to-all-done.2.far_ref, bf16[2048,768]{1,0:T(8,128)(2,1)} %bitcast.39, bf16[2048,768]{1,0:T(8,128)(2,1)} %bitcast.42, ...), custom_call_target="tpu_custom_call" | custom-call | flops 6000000000 | bytes 14680064 | tf_op jit(solution)/shard_map/pallas_call | solution.py:58
  181.7 16.8 %all-to-all-done.3.home_ref = bf16[32,152,256]{2,1,0:T(8,128)(2,1)} async-done(((bf16[32,152,256]{2,1,0:T(8,128)(2,1)}), bf16[32,152,256]{2,1,0:T(8,128)(2,1)}, u32[]{:S(2)}, u32[]{:S(2)}) %all-to-all-start.3) | async-done | bytes 2490400 | tf_op jit(solution)/shard_map/all_to_all | solution.py:37
  198.4 24.2 %all_to_all.35.home_ref = bf16[32,72,256]{2,1,0:T(8,128)(2,1)} all-to-all(bf16[32,72,256]{2,1,0:T(8,128)(2,1)} %get-tuple-element.50), channel_id=1, replica_groups=mesh['pipe'=4,'x'=4,'zh'=2,'y'=4,'core'=2] {'x','y','core'}, dimensions={0} | all-to-all | bytes 2359296 | tf_op jit(solution)/shard_map/all_to_all | solution.py:37
  222.6 4.7 %all-to-all-start.5 = ((bf16[32,72,256]{2,1,0:T(8,128)(2,1)}), bf16[32,72,256]{2,1,0:T(8,128)(2,1)}, u32[]{:S(2)}, u32[]{:S(2)}) async-start(bf16[32,72,256]{2,1,0:T(8,128)(2,1)} %get-tuple-element.51), calls=%async_computation.5 | async-start | bytes 2359296 | tf_op jit(solution)/shard_map/all_to_all | solution.py:37
  229.4 6.1 %collective-permute-start.6 = (f32[64,256]{1,0:T(8,128)}, f32[64,256]{1,0:T(8,128)S(1)}, u32[]{:S(2)}, u32[]{:S(2)}) collective-permute-start(f32[64,256]{1,0:T(8,128)} %shard_map.192.near_note_ref), channel_id=1, source_target_pairs={{0,8},{8,0},{1,9},{9,1},{2,10},{10,2},{3,11},{11,3},{4,12},{12,4},... | collective-permute-start | bytes 196616 | tf_op jit(solution)/shard_map/ppermute | solution.py:41
  235.6 5.7 %shard_map.193 = (f32[128,2048]{1,0:T(8,128)}, bf16[128,2048]{1,0:T(8,128)(2,1)}, f32[8,256]{1,0:T(8,128)}, f32[8,256]{1,0:T(8,128)}) custom-call(s32[1]{0:T(128)} %bitcast.zh_ref, bf16[32,152,256]{2,1,0:T(8,128)(2,1)} %all-to-all-done.3.home_ref, bf16[288,128]{1,0:T(8,128)(2,1)} %get-tuple-element.56.near_hot_ref, ...), custom_call_target="tpu_custom_call" | custom-call | flops 1000000000 | bytes 6291456 | tf_op jit(solution)/shard_map/pallas_call | solution.py:58
  257.7 28.2 %collective-permute-done.9.theirs_ref = f32[8,256]{1,0:T(8,128)S(1)} collective-permute-done((f32[8,256]{1,0:T(8,128)S(1)}, f32[8,256]{1,0:T(8,128)S(1)}, u32[]{:S(2)}, u32[]{:S(2)}) %collective-permute-start.9) | collective-permute-done | bytes 8224 | tf_op jit(solution)/shard_map/ppermute | solution.py:41
  289.6 9.7 %all-to-all-start.6 = ((bf16[32,32,128]{2,1,0:T(8,128)(2,1)}), bf16[32,32,128]{2,1,0:T(8,128)(2,1)S(1)}, u32[]{:S(2)}, u32[]{:S(2)}) async-start(bf16[32,32,128]{2,1,0:T(8,128)(2,1)} %bitcast.32), calls=%async_computation.6 | async-start | bytes 524288 | tf_op jit(solution)/shard_map/all_to_all | solution.py:37
  301.3 7.0 %all-to-all-done.6.got_ref = bf16[32,32,128]{2,1,0:T(8,128)(2,1)S(1)} async-done(((bf16[32,32,128]{2,1,0:T(8,128)(2,1)}), bf16[32,32,128]{2,1,0:T(8,128)(2,1)S(1)}, u32[]{:S(2)}, u32[]{:S(2)}) %all-to-all-start.6) | async-done | bytes 262176 | tf_op jit(solution)/shard_map/all_to_all | solution.py:37
  (51 shorter events, 35.7 us)
Async XLA Ops:
  11.5 8.8 %copy-start.1 = (bf16[1,128,2048]{2,1,0:T(8,128)(2,1)S(1)}, bf16[1,128,2048]{2,1,0:T(8,128)(2,1)}, u32[]{:S(2)}) copy-start(bf16[1,128,2048]{2,1,0:T(8,128)(2,1)} %param.29) | copy-start | bytes 1572868
  11.5 15.8 %copy-start.5 = (bf16[1,128,2048]{2,1,0:T(8,128)(2,1)S(1)}, bf16[1,128,2048]{2,1,0:T(8,128)(2,1)}, u32[]{:S(2)}) copy-start(bf16[1,128,2048]{2,1,0:T(8,128)(2,1)} %param.31) | copy-start | bytes 1572868
  11.5 15.9 %copy-start.3 = (s32[1,128,4]{1,2,0:T(4,128)S(1)}, s32[1,128,4]{1,2,0:T(4,128)}, u32[]{:S(2)}) copy-start(s32[1,128,4]{1,2,0:T(4,128)} %param.30) | copy-start | bytes 6148
  11.6 15.9 %copy-start.4 = (s32[1,128,4]{1,2,0:T(4,128)S(1)}, s32[1,128,4]{1,2,0:T(4,128)}, u32[]{:S(2)}) copy-start(s32[1,128,4]{1,2,0:T(4,128)} %param.28) | copy-start | bytes 6148
  11.6 52.7 %all-to-all-start = ((bf16[32,216,256]{2,1,0:T(8,128)(2,1)}), bf16[32,216,256]{2,1,0:T(8,128)(2,1)}, u32[]{:S(2)}, u32[]{:S(2)}) async-start(bf16[32,216,256]{2,1,0:T(8,128)(2,1)} %get-tuple-element.38), calls=%async_computation | async-start | bytes 7077888 | tf_op jit(solution)/shard_map/all_to_all | solution.py:37
  20.4 36.9 %collective-permute-start.2 = (bf16[128,2048]{1,0:T(8,128)(2,1)S(1)}, bf16[128,2048]{1,0:T(8,128)(2,1)S(1)}, u32[]{:S(2)}, u32[]{:S(2)}) collective-permute-start(bf16[128,2048]{1,0:T(8,128)(2,1)S(1)} %bitcast.31), channel_id=1, source_target_pairs={{0,8},{8,0},{1,9},{9,1},{2,10},{10,2},{3,11},{11,3},{4,12},{12,4},... | collective-permute-start | bytes 1572872 | tf_op jit(solution)/shard_map/ppermute | solution.py:41
  27.4 30.7 %collective-permute-start.3 = (bf16[128,2048]{1,0:T(8,128)(2,1)S(1)}, bf16[128,2048]{1,0:T(8,128)(2,1)S(1)}, u32[]{:S(2)}, u32[]{:S(2)}) collective-permute-start(bf16[128,2048]{1,0:T(8,128)(2,1)S(1)} %bitcast.50), channel_id=1, source_target_pairs={{0,8},{8,0},{1,9},{9,1},{2,10},{10,2},{3,11},{11,3},{4,12},{12,4},... | collective-permute-start | bytes 1572872 | tf_op jit(solution)/shard_map/ppermute | solution.py:41
  27.5 29.2 %collective-permute-start = (s32[8,128]{1,0:T(8,128)S(1)}, s32[8,128]{1,0:T(8,128)S(1)}, u32[]{:S(2)}, u32[]{:S(2)}) collective-permute-start(s32[8,128]{1,0:T(8,128)S(1)} %pad_add_fusion), channel_id=1, source_target_pairs={{0,8},{8,0},{1,9},{9,1},{2,10},{10,2},{3,11},{11,3},{4,12},{12,4},... | collective-permute-start | bytes 12296 | tf_op jit(solution)/shard_map/ppermute | solution.py:41
  57.2 0.8 copy-start.2
  58.0 0.8 copy-start.7
  64.3 23.2 %copy-start.6 = (bf16[128,2048]{1,0:T(8,128)(2,1)S(1)}, bf16[128,2048]{1,0:T(8,128)(2,1)}, u32[]{:S(2)}) copy-start(bf16[128,2048]{1,0:T(8,128)(2,1)} %shard_map.183.resid_ref) | copy-start | bytes 1572868
  64.3 54.4 %all-to-all-start.1 = ((bf16[32,144,256]{2,1,0:T(8,128)(2,1)}), bf16[32,144,256]{2,1,0:T(8,128)(2,1)}, u32[]{:S(2)}, u32[]{:S(2)}) async-start(bf16[32,144,256]{2,1,0:T(8,128)(2,1)} %get-tuple-element.41), calls=%async_computation.1 | async-start | bytes 4718592 | tf_op jit(solution)/shard_map/all_to_all | solution.py:37
  87.5 20.0 %collective-permute-start.1 = (bf16[128,2048]{1,0:T(8,128)(2,1)S(1)}, bf16[128,2048]{1,0:T(8,128)(2,1)S(1)}, u32[]{:S(2)}, u32[]{:S(2)}) collective-permute-start(bf16[128,2048]{1,0:T(8,128)(2,1)S(1)} %copy-done.6), channel_id=1, source_target_pairs={{0,8},{8,0},{1,9},{9,1},{2,10},{10,2},{3,11},{11,3},{4,12},{12,4},... | collective-permute-start | bytes 1572872 | tf_op jit(solution)/shard_map/ppermute | solution.py:41
  118.7 39.7 %all-to-all-start.2 = ((bf16[32,72,256]{2,1,0:T(8,128)(2,1)}), bf16[32,72,256]{2,1,0:T(8,128)(2,1)}, u32[]{:S(2)}, u32[]{:S(2)}) async-start(bf16[32,72,256]{2,1,0:T(8,128)(2,1)} %get-tuple-element.45), calls=%async_computation.2 | async-start | bytes 2359296 | tf_op jit(solution)/shard_map/all_to_all | solution.py:37
  158.4 40.0 %all-to-all-start.3 = ((bf16[32,152,256]{2,1,0:T(8,128)(2,1)}), bf16[32,152,256]{2,1,0:T(8,128)(2,1)}, u32[]{:S(2)}, u32[]{:S(2)}) async-start(bf16[32,152,256]{2,1,0:T(8,128)(2,1)} %shard_map.188), calls=%async_computation.3 | async-start | bytes 4980736 | tf_op jit(solution)/shard_map/all_to_all | solution.py:37
  222.6 32.0 %all-to-all-start.5 = ((bf16[32,72,256]{2,1,0:T(8,128)(2,1)}), bf16[32,72,256]{2,1,0:T(8,128)(2,1)}, u32[]{:S(2)}, u32[]{:S(2)}) async-start(bf16[32,72,256]{2,1,0:T(8,128)(2,1)} %get-tuple-element.51), calls=%async_computation.5 | async-start | bytes 2359296 | tf_op jit(solution)/shard_map/all_to_all | solution.py:37
  229.4 11.9 %collective-permute-start.6 = (f32[64,256]{1,0:T(8,128)}, f32[64,256]{1,0:T(8,128)S(1)}, u32[]{:S(2)}, u32[]{:S(2)}) collective-permute-start(f32[64,256]{1,0:T(8,128)} %shard_map.192.near_note_ref), channel_id=1, source_target_pairs={{0,8},{8,0},{1,9},{9,1},{2,10},{10,2},{3,11},{11,3},{4,12},{12,4},... | collective-permute-start | bytes 196616 | tf_op jit(solution)/shard_map/ppermute | solution.py:41
  241.3 6.0 %copy-start.10 = (f32[8,256]{1,0:T(8,128)S(1)}, f32[8,256]{1,0:T(8,128)}, u32[]{:S(2)}) copy-start(f32[8,256]{1,0:T(8,128)} %get-tuple-element.66) | copy-start | bytes 24580
  241.3 58.0 %collective-permute-start.8 = (bf16[128,2048]{1,0:T(8,128)(2,1)}, bf16[128,2048]{1,0:T(8,128)(2,1)S(1)}, u32[]{:S(2)}, u32[]{:S(2)}) collective-permute-start(bf16[128,2048]{1,0:T(8,128)(2,1)} %get-tuple-element.62), channel_id=1, source_target_pairs={{0,200},{8,192},{64,8},{72,0},{128,72},{136,64},{192,136},{200,128... | collective-permute-start | bytes 1572872 | tf_op jit(solution)/shard_map/ppermute | solution.py:50
  245.1 54.2 %collective-permute-start.7 = (bf16[128,2048]{1,0:T(8,128)(2,1)}, bf16[128,2048]{1,0:T(8,128)(2,1)}, u32[]{:S(2)}, u32[]{:S(2)}) collective-permute-start(bf16[128,2048]{1,0:T(8,128)(2,1)} %get-tuple-element.61), channel_id=1, source_target_pairs={{0,192},{8,200},{64,0},{72,8},{128,64},{136,72},{192,128},{200,136... | collective-permute-start | bytes 1572872 | tf_op jit(solution)/shard_map/ppermute | solution.py:50
  247.3 38.6 %collective-permute-start.9 = (f32[8,256]{1,0:T(8,128)S(1)}, f32[8,256]{1,0:T(8,128)S(1)}, u32[]{:S(2)}, u32[]{:S(2)}) collective-permute-start(f32[8,256]{1,0:T(8,128)S(1)} %copy-done.10), channel_id=1, source_target_pairs={{0,8},{8,0},{1,9},{9,1},{2,10},{10,2},{3,11},{11,3},{4,12},{12,4},... | collective-permute-start | bytes 24584 | tf_op jit(solution)/shard_map/ppermute | solution.py:41
  254.6 56.0 %collective-permute-start.5 = (bf16[128,2048]{1,0:T(8,128)(2,1)}, bf16[128,2048]{1,0:T(8,128)(2,1)}, u32[]{:S(2)}, u32[]{:S(2)}) collective-permute-start(bf16[128,2048]{1,0:T(8,128)(2,1)} %shard_map.191), channel_id=1, source_target_pairs={{0,72},{8,64},{64,136},{72,128},{128,200},{136,192},{192,8},{200,0... | collective-permute-start | bytes 1572872 | tf_op jit(solution)/shard_map/ppermute | solution.py:50
  257.7 52.8 %collective-permute-start.4 = (bf16[128,2048]{1,0:T(8,128)(2,1)}, bf16[128,2048]{1,0:T(8,128)(2,1)}, u32[]{:S(2)}, u32[]{:S(2)}) collective-permute-start(bf16[128,2048]{1,0:T(8,128)(2,1)} %shard_map.190), channel_id=1, source_target_pairs={{0,64},{8,72},{64,128},{72,136},{128,192},{136,200},{192,0},{200,8... | collective-permute-start | bytes 1572872 | tf_op jit(solution)/shard_map/ppermute | solution.py:50
  289.6 18.6 %all-to-all-start.6 = ((bf16[32,32,128]{2,1,0:T(8,128)(2,1)}), bf16[32,32,128]{2,1,0:T(8,128)(2,1)S(1)}, u32[]{:S(2)}, u32[]{:S(2)}) async-start(bf16[32,32,128]{2,1,0:T(8,128)(2,1)} %bitcast.32), calls=%async_computation.6 | async-start | bytes 524288 | tf_op jit(solution)/shard_map/all_to_all | solution.py:37
  (4 other events, 2.7 us)

commit v3 on v2

--- a/solution.py
+++ b/solution.py
@@ -198,7 +198,7 @@
     zh_ref, ids_ref, ahead_ids_ref, x_ref, g_ref, resid_ref, gain_ref, table_ref,
     sent_ref, normed_ref, onehot_ref, probs_ref, mix_ref, wide_ref, rows_ref
 ):
-    zh, gain, table = zh_ref[0], gain_ref[...], table_ref[...]
+    zh, gain, table = (zh_ref[0] & 1), gain_ref[...], table_ref[...]
     normed_ref[...], probs_ref[...], _, onehot_ref[...] = routed(ids_ref[...], x_ref[...], zh, gain, table)
     fill(wide_ref, 0, onehot_ref[...], normed_ref)
     fill(wide_ref, 1, onehot_ref[...], g_ref)
@@ -230,7 +230,7 @@
     zh_ref, ids_ref, x_ref, g_ref, gain_ref, table_ref, sent_ref, normed_ref, onehot_ref, probs_ref, wide_ref
 ):
     normed_ref[...], probs_ref[...], _, onehot_ref[...] = routed(
-        ids_ref[...], x_ref[...], zh_ref[0], gain_ref[...], table_ref[...]
+        ids_ref[...], x_ref[...], (zh_ref[0] & 1), gain_ref[...], table_ref[...]
     )
     fill(wide_ref, 0, onehot_ref[...], normed_ref)
     fill(wide_ref, 1, onehot_ref[...], g_ref)
@@ -250,7 +250,7 @@
 
 
 def ahead_pack(zh_ref, ids_ref, x_ref, gain_ref, table_ref, sent_ref, mix_ref, wide_ref, rows_ref, onehot_ref):
-    rows_ref[...], probs, pick, onehot = routed(ids_ref[...], x_ref[...], zh_ref[0], gain_ref[...], table_ref[...])
+    rows_ref[...], probs, pick, onehot = routed(ids_ref[...], x_ref[...], (zh_ref[0] & 1), gain_ref[...], table_ref[...])
     mix_ref[...] = mixed_by(onehot, pick, probs)
     onehot_ref[...] = onehot
     fill_looped(wide_ref, 0, onehot_ref, rows_ref)
@@ -365,7 +365,7 @@
 
 
 def far_experts(
-    got_ref, near_ref, near_small_ref, gate_hbm, up_hbm, down_hbm, back_ref, wide_ref, gate_ref, up_ref, down_ref, sems,
+    got_ref, near_small_ref, gate_hbm, up_hbm, down_hbm, back_ref, wide_ref, gate_ref, up_ref, down_ref, sems,
     gate_grad, up_grad
 ):
     weights = ((gate_hbm, gate_ref), (up_hbm, up_ref), (down_hbm, down_ref))
@@ -374,11 +374,10 @@
 
     def put(d, rows):
         for lane in range(2):
-            back_ref[d, pl.ds(0, ROWS), LANES[lane]] = near_ref[d, :, LANES[lane]]
-            back_ref[d, pl.ds(ROWS, ROWS), LANES[lane]] = wide_ref[lane, rows, :].astype(bf16)
+            back_ref[d, pl.ds(0, ROWS), LANES[lane]] = wide_ref[lane, rows, :].astype(bf16)
         extra = wide_ref[0, pl.ds(pl.multiple_of(AREA + d * 8, 8), 8), :].astype(bf16)
-        back_ref[d, pl.ds(2 * ROWS, 8), LANES[0]] = extra
-        back_ref[d, pl.ds(2 * ROWS, 8), LANES[1]] = extra
+        back_ref[d, pl.ds(ROWS, 8), LANES[0]] = extra
+        back_ref[d, pl.ds(ROWS, 8), LANES[1]] = extra
 
     each_peer(put)
 
@@ -407,8 +406,8 @@
 def run_far_experts(*args):
     return call(
         far_experts,
-        (shape((PEERS, 2 * ROWS + 8, 256)),),
-        [VMEM] * 3 + [HBM] * 3,
+        (shape((PEERS, ROWS + 8, 256)),),
+        [VMEM] * 2 + [HBM] * 3,
         [pltpu.VMEM((2, 2 * AREA, 128), f32)] + WEIGHTS + GRADS,
         args,
         5 * 10**9,
@@ -417,7 +416,7 @@
 
 
 def ahead_experts(
-    near_ref, far_ref, gate_hbm, up_hbm, down_hbm, first_ref, second_ref, wide_ref, gate_ref, up_ref, down_ref, sems,
+    near_ref, far_ref, gate_hbm, up_hbm, down_hbm, made_ref, wide_ref, gate_ref, up_ref, down_ref, sems,
     gate_sum, up_sum, hidden_ref
 ):
     copies = fetched(((gate_hbm, gate_ref), (up_hbm, up_ref), (down_hbm, down_ref)), sems)
@@ -451,8 +450,8 @@
 
     def put(d, rows):
         for lane in range(2):
-            first_ref[d, :, LANES[lane]] = wide_ref[lane, area_rows(d, 1), :].astype(bf16)
-            second_ref[d, :, LANES[lane]] = wide_ref[lane, area_rows(d, 0), :].astype(bf16)
+            for half in range(2):
+                made_ref[d, pl.ds(half * ROWS, ROWS), LANES[lane]] = wide_ref[lane, area_rows(d, half), :].astype(bf16)
 
     each_peer(put)
 
@@ -460,7 +459,7 @@
 def run_ahead_experts(*args):
     return call(
         ahead_experts,
-        (shape((PEERS, ROWS, 256)), shape((PEERS, ROWS, 256))),
+        (shape((PEERS, 2 * ROWS, 256)),),
         [VMEM] * 2 + [HBM] * 3,
         [pltpu.VMEM((2, 2 * AREA, 128), f32)]
         + WEIGHTS
@@ -468,7 +467,7 @@
         args,
         6 * 10**9,
         14,
-    )
+    )[0]
 
 
 def attend(length_ref, x_ref, q_ref, kc_ref, kn_ref, vc_ref, vn_ref, resid_ref):
@@ -507,7 +506,7 @@
 
 
 def behind_note(zh_ref, home_ref, near_hot_ref, far_hot_ref, note_ref):
-    pick = picks(iota((SLOTS, EXPERTS), 0) // MOST, zh_ref[0]).astype(f32)
+    pick = picks(iota((SLOTS, EXPERTS), 0) // MOST, (zh_ref[0] & 1)).astype(f32)
     small = jnp.concatenate([home_ref[d].astype(f32) for d in range(PEERS)], axis=0)[:, :128].astype(bf16)
     share = marks(iota((SLOTS, PEERS * 8), 0) // MOST * 8 == iota((SLOTS, PEERS * 8), 1))
     small = dot(share, small)
@@ -522,7 +521,7 @@
 
 
 def run_behind_note(zh, home, near_hot, far_hot):
-    tail = pl.BlockSpec((PEERS, 8, 256), lambda i: (0, 2 * ROWS // 8, 0))
+    tail = pl.BlockSpec((PEERS, 8, 256), lambda i: (0, ROWS // 8, 0))
     return pl.pallas_call(
         behind_note,
         grid=(1,),
@@ -534,32 +533,51 @@
     )(zh, home, near_hot, far_hot)
 
 
-def behind_sums(
-    zh_ref, home_ref, near_hot_ref, far_hot_ref, near_probs_ref, far_probs_ref, near_x_ref, far_x_ref, gain_ref,
-    sums_ref, sent_ref, theirs_ref, mine_ref, wide_ref, line_ref, mix_ref
-):
-    zh = zh_ref[0]
-
+def block_sums(home_ref, mix_ref, wide_ref):
     def take(d, rows):
-        for half in range(2):
-            for lane in range(2):
-                wide_ref[lane, area_rows(d, half), :] = home_ref[d, pl.ds(half * ROWS, ROWS), LANES[lane]].astype(f32)
+        for lane in range(2):
+            wide_ref[lane, rows, :] = home_ref[d, pl.ds(0, ROWS), LANES[lane]].astype(f32)
 
     each_peer(take)
-    pick = picks(iota((SLOTS, EXPERTS), 0) // MOST, zh)
-    mix_ref[0] = mixed_by(near_hot_ref[...], pick, near_probs_ref[...])
-    mix_ref[1] = mixed_by(far_hot_ref[...], pick, far_probs_ref[...])
-
     for j in range(8):
-        cols = pl.ds(j * 256, 256)
-        sums_ref[:, cols] = dot(mix_ref[0], get_rows(wide_ref, j, SLOTS), DOWN)
-        line_ref[:, cols] = dot(mix_ref[1], get_rows(wide_ref, j, SLOTS, AREA), DOWN)
-    inv, unit = unit_rows(far_x_ref[...])
+        yield pl.ds(j * 256, 256), dot(mix_ref[...], get_rows(wide_ref, j, SLOTS), DOWN)
+
+
+def behind_far(
+    zh_ref, home_ref, hot_ref, probs_ref, x_ref, gain_ref, sent_ref, gains_ref, wide_ref, line_ref, mix_ref
+):
+    pick = picks(iota((SLOTS, EXPERTS), 0) // MOST, (zh_ref[0] & 1))
+    mix_ref[...] = mixed_by(hot_ref[...], pick, probs_ref[...])
+    for cols, sums in block_sums(home_ref, mix_ref, wide_ref):
+        line_ref[:, cols] = sums
+    inv, unit = unit_rows(x_ref[...])
     sums = line_ref[...]
     sent_ref[...] = through_norm(sums, gain_ref[...], inv, unit).astype(bf16)
-    total = jnp.sum(sums * unit, axis=0, keepdims=True)
-    _, unit = unit_rows(near_x_ref[...])
-    total = total + jnp.sum(sums_ref[...] * unit, axis=0, keepdims=True)
+    gains_ref[...] = jnp.broadcast_to(jnp.sum(sums * unit, axis=0, keepdims=True), (8, D))
+
+
+SUMMING = [pltpu.VMEM((2, AREA, 128), f32), pltpu.VMEM((TOK, D), f32), pltpu.VMEM((SLOTS, TOK), bf16)]
+
+
+def run_behind_far(*args):
+    return call(
+        behind_far, (shape((TOK, D)), shape((8, D), f32)), [SMEM] + [VMEM] * 5, SUMMING, args, 10**9, 4
+    )
+
+
+def behind_near(
+    zh_ref, home_ref, hot_ref, probs_ref, logit_ref, gains_ref, x_ref, g_ref, gain_ref, table_ref,
+    sent_ref, mine_ref, theirs_ref, wide_ref, line_ref, mix_ref
+):
+    zh = (zh_ref[0] & 1)
+    pick = picks(iota((SLOTS, EXPERTS), 0) // MOST, zh)
+    mix_ref[...] = mixed_by(hot_ref[...], pick, probs_ref[...])
+    for cols, sums in block_sums(home_ref, mix_ref, wide_ref):
+        line_ref[:, cols] = sums
+    inv, unit = unit_rows(x_ref[...])
+    sums = line_ref[...] + dot(logit_ref[...], table_ref[...], DOWN)
+    sent_ref[...] = (g_ref[...].astype(f32) + through_norm(sums, gain_ref[...], inv, unit)).astype(bf16)
+    total = jnp.sum(sums * unit, axis=0, keepdims=True) + gains_ref[pl.ds(0, 1), :]
     theirs_ref[...] = jnp.zeros((8, 256), f32)
     mine_ref[...] = jnp.zeros((8, 256), f32)
     for x in range(4):
@@ -568,112 +586,106 @@
         theirs_ref[pl.ds(x, 1), :] = jnp.where(zh == 0, second, first)
 
 
-def run_behind_sums(*args):
-    return call(
-        behind_sums,
-        (shape((TOK, D), f32), shape((TOK, D)), shape((8, 256), f32), shape((8, 256), f32)),
-        [SMEM] + [VMEM] * 8,
-        [
-            pltpu.VMEM((2, 2 * AREA, 128), f32),
-            pltpu.VMEM((TOK, D), f32),
-            pltpu.VMEM((2, SLOTS, TOK), bf16),
-        ],
+def run_behind_near(*args):
+    return call(
+        behind_near,
+        (shape((TOK, D)), shape((8, 256), f32), shape((8, 256), f32)),
+        [SMEM] + [VMEM] * 9,
+        SUMMING,
         args,
         10**9,
-        6,
-    )
-
-
-def behind_end(
-    near_note_ref, far_note_ref, sums_ref, near_probs_ref, far_probs_ref, x_ref, g_ref, gain_ref, table_ref,
-    sent_ref, near_logit_ref, far_logit_ref
+        5,
+    )
+
+
+def behind_logits(
+    zh_ref, near_note_ref, far_note_ref, near_probs_ref, far_probs_ref, near_normed_ref, far_normed_ref,
+    logit_ref, parts_ref
 ):
     near_tok, far_tok = pl.ds(0, TOK), pl.ds(TOK, TOK)
 
     def logit_grads(probs, grads):
         return (probs * (grads - jnp.sum(probs * grads, axis=0, keepdims=True))).astype(bf16)
 
-    near_logit_ref[...] = logit_grads(near_probs_ref[...], near_note_ref[:, near_tok] + far_note_ref[:, far_tok])
-    far_logit_ref[...] = logit_grads(far_probs_ref[...], near_note_ref[:, far_tok] + far_note_ref[:, near_tok])
-    inv, unit = unit_rows(x_ref[...])
-    sums = sums_ref[...] + dot(near_logit_ref[...], table_ref[...], DOWN)
-    sent_ref[...] = (g_ref[...].astype(f32) + through_norm(sums, gain_ref[...], inv, unit)).astype(bf16)
-
-
-def run_behind_end(*args):
-    return call(
-        behind_end,
-        (shape((TOK, D)), shape((EXPERTS, TOK)), shape((EXPERTS, TOK))),
-        [VMEM] * 9,
+    near_logit = logit_grads(near_probs_ref[...], near_note_ref[:, near_tok] + far_note_ref[:, far_tok])
+    far_logit = logit_grads(far_probs_ref[...], near_note_ref[:, far_tok] + far_note_ref[:, near_tok])
+    logit_ref[...] = near_logit
+    for x in range(4):
+        cols = pl.ds(pl.multiple_of(x * 512 + (zh_ref[0] & 1) * 256, 256), 256)
+        part = dot(near_logit, near_normed_ref[:, cols]) + dot(far_logit, far_normed_ref[:, cols])
+        both = jnp.concatenate([part, jnp.zeros((128 - EXPERTS, 256), f32)], axis=0).T.astype(bf16)
+        for peer in range(8):
+            parts_ref[x * 8 + peer] = both[peer * 32 : peer * 32 + 32]
+
+
+def run_behind_logits(*args):
+    return call(
+        behind_logits,
+        (shape((EXPERTS, TOK)), shape((PEERS, PEERS, 128))),
+        [SMEM] + [VMEM] * 6,
         [],
         args,
         10**9,
-        4,
-    )
-
-
-def share_parts(
-    zh_ref, near_logit_ref, far_logit_ref, mine_ref, theirs_ref, near_normed_ref, far_normed_ref, near_x_ref,
-    far_x_ref, table_ref, shares_ref
-):
-    zh = zh_ref[0]
-    near_logit, far_logit = near_logit_ref[...], far_logit_ref[...]
-    _, near_unit = unit_rows(near_x_ref[...])
-    _, far_unit = unit_rows(far_x_ref[...])
-    near_term, far_term = dot(near_logit, table_ref[...], DOWN), dot(far_logit, table_ref[...], DOWN)
-    total = jnp.sum(near_term * near_unit + far_term * far_unit, axis=0, keepdims=True)
-    row = iota((128 - EXPERTS, 256), 0)
-    for x in range(4):
-        first, second = total[:, x * 512 : x * 512 + 256], total[:, x * 512 + 256 : x * 512 + 512]
-        gains = jnp.where(zh == 0, first, second) + mine_ref[pl.ds(x, 1), :] + theirs_ref[pl.ds(x, 1), :]
-        cols = pl.ds(pl.multiple_of(x * 512 + zh * 256, 256), 256)
-        part = dot(near_logit, near_normed_ref[:, cols]) + dot(far_logit, far_normed_ref[:, cols])
-        both = jnp.concatenate([part, jnp.where(row == 0, gains, 0.0)], axis=0)
-        shares_ref[pl.ds(x * 256, 256), :] = both.T.astype(bf16)
+        2,
+    )
+
+
+def share_parts(parts_ref, mine_ref, theirs_ref, shares_ref):
+    shares_ref[:, pl.ds(0, PEERS), :] = parts_ref[...]
+    gains = mine_ref[...] + theirs_ref[...]
+    for d in range(PEERS):
+        tile = gains[d // 8 : d // 8 + 1, d % 8 // 4 * 128 : d % 8 // 4 * 128 + 128]
+        shares_ref[d, pl.ds(PEERS, 8), :] = jnp.broadcast_to(tile, (8, 128)).astype(bf16)
 
 
 def run_share_parts(*args):
-    return call(share_parts, (shape((D // 2, 128)),), [SMEM] + [VMEM] * 9, [], args, 10**9, 3)[0]
-
-
-def ahead_sums(home_ref, mix_ref, wide_ref):
-    def take(d, rows):
-        for lane in range(2):
-            wide_ref[lane, rows, :] = home_ref[d, :, LANES[lane]].astype(f32)
-
-    each_peer(take)
-    for j in range(8):
-        yield pl.ds(j * 256, 256), dot(mix_ref[...], get_rows(wide_ref, j, SLOTS), DOWN)
+    return call(share_parts, (shape((PEERS, PEERS + 8, 128)),), [VMEM] * 3, [], args, 10**8, 1)[0]
 
 
 def ahead_far(home_ref, mix_ref, out_ref, wide_ref):
-    for cols, sums in ahead_sums(home_ref, mix_ref, wide_ref):
+    for cols, sums in block_sums(home_ref, mix_ref, wide_ref):
         out_ref[:, cols] = sums.astype(bf16)
 
 
 def ahead_near(home_ref, mix_ref, resid_ref, out_ref, wide_ref):
-    for cols, sums in ahead_sums(home_ref, mix_ref, wide_ref):
+    for cols, sums in block_sums(home_ref, mix_ref, wide_ref):
         out_ref[:, cols] = (resid_ref[:, cols].astype(f32) + sums).astype(bf16)
 
 
-def run_ahead_end(kernel, *args):
-    return call(
-        kernel, (shape((TOK, D)),), [VMEM] * len(args), [pltpu.VMEM((2, AREA, 128), f32)], args, 10**9, 3
-    )[0]
-
-
-def share_sums(got_ref, router_ref, gain_ref):
+def run_ahead_end(kernel, half, home, *rest):
+    return pl.pallas_call(
+        kernel,
+        grid=(1,),
+        out_shape=shape((TOK, D)),
+        in_specs=[pl.BlockSpec((PEERS, ROWS, 256), lambda i: (0, half, 0))] + [whole(a) for a in rest],
+        out_specs=pl.BlockSpec((TOK, D), lambda i: (0, 0)),
+        scratch_shapes=[pltpu.VMEM((2, AREA, 128), f32)],
+        compiler_params=pltpu.CompilerParams(vmem_limit_bytes=63 * 2**20),
+        cost_estimate=pl.CostEstimate(flops=10**9, transcendentals=0, bytes_accessed=3 * 2**20),
+    )(home, *rest)
+
+
+def share_sums(place_ref, got_ref, router_ref, gain_ref):
     total = got_ref[0].astype(f32)
     for source in range(1, PEERS):
         total = total + got_ref[source].astype(f32)
     total = total * factor
-    router_ref[...] = total[:, :EXPERTS]
-    gain_ref[...] = total.T[EXPERTS : EXPERTS + 1, :]
-
-
-def run_share_sums(got):
-    return call(
-        share_sums, (shape((PEERS, EXPERTS), f32), shape((1, PEERS), f32)), [VMEM], [], (got,), 10**6, 1
+    router_ref[...] = total[:PEERS, :EXPERTS]
+    gain = total[PEERS : PEERS + 1, :32]
+    for k in range(1, 4):
+        gain = jnp.where((place_ref[0] >> 1) == k, total[PEERS : PEERS + 1, k * 32 : k * 32 + 32], gain)
+    gain_ref[...] = gain
+
+
+def run_share_sums(place, got):
+    return call(
+        share_sums,
+        (shape((PEERS, EXPERTS), f32), shape((1, PEERS), f32)),
+        [SMEM, VMEM],
+        [],
+        (place, got),
+        10**6,
+        1,
     )
 
 
@@ -695,7 +707,8 @@
     backward_ids,
     output_grad,
 ):
-    zh = lax.axis_index("zh").astype(jnp.int32).reshape(1)
+    near_y, core = lax.axis_index("y") & 1, lax.axis_index("core")
+    zh = (lax.axis_index("zh") + 4 * near_y + 2 * core).astype(jnp.int32).reshape(1)
     gain = norm_gain
     table = router[0].T
     weights = (gate_weight[0, 0], up_weight[0, 0], down_weight[0, 0])
@@ -718,44 +731,40 @@
         zh, ids_b, ids_f, back_x, back_g, resid, gain, table
     )
     got_1 = spread_out(sent_1)
-    sent_2, normed_c, hot_c, probs_c = run_far_pack(zh, ids_far[:4], x_far, g_far, gain, table)
+    sent_3, normed_c, hot_c, probs_c = run_far_pack(zh, ids_far[:4], x_far, g_far, gain, table)
+    sent_2, mix_h = run_ahead_pack(zh, ids_far[4:], resid_far, gain, table)
     sent_2, _ = lax.optimization_barrier((sent_2, got_1))
     got_2 = spread_out(sent_2)
-    sent_3, mix_h = run_ahead_pack(zh, ids_far[4:], resid_far, gain, table)
     sent_3, got_2 = lax.optimization_barrier((sent_3, got_2))
     got_3 = spread_out(sent_3)
     back_b, small_b = run_near_experts(got_1, *weights)
-    back = run_far_experts(got_2, back_b, small_b, *weights)
-    back, got_3 = lax.optimization_barrier((back, got_3))
-    home_b = spread_out(back)
-    made_1, made_2 = run_ahead_experts(got_1, got_3, *weights)
-    made_1, home_b = lax.optimization_barrier((made_1, home_b))
-    home_1 = spread_out(made_1)
-    note = run_behind_note(zh, home_b, hot_b, hot_c)
+    made = run_ahead_experts(got_1, got_2, *weights)
+    made, got_3 = lax.optimization_barrier((made, got_3))
+    home_f = spread_out(made)
+    back_c = run_far_experts(got_3, small_b, *weights)
+    back_c, home_f = lax.optimization_barrier((back_c, home_f))
+    home_c = spread_out(back_c)
+    own_h = run_ahead_end(ahead_far, 1, home_f, mix_h)
+    moved_h = moved(own_h, False, 1)
+    own_f = run_ahead_end(ahead_near, 0, home_f, mix_f, resid)
+    moved_f = moved(own_f, True, 1)
+    back_b, home_c = lax.optimization_barrier((back_b, home_c))
+    home_d = spread_out(back_b)
+    note = run_behind_note(zh, home_c, hot_b, hot_c)
     far_note = swapped(note)
-    sums_b, own_c, theirs, mine = run_behind_sums(
-        zh, home_b, hot_b, hot_c, probs_b, probs_c, back_x, x_far, gain
-    )
+    own_c, gains_c = run_behind_far(zh, home_c, hot_c, probs_c, x_far, gain)
     moved_c = moved(own_c, False, -1)
-    own_b, logit_b, logit_c = run_behind_end(
-        note, far_note, sums_b, probs_b, probs_c, back_x, back_g, gain, table
-    )
+    logit_b, parts = run_behind_logits(zh, note, far_note, probs_b, probs_c, normed_b, normed_c)
+    own_b, mine, theirs = run_behind_near(
+        zh, home_d, hot_b, probs_b, logit_b, gains_c, back_x, back_g, gain, table
+    )
+    theirs = swapped(theirs)
     moved_b = moved(own_b, True, -1)
-    made_2, home_1 = lax.optimization_barrier((made_2, home_1))
-    home_2 = spread_out(made_2)
-    own_h = run_ahead_end(ahead_far, home_1, mix_h)
-    moved_h = moved(own_h, False, 1)
-    theirs = swapped(theirs)
-    shares = run_share_parts(
-        zh, logit_b, logit_c, mine, theirs, normed_b, normed_c, back_x, x_far, table
-    )
-    own_f = run_ahead_end(ahead_near, home_2, mix_f, resid)
-    moved_f = moved(own_f, True, 1)
-    shares, own_f = lax.optimization_barrier((shares, own_f))
-    got_s = spread_out(shares.reshape(PEERS, PEERS, 128))
-    router_grad, gain_grad = run_share_sums(got_s)
+    shares = run_share_parts(parts, mine, theirs)
+    got_s = spread_out(shares)
+    router_grad, gain_grad = run_share_sums(zh, got_s)
+    forward_output = (moved_f.astype(f32) + moved_h.astype(f32)).astype(bf16)
     input_grad = (moved_b.astype(f32) + moved_c.astype(f32)).astype(bf16)
-    forward_output = (moved_f.astype(f32) + moved_h.astype(f32)).astype(bf16)
     return forward_output[None], input_grad[None], router_grad[None], gain_grad
 
 

time: 314 us -> 336 us (1.070)
  starting transfers between devices: 96.3 us -> 114 us
  waiting for transfers between devices: 95.2 us -> 99.6 us
    ppermute x4, starting transfers between devices: 2.17 us -> 37.3 us  [moved(): return lax.ppermute(x, ('pipe', 'zh'), pairs)]
    all_to_all x6, waiting for transfers between devices: 29.5 us -> 42.6 us  [spread_out(): return lax.all_to_all(x, XY, 0, 0, tiled=True)]
    ppermute x6, starting transfers between devices: 29.2 us -> 19.9 us  [swapped(): return lax.ppermute(x, 'zh', [(0, 1), (1, 0)])]
    ppermute x6, waiting for transfers between devices: 65.8 us -> 57 us  [swapped(): return lax.ppermute(x, 'zh', [(0, 1), (1, 0)])]
    all_to_all x6, starting transfers between devices: 65 us -> 57.2 us  [spread_out(): return lax.all_to_all(x, XY, 0, 0, tiled=True)]
    pallas_call x13 -> x12, Pallas kernels: 84.3 us -> 77.8 us  [call(): pl.pallas_call(kernel, out_shape=outs, in_specs=ins, out_specs=tuple((VME...]
    pallas_call x0 -> x2, Pallas kernels: none -> 6 us  [run_ahead_end(): pl.pallas_call(kernel, grid=(1,), out_shape=shape((TOK, D)), in_specs=[pl...]
  transfers between devices with their start and end apart: 16 -> 16, of which waited for: 7 -> 9; matrix products, arithmetic and copies ran while one was open for 1% -> 1% of each run, Pallas kernels for 24% -> 23%
where the time goes in v3:
time: 336 us; the launch traced here: 335 us
  starting transfers between devices  114 us (34%)
  waiting for transfers between devices  99.6 us (30%)
  Pallas kernels  85.9 us (26%)
  blocking collectives  25.5 us (8%)
  local copies, waits for them, and re-layouts  4.19 us (1%)
  other arithmetic  4.09 us (1%)
    pallas_call x12, Pallas kernels, call(): pl.pallas_call(kernel, out_shape=outs, in_specs=ins, out_specs=tuple((VME...  77.8 us
    all_to_all x6, starting transfers between devices, spread_out(): return lax.all_to_all(x, XY, 0, 0, tiled=True)  57.2 us
    ppermute x6, waiting for transfers between devices, swapped(): return lax.ppermute(x, 'zh', [(0, 1), (1, 0)])  57 us
    all_to_all x6, waiting for transfers between devices, spread_out(): return lax.all_to_all(x, XY, 0, 0, tiled=True)  42.6 us
    ppermute x4, starting transfers between devices, moved(): return lax.ppermute(x, ('pipe', 'zh'), pairs)  37.3 us
    all_to_all x1, blocking collectives, spread_out(): return lax.all_to_all(x, XY, 0, 0, tiled=True)  25.5 us
    ppermute x6, starting transfers between devices, swapped(): return lax.ppermute(x, 'zh', [(0, 1), (1, 0)])  19.9 us
  transfers between devices with their start and end apart: 16, of which 9 were waited for; matrix products, arithmetic and copies ran while one was open for 1% of the time, Pallas kernels for 23%

profile of v3, /device:TPU:1, one launch (start us, length us, event | category | flops | bytes accessed | tf_op | source)
XLA Modules:
  0.0 335.2 jit_solution(5003444535526938689)
XLA Ops:
  4.9 6.6 %shard_map.184 = (bf16[32,216,256]{2,1,0:T(8,128)(2,1)}, bf16[128,2048]{1,0:T(8,128)(2,1)}, bf16[288,128]{1,0:T(8,128)(2,1)}, f32[64,128]{1,0:T(8,128)}, bf16[288,128]{1,0:T(8,128)(2,1)}) custom-call(s32[1]{0:T(128)} %bitcast.zh_ref.place_ref, s32[4,128]{1,0:T(4,128)} %bitcast.26, s32[4,128]{1,0:T(4,128)} %bitcast.28, bf16[128,2048]{1,0:T(8,128)(2,1)} %bitcast.41, ...), custom_call_target="tpu_custom_call" | custom-call | flops 2000000000 | bytes 8388608 | tf_op jit(solution)/shard_map/pallas_call | solution.py:58
  11.6 8.8 %all-to-all-start = ((bf16[32,216,256]{2,1,0:T(8,128)(2,1)}), bf16[32,216,256]{2,1,0:T(8,128)(2,1)}, u32[]{:S(2)}, u32[]{:S(2)}) async-start(bf16[32,216,256]{2,1,0:T(8,128)(2,1)} %get-tuple-element.35), calls=%async_computation | async-start | bytes 7077888 | tf_op jit(solution)/shard_map/all_to_all | solution.py:37
  20.3 7.0 %collective-permute-start.3 = (bf16[128,2048]{1,0:T(8,128)(2,1)S(1)}, bf16[128,2048]{1,0:T(8,128)(2,1)S(1)}, u32[]{:S(2)}, u32[]{:S(2)}) collective-permute-start(bf16[128,2048]{1,0:T(8,128)(2,1)S(1)} %copy-done.6), channel_id=1, source_target_pairs={{0,8},{8,0},{1,9},{9,1},{2,10},{10,2},{3,11},{11,3},{4,12},{12,4},... | collective-permute-start | bytes 1572872 | tf_op jit(solution)/shard_map/ppermute | solution.py:41
  27.5 14.2 %collective-permute-done = s32[8,128]{1,0:T(8,128)S(1)} collective-permute-done((s32[8,128]{1,0:T(8,128)S(1)}, s32[8,128]{1,0:T(8,128)S(1)}, u32[]{:S(2)}, u32[]{:S(2)}) %collective-permute-start) | collective-permute-done | bytes 4128 | tf_op jit(solution)/shard_map/ppermute | solution.py:41
  43.1 5.1 %shard_map.186 = (bf16[32,72,256]{2,1,0:T(8,128)(2,1)}, bf16[288,128]{1,0:T(8,128)(2,1)}) custom-call(s32[1]{0:T(128)} %bitcast.zh_ref.place_ref, s32[4,128]{1,0:T(4,128)} %get-tuple-element.66.ids_ref, bf16[128,2048]{1,0:T(8,128)(2,1)} %copy-done.8, f32[1,2048]{1,0:T(1,128)} %gain_ref.9, bf16[64,2048]{1,0:T(8,128)(2,1)} %bitcast.48), custom_call_target="tpu_custom_call" | custom-call | flops 1000000000 | bytes 4194304 | tf_op jit(solution)/shard_map/pallas_call | solution.py:58
  48.2 16.0 %all-to-all-done.near_ref.got_ref = bf16[32,216,256]{2,1,0:T(8,128)(2,1)} async-done(((bf16[32,216,256]{2,1,0:T(8,128)(2,1)}), bf16[32,216,256]{2,1,0:T(8,128)(2,1)}, u32[]{:S(2)}, u32[]{:S(2)}) %all-to-all-start) | async-done | bytes 3538976 | tf_op jit(solution)/shard_map/all_to_all | solution.py:37
  64.3 6.4 %all-to-all-start.1 = ((bf16[32,72,256]{2,1,0:T(8,128)(2,1)}), bf16[32,72,256]{2,1,0:T(8,128)(2,1)}, u32[]{:S(2)}, u32[]{:S(2)}) async-start(bf16[32,72,256]{2,1,0:T(8,128)(2,1)} %get-tuple-element.38), calls=%async_computation.1 | async-start | bytes 2359296 | tf_op jit(solution)/shard_map/all_to_all | solution.py:37
  70.7 7.0 %collective-permute-start.1 = (bf16[128,2048]{1,0:T(8,128)(2,1)S(1)}, bf16[128,2048]{1,0:T(8,128)(2,1)S(1)}, u32[]{:S(2)}, u32[]{:S(2)}) collective-permute-start(bf16[128,2048]{1,0:T(8,128)(2,1)S(1)} %bitcast.43), channel_id=1, source_target_pairs={{0,8},{8,0},{1,9},{9,1},{2,10},{10,2},{3,11},{11,3},{4,12},{12,4},... | collective-permute-start | bytes 1572872 | tf_op jit(solution)/shard_map/ppermute | solution.py:41
  77.8 14.0 %collective-permute-done.1.x_ref = bf16[128,2048]{1,0:T(8,128)(2,1)S(1)} collective-permute-done((bf16[128,2048]{1,0:T(8,128)(2,1)S(1)}, bf16[128,2048]{1,0:T(8,128)(2,1)S(1)}, u32[]{:S(2)}, u32[]{:S(2)}) %collective-permute-start.1) | collective-permute-done | bytes 524320 | tf_op jit(solution)/shard_map/ppermute | solution.py:41
  91.9 15.1 %collective-permute-done.2.g_ref = bf16[128,2048]{1,0:T(8,128)(2,1)S(1)} collective-permute-done((bf16[128,2048]{1,0:T(8,128)(2,1)S(1)}, bf16[128,2048]{1,0:T(8,128)(2,1)S(1)}, u32[]{:S(2)}, u32[]{:S(2)}) %collective-permute-start.2) | collective-permute-done | bytes 524320 | tf_op jit(solution)/shard_map/ppermute | solution.py:41
  107.8 5.1 %shard_map.185 = (bf16[32,144,256]{2,1,0:T(8,128)(2,1)}, bf16[128,2048]{1,0:T(8,128)(2,1)}, bf16[288,128]{1,0:T(8,128)(2,1)}, f32[64,128]{1,0:T(8,128)}) custom-call(s32[1]{0:T(128)} %bitcast.zh_ref.place_ref, s32[4,128]{1,0:T(4,128)} %get-tuple-element.67.ids_ref, bf16[128,2048]{1,0:T(8,128)(2,1)} %copy-done.7, bf16[128,2048]{1,0:T(8,128)(2,1)} %copy-done.9, ...), custom_call_target="tpu_custom_call" | custom-call | flops 1000000000 | bytes 6291456 | tf_op jit(solution)/shard_map/pallas_call | solution.py:58
  112.9 23.1 %all-to-all-start.2 = ((bf16[32,144,256]{2,1,0:T(8,128)(2,1)}), bf16[32,144,256]{2,1,0:T(8,128)(2,1)}, u32[]{:S(2)}, u32[]{:S(2)}) async-start(bf16[32,144,256]{2,1,0:T(8,128)(2,1)} %get-tuple-element.40), calls=%async_computation.2 | async-start | bytes 4718592 | tf_op jit(solution)/shard_map/all_to_all | solution.py:37
  136.0 15.9 %shard_map.187 = bf16[32,144,256]{2,1,0:T(8,128)(2,1)} custom-call(bf16[32,216,256]{2,1,0:T(8,128)(2,1)} %all-to-all-done.near_ref.got_ref, bf16[32,72,256]{2,1,0:T(8,128)(2,1)} %all-to-all-done.1.far_ref, bf16[2048,768]{1,0:T(8,128)(2,1)} %bitcast.30, bf16[2048,768]{1,0:T(8,128)(2,1)} %bitcast.33, bf16[768,2048]{1,0:T(8,128)(2,1)} %bitcast.36), custom_call_target="tpu_custom_call" | custom-call | flops 6000000000 | bytes 14680064 | tf_op jit(solution)/shard_map/pallas_call | solution.py:58
  151.9 15.3 %all-to-all-done.2.got_ref = bf16[32,144,256]{2,1,0:T(8,128)(2,1)} async-done(((bf16[32,144,256]{2,1,0:T(8,128)(2,1)}), bf16[32,144,256]{2,1,0:T(8,128)(2,1)}, u32[]{:S(2)}, u32[]{:S(2)}) %all-to-all-start.2) | async-done | bytes 2359328 | tf_op jit(solution)/shard_map/all_to_all | solution.py:37
  167.3 5.4 %all-to-all-start.3 = ((bf16[32,144,256]{2,1,0:T(8,128)(2,1)}), bf16[32,144,256]{2,1,0:T(8,128)(2,1)}, u32[]{:S(2)}, u32[]{:S(2)}) async-start(bf16[32,144,256]{2,1,0:T(8,128)(2,1)} %shard_map.187), calls=%async_computation.3 | async-start | bytes 4718592 | tf_op jit(solution)/shard_map/all_to_all | solution.py:37
  172.7 15.6 %shard_map.188 = (bf16[32,72,256]{2,1,0:T(8,128)(2,1)}, f32[256,128]{1,0:T(8,128)}) custom-call(bf16[32,216,256]{2,1,0:T(8,128)(2,1)} %all-to-all-done.near_ref.got_ref, bf16[2048,768]{1,0:T(8,128)(2,1)} %bitcast.31, bf16[2048,768]{1,0:T(8,128)(2,1)} %bitcast.34, bf16[768,2048]{1,0:T(8,128)(2,1)} %bitcast.37), custom_call_target="tpu_custom_call" | custom-call | flops 5000000000 | bytes 13631488 | tf_op jit(solution)/shard_map/pallas_call | solution.py:58
  188.3 11.9 %shard_map.189 = bf16[32,80,256]{2,1,0:T(8,128)(2,1)} custom-call(bf16[32,144,256]{2,1,0:T(8,128)(2,1)} %all-to-all-done.2.got_ref, f32[256,128]{1,0:T(8,128)} %get-tuple-element.42.near_small_ref, bf16[2048,768]{1,0:T(8,128)(2,1)} %bitcast.32, bf16[2048,768]{1,0:T(8,128)(2,1)} %bitcast.35, bf16[768,2048]{1,0:T(8,128)(2,1)} %bitcast.38), custom_call_target="tpu_custom_call" | custom-call | flops 5000000000 | bytes 15728640 | tf_op jit(solution)/shard_map/pallas_call | solution.py:58
  204.0 25.5 %all_to_all.35.home_ref = bf16[32,80,256]{2,1,0:T(8,128)(2,1)} all-to-all(bf16[32,80,256]{2,1,0:T(8,128)(2,1)} %shard_map.189), channel_id=1, replica_groups=mesh['pipe'=4,'x'=4,'zh'=2,'y'=4,'core'=2] {'x','y','core'}, dimensions={0} | all-to-all | bytes 2621440 | tf_op jit(solution)/shard_map/all_to_all | solution.py:37
  239.9 6.2 %collective-permute-start.5 = (bf16[128,2048]{1,0:T(8,128)(2,1)}, bf16[128,2048]{1,0:T(8,128)(2,1)}, u32[]{:S(2)}, u32[]{:S(2)}) collective-permute-start(bf16[128,2048]{1,0:T(8,128)(2,1)} %shard_map.191), channel_id=1, source_target_pairs={{0,72},{8,64},{64,136},{72,128},{128,200},{136,192},{192,8},{200,0... | collective-permute-start | bytes 1572872 | tf_op jit(solution)/shard_map/ppermute | solution.py:50
  267.3 26.1 %collective-permute-start.7 = (bf16[128,2048]{1,0:T(8,128)(2,1)}, bf16[128,2048]{1,0:T(8,128)(2,1)}, u32[]{:S(2)}, u32[]{:S(2)}) collective-permute-start(bf16[128,2048]{1,0:T(8,128)(2,1)} %get-tuple-element.59), channel_id=1, source_target_pairs={{0,192},{8,200},{64,0},{72,8},{128,64},{136,72},{192,128},{200,136... | collective-permute-start | bytes 1572872 | tf_op jit(solution)/shard_map/ppermute | solution.py:50
  293.4 5.0 %collective-permute-start.9 = (f32[8,256]{1,0:T(8,128)}, f32[8,256]{1,0:T(8,128)S(1)}, u32[]{:S(2)}, u32[]{:S(2)}) collective-permute-start(f32[8,256]{1,0:T(8,128)} %get-tuple-element.63), channel_id=1, source_target_pairs={{0,8},{8,0},{1,9},{9,1},{2,10},{10,2},{3,11},{11,3},{4,12},{12,4},... | collective-permute-start | bytes 24584 | tf_op jit(solution)/shard_map/ppermute | solution.py:41
  298.4 11.3 %collective-permute-done.9.theirs_ref = f32[8,256]{1,0:T(8,128)S(1)} collective-permute-done((f32[8,256]{1,0:T(8,128)}, f32[8,256]{1,0:T(8,128)S(1)}, u32[]{:S(2)}, u32[]{:S(2)}) %collective-permute-start.9) | collective-permute-done | bytes 8224 | tf_op jit(solution)/shard_map/ppermute | solution.py:41
  312.0 9.0 %all-to-all-start.6 = ((bf16[32,40,128]{2,1,0:T(8,128)(2,1)}), bf16[32,40,128]{2,1,0:T(8,128)(2,1)S(1)}, u32[]{:S(2)}, u32[]{:S(2)}) async-start(bf16[32,40,128]{2,1,0:T(8,128)(2,1)} %shard_map.196), calls=%async_computation.6 | async-start | bytes 655360 | tf_op jit(solution)/shard_map/all_to_all | solution.py:37
  323.2 7.5 %all-to-all-done.6.got_ref = bf16[32,40,128]{2,1,0:T(8,128)(2,1)S(1)} async-done(((bf16[32,40,128]{2,1,0:T(8,128)(2,1)}), bf16[32,40,128]{2,1,0:T(8,128)(2,1)S(1)}, u32[]{:S(2)}, u32[]{:S(2)}) %all-to-all-start.6) | async-done | bytes 327712 | tf_op jit(solution)/shard_map/all_to_all | solution.py:37
  (50 shorter events, 50.4 us)
Async XLA Ops:
  11.5 8.8 %copy-start.6 = (bf16[128,2048]{1,0:T(8,128)(2,1)S(1)}, bf16[128,2048]{1,0:T(8,128)(2,1)}, u32[]{:S(2)}) copy-start(bf16[128,2048]{1,0:T(8,128)(2,1)} %shard_map.183.resid_ref) | copy-start | bytes 1572868
  11.5 15.8 %copy-start.2 = (s32[1,128,4]{1,2,0:T(4,128)S(1)}, s32[1,128,4]{1,2,0:T(4,128)}, u32[]{:S(2)}) copy-start(s32[1,128,4]{1,2,0:T(4,128)} %param.30) | copy-start | bytes 6148
  11.5 15.8 %copy-start.3 = (s32[1,128,4]{1,2,0:T(4,128)S(1)}, s32[1,128,4]{1,2,0:T(4,128)}, u32[]{:S(2)}) copy-start(s32[1,128,4]{1,2,0:T(4,128)} %param.28) | copy-start | bytes 6148
  11.6 52.7 %all-to-all-start = ((bf16[32,216,256]{2,1,0:T(8,128)(2,1)}), bf16[32,216,256]{2,1,0:T(8,128)(2,1)}, u32[]{:S(2)}, u32[]{:S(2)}) async-start(bf16[32,216,256]{2,1,0:T(8,128)(2,1)} %get-tuple-element.35), calls=%async_computation | async-start | bytes 7077888 | tf_op jit(solution)/shard_map/all_to_all | solution.py:37
  20.3 21.9 %collective-permute-start.3 = (bf16[128,2048]{1,0:T(8,128)(2,1)S(1)}, bf16[128,2048]{1,0:T(8,128)(2,1)S(1)}, u32[]{:S(2)}, u32[]{:S(2)}) collective-permute-start(bf16[128,2048]{1,0:T(8,128)(2,1)S(1)} %copy-done.6), channel_id=1, source_target_pairs={{0,8},{8,0},{1,9},{9,1},{2,10},{10,2},{3,11},{11,3},{4,12},{12,4},... | collective-permute-start | bytes 1572872 | tf_op jit(solution)/shard_map/ppermute | solution.py:41
  27.4 14.3 %collective-permute-start = (s32[8,128]{1,0:T(8,128)S(1)}, s32[8,128]{1,0:T(8,128)S(1)}, u32[]{:S(2)}, u32[]{:S(2)}) collective-permute-start(s32[8,128]{1,0:T(8,128)S(1)} %pad_add_fusion), channel_id=1, source_target_pairs={{0,8},{8,0},{1,9},{9,1},{2,10},{10,2},{3,11},{11,3},{4,12},{12,4},... | collective-permute-start | bytes 12296 | tf_op jit(solution)/shard_map/ppermute | solution.py:41
  42.3 0.8 copy-start.8
  43.1 27.6 %copy-start.4 = (bf16[1,128,2048]{2,1,0:T(8,128)(2,1)S(1)}, bf16[1,128,2048]{2,1,0:T(8,128)(2,1)}, u32[]{:S(2)}) copy-start(bf16[1,128,2048]{2,1,0:T(8,128)(2,1)} %param.29) | copy-start | bytes 1572868
  48.2 29.5 %copy-start.5 = (bf16[1,128,2048]{2,1,0:T(8,128)(2,1)S(1)}, bf16[1,128,2048]{2,1,0:T(8,128)(2,1)}, u32[]{:S(2)}) copy-start(bf16[1,128,2048]{2,1,0:T(8,128)(2,1)} %param.31) | copy-start | bytes 1572868
  64.3 48.6 %all-to-all-start.1 = ((bf16[32,72,256]{2,1,0:T(8,128)(2,1)}), bf16[32,72,256]{2,1,0:T(8,128)(2,1)}, u32[]{:S(2)}, u32[]{:S(2)}) async-start(bf16[32,72,256]{2,1,0:T(8,128)(2,1)} %get-tuple-element.38), calls=%async_computation.1 | async-start | bytes 2359296 | tf_op jit(solution)/shard_map/all_to_all | solution.py:37
  70.7 21.1 %collective-permute-start.1 = (bf16[128,2048]{1,0:T(8,128)(2,1)S(1)}, bf16[128,2048]{1,0:T(8,128)(2,1)S(1)}, u32[]{:S(2)}, u32[]{:S(2)}) collective-permute-start(bf16[128,2048]{1,0:T(8,128)(2,1)S(1)} %bitcast.43), channel_id=1, source_target_pairs={{0,8},{8,0},{1,9},{9,1},{2,10},{10,2},{3,11},{11,3},{4,12},{12,4},... | collective-permute-start | bytes 1572872 | tf_op jit(solution)/shard_map/ppermute | solution.py:41
  77.7 29.2 %collective-permute-start.2 = (bf16[128,2048]{1,0:T(8,128)(2,1)S(1)}, bf16[128,2048]{1,0:T(8,128)(2,1)S(1)}, u32[]{:S(2)}, u32[]{:S(2)}) collective-permute-start(bf16[128,2048]{1,0:T(8,128)(2,1)S(1)} %bitcast.46), channel_id=1, source_target_pairs={{0,8},{8,0},{1,9},{9,1},{2,10},{10,2},{3,11},{11,3},{4,12},{12,4},... | collective-permute-start | bytes 1572872 | tf_op jit(solution)/shard_map/ppermute | solution.py:41
  91.9 15.1 %copy-start.7 = (bf16[128,2048]{1,0:T(8,128)(2,1)}, bf16[128,2048]{1,0:T(8,128)(2,1)S(1)}, u32[]{:S(2)}) copy-start(bf16[128,2048]{1,0:T(8,128)(2,1)S(1)} %collective-permute-done.1.x_ref) | copy-start | bytes 1572868
  107.0 0.8 copy-start.9
  112.9 54.4 %all-to-all-start.2 = ((bf16[32,144,256]{2,1,0:T(8,128)(2,1)}), bf16[32,144,256]{2,1,0:T(8,128)(2,1)}, u32[]{:S(2)}, u32[]{:S(2)}) async-start(bf16[32,144,256]{2,1,0:T(8,128)(2,1)} %get-tuple-element.40), calls=%async_computation.2 | async-start | bytes 4718592 | tf_op jit(solution)/shard_map/all_to_all | solution.py:37
  167.3 36.7 %all-to-all-start.3 = ((bf16[32,144,256]{2,1,0:T(8,128)(2,1)}), bf16[32,144,256]{2,1,0:T(8,128)(2,1)}, u32[]{:S(2)}, u32[]{:S(2)}) async-start(bf16[32,144,256]{2,1,0:T(8,128)(2,1)} %shard_map.187), calls=%async_computation.3 | async-start | bytes 4718592 | tf_op jit(solution)/shard_map/all_to_all | solution.py:37
  229.5 33.7 %all-to-all-start.5 = ((bf16[32,72,256]{2,1,0:T(8,128)(2,1)}), bf16[32,72,256]{2,1,0:T(8,128)(2,1)}, u32[]{:S(2)}, u32[]{:S(2)}) async-start(bf16[32,72,256]{2,1,0:T(8,128)(2,1)} %get-tuple-element.49), calls=%async_computation.5 | async-start | bytes 2359296 | tf_op jit(solution)/shard_map/all_to_all | solution.py:37
  239.9 81.1 %collective-permute-start.5 = (bf16[128,2048]{1,0:T(8,128)(2,1)}, bf16[128,2048]{1,0:T(8,128)(2,1)}, u32[]{:S(2)}, u32[]{:S(2)}) collective-permute-start(bf16[128,2048]{1,0:T(8,128)(2,1)} %shard_map.191), channel_id=1, source_target_pairs={{0,72},{8,64},{64,136},{72,128},{128,200},{136,192},{192,8},{200,0... | collective-permute-start | bytes 1572872 | tf_op jit(solution)/shard_map/ppermute | solution.py:50
  246.1 75.0 %collective-permute-start.4 = (bf16[128,2048]{1,0:T(8,128)(2,1)}, bf16[128,2048]{1,0:T(8,128)(2,1)}, u32[]{:S(2)}, u32[]{:S(2)}) collective-permute-start(bf16[128,2048]{1,0:T(8,128)(2,1)} %shard_map.190), channel_id=1, source_target_pairs={{0,64},{8,72},{64,128},{72,136},{128,192},{136,200},{192,0},{200,8... | collective-permute-start | bytes 1572872 | tf_op jit(solution)/shard_map/ppermute | solution.py:50
  248.7 11.4 %collective-permute-start.6 = (f32[64,256]{1,0:T(8,128)}, f32[64,256]{1,0:T(8,128)S(1)}, u32[]{:S(2)}, u32[]{:S(2)}) collective-permute-start(f32[64,256]{1,0:T(8,128)} %shard_map.192.near_note_ref), channel_id=1, source_target_pairs={{0,8},{8,0},{1,9},{9,1},{2,10},{10,2},{3,11},{11,3},{4,12},{12,4},... | collective-permute-start | bytes 196616 | tf_op jit(solution)/shard_map/ppermute | solution.py:41
  253.4 79.9 %collective-permute-start.8 = (bf16[128,2048]{1,0:T(8,128)(2,1)}, bf16[128,2048]{1,0:T(8,128)(2,1)S(1)}, u32[]{:S(2)}, u32[]{:S(2)}) collective-permute-start(bf16[128,2048]{1,0:T(8,128)(2,1)} %get-tuple-element.60), channel_id=1, source_target_pairs={{0,200},{8,192},{64,8},{72,0},{128,72},{136,64},{192,136},{200,128... | collective-permute-start | bytes 1572872 | tf_op jit(solution)/shard_map/ppermute | solution.py:50
  267.3 66.0 %collective-permute-start.7 = (bf16[128,2048]{1,0:T(8,128)(2,1)}, bf16[128,2048]{1,0:T(8,128)(2,1)}, u32[]{:S(2)}, u32[]{:S(2)}) collective-permute-start(bf16[128,2048]{1,0:T(8,128)(2,1)} %get-tuple-element.59), channel_id=1, source_target_pairs={{0,192},{8,200},{64,0},{72,8},{128,64},{136,72},{192,128},{200,136... | collective-permute-start | bytes 1572872 | tf_op jit(solution)/shard_map/ppermute | solution.py:50
  293.4 16.3 %collective-permute-start.9 = (f32[8,256]{1,0:T(8,128)}, f32[8,256]{1,0:T(8,128)S(1)}, u32[]{:S(2)}, u32[]{:S(2)}) collective-permute-start(f32[8,256]{1,0:T(8,128)} %get-tuple-element.63), channel_id=1, source_target_pairs={{0,8},{8,0},{1,9},{9,1},{2,10},{10,2},{3,11},{11,3},{4,12},{12,4},... | collective-permute-start | bytes 24584 | tf_op jit(solution)/shard_map/ppermute | solution.py:41
  312.0 18.6 %all-to-all-start.6 = ((bf16[32,40,128]{2,1,0:T(8,128)(2,1)}), bf16[32,40,128]{2,1,0:T(8,128)(2,1)S(1)}, u32[]{:S(2)}, u32[]{:S(2)}) async-start(bf16[32,40,128]{2,1,0:T(8,128)(2,1)} %shard_map.196), calls=%async_computation.6 | async-start | bytes 655360 | tf_op jit(solution)/shard_map/all_to_all | solution.py:37
  (3 other events, 1.9 us)

commit v4 on v2

--- a/solution.py
+++ b/solution.py
@@ -417,7 +417,7 @@
 
 
 def ahead_experts(
-    near_ref, far_ref, gate_hbm, up_hbm, down_hbm, first_ref, second_ref, wide_ref, gate_ref, up_ref, down_ref, sems,
+    near_ref, far_ref, gate_hbm, up_hbm, down_hbm, made_ref, wide_ref, gate_ref, up_ref, down_ref, sems,
     gate_sum, up_sum, hidden_ref
 ):
     copies = fetched(((gate_hbm, gate_ref), (up_hbm, up_ref), (down_hbm, down_ref)), sems)
@@ -451,8 +451,8 @@
 
     def put(d, rows):
         for lane in range(2):
-            first_ref[d, :, LANES[lane]] = wide_ref[lane, area_rows(d, 1), :].astype(bf16)
-            second_ref[d, :, LANES[lane]] = wide_ref[lane, area_rows(d, 0), :].astype(bf16)
+            for half in range(2):
+                made_ref[d, pl.ds(half * ROWS, ROWS), LANES[lane]] = wide_ref[lane, area_rows(d, half), :].astype(bf16)
 
     each_peer(put)
 
@@ -460,7 +460,7 @@
 def run_ahead_experts(*args):
     return call(
         ahead_experts,
-        (shape((PEERS, ROWS, 256)), shape((PEERS, ROWS, 256))),
+        (shape((PEERS, 2 * ROWS, 256)),),
         [VMEM] * 2 + [HBM] * 3,
         [pltpu.VMEM((2, 2 * AREA, 128), f32)]
         + WEIGHTS
@@ -468,7 +468,7 @@
         args,
         6 * 10**9,
         14,
-    )
+    )[0]
 
 
 def attend(length_ref, x_ref, q_ref, kc_ref, kn_ref, vc_ref, vn_ref, resid_ref):
@@ -656,10 +656,17 @@
         out_ref[:, cols] = (resid_ref[:, cols].astype(f32) + sums).astype(bf16)
 
 
-def run_ahead_end(kernel, *args):
-    return call(
-        kernel, (shape((TOK, D)),), [VMEM] * len(args), [pltpu.VMEM((2, AREA, 128), f32)], args, 10**9, 3
-    )[0]
+def run_ahead_end(kernel, half, home, *rest):
+    return pl.pallas_call(
+        kernel,
+        grid=(1,),
+        out_shape=shape((TOK, D)),
+        in_specs=[pl.BlockSpec((PEERS, ROWS, 256), lambda i: (0, half, 0))] + [whole(a) for a in rest],
+        out_specs=pl.BlockSpec((TOK, D), lambda i: (0, 0)),
+        scratch_shapes=[pltpu.VMEM((2, AREA, 128), f32)],
+        compiler_params=pltpu.CompilerParams(vmem_limit_bytes=63 * 2**20),
+        cost_estimate=pl.CostEstimate(flops=10**9, transcendentals=0, bytes_accessed=3 * 2**20),
+    )(home, *rest)
 
 
 def share_sums(got_ref, router_ref, gain_ref):
@@ -728,9 +735,9 @@
     back = run_far_experts(got_2, back_b, small_b, *weights)
     back, got_3 = lax.optimization_barrier((back, got_3))
     home_b = spread_out(back)
-    made_1, made_2 = run_ahead_experts(got_1, got_3, *weights)
-    made_1, home_b = lax.optimization_barrier((made_1, home_b))
-    home_1 = spread_out(made_1)
+    made = run_ahead_experts(got_1, got_3, *weights)
+    made, home_b = lax.optimization_barrier((made, home_b))
+    home_f = spread_out(made)
     note = run_behind_note(zh, home_b, hot_b, hot_c)
     far_note = swapped(note)
     sums_b, own_c, theirs, mine = run_behind_sums(
@@ -741,15 +748,13 @@
         note, far_note, sums_b, probs_b, probs_c, back_x, back_g, gain, table
     )
     moved_b = moved(own_b, True, -1)
-    made_2, home_1 = lax.optimization_barrier((made_2, home_1))
-    home_2 = spread_out(made_2)
-    own_h = run_ahead_end(ahead_far, home_1, mix_h)
+    own_h = run_ahead_end(ahead_far, 1, home_f, mix_h)
     moved_h = moved(own_h, False, 1)
     theirs = swapped(theirs)
     shares = run_share_parts(
         zh, logit_b, logit_c, mine, theirs, normed_b, normed_c, back_x, x_far, table
     )
-    own_f = run_ahead_end(ahead_near, home_2, mix_f, resid)
+    own_f = run_ahead_end(ahead_near, 0, home_f, mix_f, resid)
     moved_f = moved(own_f, True, 1)
     shares, own_f = lax.optimization_barrier((shares, own_f))
     got_s = spread_out(shares.reshape(PEERS, PEERS, 128))

time: 314 us -> 290 us (0.924)
  blocking collectives: 24.2 us -> 0 us
  starting transfers between devices: 96.3 us -> 103 us
  waiting for transfers between devices: 95.2 us -> 89 us
    all_to_all x1 -> x0, blocking collectives: 24.2 us -> none  [spread_out(): return lax.all_to_all(x, XY, 0, 0, tiled=True)]
    ppermute x6, waiting for transfers between devices: 65.8 us -> 52.4 us  [swapped(): return lax.ppermute(x, 'zh', [(0, 1), (1, 0)])]
    all_to_all x6, waiting for transfers between devices: 29.5 us -> 36.6 us  [spread_out(): return lax.all_to_all(x, XY, 0, 0, tiled=True)]
    ppermute x4, starting transfers between devices: 2.17 us -> 8.56 us  [moved(): return lax.ppermute(x, ('pipe', 'zh'), pairs)]
    pallas_call x13 -> x11, Pallas kernels: 84.3 us -> 78.1 us  [call(): pl.pallas_call(kernel, out_shape=outs, in_specs=ins, out_specs=tuple((VME...]
    pallas_call x0 -> x2, Pallas kernels: none -> 6.03 us  [run_ahead_end(): pl.pallas_call(kernel, grid=(1,), out_shape=shape((TOK, D)), in_specs=[pl...]
  transfers between devices with their start and end apart: 16 -> 16, of which waited for: 7 -> 8; matrix products, arithmetic and copies ran while one was open for 1% -> 1% of each run, Pallas kernels for 24% -> 26%
where the time goes in v4:
time: 290 us; the launch traced here: 289 us
  starting transfers between devices  103 us (36%)
  waiting for transfers between devices  89 us (31%)
  Pallas kernels  86.3 us (30%)
  local copies, waits for them, and re-layouts  4.89 us (2%)
  other arithmetic  4.09 us (1%)
    pallas_call x11, Pallas kernels, call(): pl.pallas_call(kernel, out_shape=outs, in_specs=ins, out_specs=tuple((VME...  78.1 us
    all_to_all x6, starting transfers between devices, spread_out(): return lax.all_to_all(x, XY, 0, 0, tiled=True)  65.4 us
    ppermute x6, waiting for transfers between devices, swapped(): return lax.ppermute(x, 'zh', [(0, 1), (1, 0)])  52.4 us
    all_to_all x6, waiting for transfers between devices, spread_out(): return lax.all_to_all(x, XY, 0, 0, tiled=True)  36.6 us
    ppermute x6, starting transfers between devices, swapped(): return lax.ppermute(x, 'zh', [(0, 1), (1, 0)])  29.2 us
    ppermute x4, starting transfers between devices, moved(): return lax.ppermute(x, ('pipe', 'zh'), pairs)  8.56 us
    pallas_call x2, Pallas kernels, run_ahead_end(): pl.pallas_call(kernel, grid=(1,), out_shape=shape((TOK, D)), in_specs=[pl...  6.03 us
  transfers between devices with their start and end apart: 16, of which 8 were waited for; matrix products, arithmetic and copies ran while one was open for 1% of the time, Pallas kernels for 26%

profile of v4, /device:TPU:1, one launch (start us, length us, event | category | flops | bytes accessed | tf_op | source)
XLA Modules:
  0.0 288.9 jit_solution(9552571575159875074)
XLA Ops:
  4.9 6.6 %shard_map.184 = (bf16[32,216,256]{2,1,0:T(8,128)(2,1)}, bf16[128,2048]{1,0:T(8,128)(2,1)}, bf16[288,128]{1,0:T(8,128)(2,1)}, f32[64,128]{1,0:T(8,128)}, bf16[288,128]{1,0:T(8,128)(2,1)}) custom-call(s32[1]{0:T(128)} %bitcast.zh_ref, s32[4,128]{1,0:T(4,128)} %bitcast.33, s32[4,128]{1,0:T(4,128)} %bitcast.35, bf16[128,2048]{1,0:T(8,128)(2,1)} %bitcast.27, ...), custom_call_target="tpu_custom_call" | custom-call | flops 2000000000 | bytes 8388608 | tf_op jit(solution)/shard_map/pallas_call | solution.py:58
  11.6 8.8 %all-to-all-start = ((bf16[32,216,256]{2,1,0:T(8,128)(2,1)}), bf16[32,216,256]{2,1,0:T(8,128)(2,1)}, u32[]{:S(2)}, u32[]{:S(2)}) async-start(bf16[32,216,256]{2,1,0:T(8,128)(2,1)} %get-tuple-element.34), calls=%async_computation | async-start | bytes 7077888 | tf_op jit(solution)/shard_map/all_to_all | solution.py:37
  20.4 7.0 %collective-permute-start.2 = (bf16[128,2048]{1,0:T(8,128)(2,1)S(1)}, bf16[128,2048]{1,0:T(8,128)(2,1)S(1)}, u32[]{:S(2)}, u32[]{:S(2)}) collective-permute-start(bf16[128,2048]{1,0:T(8,128)(2,1)S(1)} %bitcast.31), channel_id=1, source_target_pairs={{0,8},{8,0},{1,9},{9,1},{2,10},{10,2},{3,11},{11,3},{4,12},{12,4},... | collective-permute-start | bytes 1572872 | tf_op jit(solution)/shard_map/ppermute | solution.py:41
  27.5 5.4 %collective-permute-start = (s32[8,128]{1,0:T(8,128)S(1)}, s32[8,128]{1,0:T(8,128)S(1)}, u32[]{:S(2)}, u32[]{:S(2)}) collective-permute-start(s32[8,128]{1,0:T(8,128)S(1)} %pad_add_fusion), channel_id=1, source_target_pairs={{0,8},{8,0},{1,9},{9,1},{2,10},{10,2},{3,11},{11,3},{4,12},{12,4},... | collective-permute-start | bytes 12296 | tf_op jit(solution)/shard_map/ppermute | solution.py:41
  32.8 23.8 %collective-permute-done = s32[8,128]{1,0:T(8,128)S(1)} collective-permute-done((s32[8,128]{1,0:T(8,128)S(1)}, s32[8,128]{1,0:T(8,128)S(1)}, u32[]{:S(2)}, u32[]{:S(2)}) %collective-permute-start) | collective-permute-done | bytes 4128 | tf_op jit(solution)/shard_map/ppermute | solution.py:41
  58.8 5.1 %shard_map.186 = (bf16[32,144,256]{2,1,0:T(8,128)(2,1)}, bf16[128,2048]{1,0:T(8,128)(2,1)}, bf16[288,128]{1,0:T(8,128)(2,1)}, f32[64,128]{1,0:T(8,128)}) custom-call(s32[1]{0:T(128)} %bitcast.zh_ref, s32[4,128]{1,0:T(4,128)} %get-tuple-element.64.ids_ref, bf16[128,2048]{1,0:T(8,128)(2,1)} %copy-done.2, bf16[128,2048]{1,0:T(8,128)(2,1)} %copy-done.7, ...), custom_call_target="tpu_custom_call" | custom-call | flops 1000000000 | bytes 6291456 | tf_op jit(solution)/shard_map/pallas_call | solution.py:58
  64.3 23.1 %all-to-all-start.1 = ((bf16[32,144,256]{2,1,0:T(8,128)(2,1)}), bf16[32,144,256]{2,1,0:T(8,128)(2,1)}, u32[]{:S(2)}, u32[]{:S(2)}) async-start(bf16[32,144,256]{2,1,0:T(8,128)(2,1)} %get-tuple-element.37), calls=%async_computation.1 | async-start | bytes 4718592 | tf_op jit(solution)/shard_map/all_to_all | solution.py:37
  87.4 6.2 %collective-permute-start.1 = (bf16[128,2048]{1,0:T(8,128)(2,1)S(1)}, bf16[128,2048]{1,0:T(8,128)(2,1)S(1)}, u32[]{:S(2)}, u32[]{:S(2)}) collective-permute-start(bf16[128,2048]{1,0:T(8,128)(2,1)S(1)} %copy-done.6), channel_id=1, source_target_pairs={{0,8},{8,0},{1,9},{9,1},{2,10},{10,2},{3,11},{11,3},{4,12},{12,4},... | collective-permute-start | bytes 1572872 | tf_op jit(solution)/shard_map/ppermute | solution.py:41
  93.6 13.8 %collective-permute-done.1.x_ref = bf16[128,2048]{1,0:T(8,128)(2,1)S(1)} collective-permute-done((bf16[128,2048]{1,0:T(8,128)(2,1)S(1)}, bf16[128,2048]{1,0:T(8,128)(2,1)S(1)}, u32[]{:S(2)}, u32[]{:S(2)}) %collective-permute-start.1) | collective-permute-done | bytes 524320 | tf_op jit(solution)/shard_map/ppermute | solution.py:41
  113.1 5.5 %all-to-all-done.1.got_ref = bf16[32,144,256]{2,1,0:T(8,128)(2,1)} async-done(((bf16[32,144,256]{2,1,0:T(8,128)(2,1)}), bf16[32,144,256]{2,1,0:T(8,128)(2,1)}, u32[]{:S(2)}, u32[]{:S(2)}) %all-to-all-start.1) | async-done | bytes 2359328 | tf_op jit(solution)/shard_map/all_to_all | solution.py:37
  118.6 11.2 %all-to-all-start.2 = ((bf16[32,72,256]{2,1,0:T(8,128)(2,1)}), bf16[32,72,256]{2,1,0:T(8,128)(2,1)}, u32[]{:S(2)}, u32[]{:S(2)}) async-start(bf16[32,72,256]{2,1,0:T(8,128)(2,1)} %get-tuple-element.41), calls=%async_computation.2 | async-start | bytes 2359296 | tf_op jit(solution)/shard_map/all_to_all | solution.py:37
  129.8 15.6 %shard_map.187 = (bf16[32,72,256]{2,1,0:T(8,128)(2,1)}, f32[256,128]{1,0:T(8,128)}) custom-call(bf16[32,216,256]{2,1,0:T(8,128)(2,1)} %all-to-all-done.got_ref.near_ref, bf16[2048,768]{1,0:T(8,128)(2,1)} %bitcast.37, bf16[2048,768]{1,0:T(8,128)(2,1)} %bitcast.40, bf16[768,2048]{1,0:T(8,128)(2,1)} %bitcast.43), custom_call_target="tpu_custom_call" | custom-call | flops 5000000000 | bytes 13631488 | tf_op jit(solution)/shard_map/pallas_call | solution.py:58
  145.5 12.8 %shard_map.188 = bf16[32,152,256]{2,1,0:T(8,128)(2,1)} custom-call(bf16[32,144,256]{2,1,0:T(8,128)(2,1)} %all-to-all-done.1.got_ref, bf16[32,72,256]{2,1,0:T(8,128)(2,1)} %get-tuple-element.39.near_ref, f32[256,128]{1,0:T(8,128)} %get-tuple-element.40.near_small_ref, bf16[2048,768]{1,0:T(8,128)(2,1)} %bitcast.38, bf16[2048,768]{1,0:T(8,128)(2,1)} %bitcast.41, ...), custom_call_target="tpu_custom_call" | custom-call | flops 5000000000 | bytes 15728640 | tf_op jit(solution)/shard_map/pallas_call | solution.py:58
  158.3 7.4 %all-to-all-start.3 = ((bf16[32,152,256]{2,1,0:T(8,128)(2,1)}), bf16[32,152,256]{2,1,0:T(8,128)(2,1)}, u32[]{:S(2)}, u32[]{:S(2)}) async-start(bf16[32,152,256]{2,1,0:T(8,128)(2,1)} %shard_map.188), calls=%async_computation.3 | async-start | bytes 4980736 | tf_op jit(solution)/shard_map/all_to_all | solution.py:37
  165.7 15.8 %shard_map.189 = bf16[32,144,256]{2,1,0:T(8,128)(2,1)} custom-call(bf16[32,216,256]{2,1,0:T(8,128)(2,1)} %all-to-all-done.got_ref.near_ref, bf16[32,72,256]{2,1,0:T(8,128)(2,1)} %all-to-all-done.2.far_ref, bf16[2048,768]{1,0:T(8,128)(2,1)} %bitcast.39, bf16[2048,768]{1,0:T(8,128)(2,1)} %bitcast.42, bf16[768,2048]{1,0:T(8,128)(2,1)} %bitcast.45), custom_call_target="tpu_custom_call" | custom-call | flops 6000000000 | bytes 14680064 | tf_op jit(solution)/shard_map/pallas_call | solution.py:58
  181.6 16.8 %all-to-all-done.3.home_ref = bf16[32,152,256]{2,1,0:T(8,128)(2,1)} async-done(((bf16[32,152,256]{2,1,0:T(8,128)(2,1)}), bf16[32,152,256]{2,1,0:T(8,128)(2,1)}, u32[]{:S(2)}, u32[]{:S(2)}) %all-to-all-start.3) | async-done | bytes 2490400 | tf_op jit(solution)/shard_map/all_to_all | solution.py:37
  198.4 5.2 %all-to-all-start.4 = ((bf16[32,144,256]{2,1,0:T(8,128)(2,1)}), bf16[32,144,256]{2,1,0:T(8,128)(2,1)}, u32[]{:S(2)}, u32[]{:S(2)}) async-start(bf16[32,144,256]{2,1,0:T(8,128)(2,1)} %shard_map.189), calls=%async_computation.4 | async-start | bytes 4718592 | tf_op jit(solution)/shard_map/all_to_all | solution.py:37
  205.8 6.1 %collective-permute-start.6 = (f32[64,256]{1,0:T(8,128)}, f32[64,256]{1,0:T(8,128)S(1)}, u32[]{:S(2)}, u32[]{:S(2)}) collective-permute-start(f32[64,256]{1,0:T(8,128)} %shard_map.192.near_note_ref), channel_id=1, source_target_pairs={{0,8},{8,0},{1,9},{9,1},{2,10},{10,2},{3,11},{11,3},{4,12},{12,4},... | collective-permute-start | bytes 196616 | tf_op jit(solution)/shard_map/ppermute | solution.py:41
  211.9 5.7 %shard_map.193 = (f32[128,2048]{1,0:T(8,128)}, bf16[128,2048]{1,0:T(8,128)(2,1)}, f32[8,256]{1,0:T(8,128)}, f32[8,256]{1,0:T(8,128)}) custom-call(s32[1]{0:T(128)} %bitcast.zh_ref, bf16[32,152,256]{2,1,0:T(8,128)(2,1)} %all-to-all-done.3.home_ref, bf16[288,128]{1,0:T(8,128)(2,1)} %get-tuple-element.48.near_hot_ref, ...), custom_call_target="tpu_custom_call" | custom-call | flops 1000000000 | bytes 6291456 | tf_op jit(solution)/shard_map/pallas_call | solution.py:58
  227.9 7.0 %all-to-all-done.4.home_ref = bf16[32,144,256]{2,1,0:T(8,128)(2,1)} async-done(((bf16[32,144,256]{2,1,0:T(8,128)(2,1)}), bf16[32,144,256]{2,1,0:T(8,128)(2,1)}, u32[]{:S(2)}, u32[]{:S(2)}) %all-to-all-start.4) | async-done | bytes 2359328 | tf_op jit(solution)/shard_map/all_to_all | solution.py:37
  241.6 5.8 %collective-permute-start.4 = (bf16[128,2048]{1,0:T(8,128)(2,1)}, bf16[128,2048]{1,0:T(8,128)(2,1)}, u32[]{:S(2)}, u32[]{:S(2)}) collective-permute-start(bf16[128,2048]{1,0:T(8,128)(2,1)} %shard_map.190), channel_id=1, source_target_pairs={{0,64},{8,72},{64,128},{72,136},{128,192},{136,200},{192,0},{200,8... | collective-permute-start | bytes 1572872 | tf_op jit(solution)/shard_map/ppermute | solution.py:50
  247.4 14.8 %collective-permute-done.9.theirs_ref = f32[8,256]{1,0:T(8,128)S(1)} collective-permute-done((f32[8,256]{1,0:T(8,128)S(1)}, f32[8,256]{1,0:T(8,128)S(1)}, u32[]{:S(2)}, u32[]{:S(2)}) %collective-permute-start.9) | collective-permute-done | bytes 8224 | tf_op jit(solution)/shard_map/ppermute | solution.py:41
  265.9 9.7 %all-to-all-start.5 = ((bf16[32,32,128]{2,1,0:T(8,128)(2,1)}), bf16[32,32,128]{2,1,0:T(8,128)(2,1)S(1)}, u32[]{:S(2)}, u32[]{:S(2)}) async-start(bf16[32,32,128]{2,1,0:T(8,128)(2,1)} %bitcast.32), calls=%async_computation.5 | async-start | bytes 524288 | tf_op jit(solution)/shard_map/all_to_all | solution.py:37
  277.5 7.0 %all-to-all-done.5.got_ref = bf16[32,32,128]{2,1,0:T(8,128)(2,1)S(1)} async-done(((bf16[32,32,128]{2,1,0:T(8,128)(2,1)}), bf16[32,32,128]{2,1,0:T(8,128)(2,1)S(1)}, u32[]{:S(2)}, u32[]{:S(2)}) %all-to-all-start.5) | async-done | bytes 262176 | tf_op jit(solution)/shard_map/all_to_all | solution.py:37
  (50 shorter events, 41.2 us)
Async XLA Ops:
  11.5 8.8 %copy-start.1 = (bf16[1,128,2048]{2,1,0:T(8,128)(2,1)S(1)}, bf16[1,128,2048]{2,1,0:T(8,128)(2,1)}, u32[]{:S(2)}) copy-start(bf16[1,128,2048]{2,1,0:T(8,128)(2,1)} %param.29) | copy-start | bytes 1572868
  11.6 15.8 %copy-start.5 = (bf16[1,128,2048]{2,1,0:T(8,128)(2,1)S(1)}, bf16[1,128,2048]{2,1,0:T(8,128)(2,1)}, u32[]{:S(2)}) copy-start(bf16[1,128,2048]{2,1,0:T(8,128)(2,1)} %param.31) | copy-start | bytes 1572868
  11.6 15.9 %copy-start.3 = (s32[1,128,4]{1,2,0:T(4,128)S(1)}, s32[1,128,4]{1,2,0:T(4,128)}, u32[]{:S(2)}) copy-start(s32[1,128,4]{1,2,0:T(4,128)} %param.30) | copy-start | bytes 6148
  11.6 15.9 %copy-start.4 = (s32[1,128,4]{1,2,0:T(4,128)S(1)}, s32[1,128,4]{1,2,0:T(4,128)}, u32[]{:S(2)}) copy-start(s32[1,128,4]{1,2,0:T(4,128)} %param.28) | copy-start | bytes 6148
  11.6 52.7 %all-to-all-start = ((bf16[32,216,256]{2,1,0:T(8,128)(2,1)}), bf16[32,216,256]{2,1,0:T(8,128)(2,1)}, u32[]{:S(2)}, u32[]{:S(2)}) async-start(bf16[32,216,256]{2,1,0:T(8,128)(2,1)} %get-tuple-element.34), calls=%async_computation | async-start | bytes 7077888 | tf_op jit(solution)/shard_map/all_to_all | solution.py:37
  20.4 36.9 %collective-permute-start.2 = (bf16[128,2048]{1,0:T(8,128)(2,1)S(1)}, bf16[128,2048]{1,0:T(8,128)(2,1)S(1)}, u32[]{:S(2)}, u32[]{:S(2)}) collective-permute-start(bf16[128,2048]{1,0:T(8,128)(2,1)S(1)} %bitcast.31), channel_id=1, source_target_pairs={{0,8},{8,0},{1,9},{9,1},{2,10},{10,2},{3,11},{11,3},{4,12},{12,4},... | collective-permute-start | bytes 1572872 | tf_op jit(solution)/shard_map/ppermute | solution.py:41
  27.4 30.7 %collective-permute-start.3 = (bf16[128,2048]{1,0:T(8,128)(2,1)S(1)}, bf16[128,2048]{1,0:T(8,128)(2,1)S(1)}, u32[]{:S(2)}, u32[]{:S(2)}) collective-permute-start(bf16[128,2048]{1,0:T(8,128)(2,1)S(1)} %bitcast.50), channel_id=1, source_target_pairs={{0,8},{8,0},{1,9},{9,1},{2,10},{10,2},{3,11},{11,3},{4,12},{12,4},... | collective-permute-start | bytes 1572872 | tf_op jit(solution)/shard_map/ppermute | solution.py:41
  27.5 29.2 %collective-permute-start = (s32[8,128]{1,0:T(8,128)S(1)}, s32[8,128]{1,0:T(8,128)S(1)}, u32[]{:S(2)}, u32[]{:S(2)}) collective-permute-start(s32[8,128]{1,0:T(8,128)S(1)} %pad_add_fusion), channel_id=1, source_target_pairs={{0,8},{8,0},{1,9},{9,1},{2,10},{10,2},{3,11},{11,3},{4,12},{12,4},... | collective-permute-start | bytes 12296 | tf_op jit(solution)/shard_map/ppermute | solution.py:41
  58.0 0.8 copy-start.7
  63.9 23.5 %copy-start.6 = (bf16[128,2048]{1,0:T(8,128)(2,1)S(1)}, bf16[128,2048]{1,0:T(8,128)(2,1)}, u32[]{:S(2)}) copy-start(bf16[128,2048]{1,0:T(8,128)(2,1)} %shard_map.183.resid_ref) | copy-start | bytes 1572868
  64.3 54.3 %all-to-all-start.1 = ((bf16[32,144,256]{2,1,0:T(8,128)(2,1)}), bf16[32,144,256]{2,1,0:T(8,128)(2,1)}, u32[]{:S(2)}, u32[]{:S(2)}) async-start(bf16[32,144,256]{2,1,0:T(8,128)(2,1)} %get-tuple-element.37), calls=%async_computation.1 | async-start | bytes 4718592 | tf_op jit(solution)/shard_map/all_to_all | solution.py:37
  87.4 20.0 %collective-permute-start.1 = (bf16[128,2048]{1,0:T(8,128)(2,1)S(1)}, bf16[128,2048]{1,0:T(8,128)(2,1)S(1)}, u32[]{:S(2)}, u32[]{:S(2)}) collective-permute-start(bf16[128,2048]{1,0:T(8,128)(2,1)S(1)} %copy-done.6), channel_id=1, source_target_pairs={{0,8},{8,0},{1,9},{9,1},{2,10},{10,2},{3,11},{11,3},{4,12},{12,4},... | collective-permute-start | bytes 1572872 | tf_op jit(solution)/shard_map/ppermute | solution.py:41
  107.4 0.8 copy-start.8
  118.6 39.7 %all-to-all-start.2 = ((bf16[32,72,256]{2,1,0:T(8,128)(2,1)}), bf16[32,72,256]{2,1,0:T(8,128)(2,1)}, u32[]{:S(2)}, u32[]{:S(2)}) async-start(bf16[32,72,256]{2,1,0:T(8,128)(2,1)} %get-tuple-element.41), calls=%async_computation.2 | async-start | bytes 2359296 | tf_op jit(solution)/shard_map/all_to_all | solution.py:37
  158.3 40.1 %all-to-all-start.3 = ((bf16[32,152,256]{2,1,0:T(8,128)(2,1)}), bf16[32,152,256]{2,1,0:T(8,128)(2,1)}, u32[]{:S(2)}, u32[]{:S(2)}) async-start(bf16[32,152,256]{2,1,0:T(8,128)(2,1)} %shard_map.188), calls=%async_computation.3 | async-start | bytes 4980736 | tf_op jit(solution)/shard_map/all_to_all | solution.py:37
  198.4 36.6 %all-to-all-start.4 = ((bf16[32,144,256]{2,1,0:T(8,128)(2,1)}), bf16[32,144,256]{2,1,0:T(8,128)(2,1)}, u32[]{:S(2)}, u32[]{:S(2)}) async-start(bf16[32,144,256]{2,1,0:T(8,128)(2,1)} %shard_map.189), calls=%async_computation.4 | async-start | bytes 4718592 | tf_op jit(solution)/shard_map/all_to_all | solution.py:37
  205.8 11.9 %collective-permute-start.6 = (f32[64,256]{1,0:T(8,128)}, f32[64,256]{1,0:T(8,128)S(1)}, u32[]{:S(2)}, u32[]{:S(2)}) collective-permute-start(f32[64,256]{1,0:T(8,128)} %shard_map.192.near_note_ref), channel_id=1, source_target_pairs={{0,8},{8,0},{1,9},{9,1},{2,10},{10,2},{3,11},{11,3},{4,12},{12,4},... | collective-permute-start | bytes 196616 | tf_op jit(solution)/shard_map/ppermute | solution.py:41
  217.6 5.9 %copy-start.10 = (f32[8,256]{1,0:T(8,128)S(1)}, f32[8,256]{1,0:T(8,128)}, u32[]{:S(2)}) copy-start(f32[8,256]{1,0:T(8,128)} %get-tuple-element.58) | copy-start | bytes 24580
  217.6 57.9 %collective-permute-start.8 = (bf16[128,2048]{1,0:T(8,128)(2,1)}, bf16[128,2048]{1,0:T(8,128)(2,1)S(1)}, u32[]{:S(2)}, u32[]{:S(2)}) collective-permute-start(bf16[128,2048]{1,0:T(8,128)(2,1)} %get-tuple-element.54), channel_id=1, source_target_pairs={{0,200},{8,192},{64,8},{72,0},{128,72},{136,64},{192,136},{200,128... | collective-permute-start | bytes 1572872 | tf_op jit(solution)/shard_map/ppermute | solution.py:50
  221.4 54.1 %collective-permute-start.7 = (bf16[128,2048]{1,0:T(8,128)(2,1)}, bf16[128,2048]{1,0:T(8,128)(2,1)}, u32[]{:S(2)}, u32[]{:S(2)}) collective-permute-start(bf16[128,2048]{1,0:T(8,128)(2,1)} %get-tuple-element.53), channel_id=1, source_target_pairs={{0,192},{8,200},{64,0},{72,8},{128,64},{136,72},{192,128},{200,136... | collective-permute-start | bytes 1572872 | tf_op jit(solution)/shard_map/ppermute | solution.py:50
  223.6 38.6 %collective-permute-start.9 = (f32[8,256]{1,0:T(8,128)S(1)}, f32[8,256]{1,0:T(8,128)S(1)}, u32[]{:S(2)}, u32[]{:S(2)}) collective-permute-start(f32[8,256]{1,0:T(8,128)S(1)} %copy-done.10), channel_id=1, source_target_pairs={{0,8},{8,0},{1,9},{9,1},{2,10},{10,2},{3,11},{11,3},{4,12},{12,4},... | collective-permute-start | bytes 24584 | tf_op jit(solution)/shard_map/ppermute | solution.py:41
  237.9 48.9 %collective-permute-start.5 = (bf16[128,2048]{1,0:T(8,128)(2,1)}, bf16[128,2048]{1,0:T(8,128)(2,1)}, u32[]{:S(2)}, u32[]{:S(2)}) collective-permute-start(bf16[128,2048]{1,0:T(8,128)(2,1)} %shard_map.191), channel_id=1, source_target_pairs={{0,72},{8,64},{64,136},{72,128},{128,200},{136,192},{192,8},{200,0... | collective-permute-start | bytes 1572872 | tf_op jit(solution)/shard_map/ppermute | solution.py:50
  241.6 45.2 %collective-permute-start.4 = (bf16[128,2048]{1,0:T(8,128)(2,1)}, bf16[128,2048]{1,0:T(8,128)(2,1)}, u32[]{:S(2)}, u32[]{:S(2)}) collective-permute-start(bf16[128,2048]{1,0:T(8,128)(2,1)} %shard_map.190), channel_id=1, source_target_pairs={{0,64},{8,72},{64,128},{72,136},{128,192},{136,200},{192,0},{200,8... | collective-permute-start | bytes 1572872 | tf_op jit(solution)/shard_map/ppermute | solution.py:50
  265.9 18.6 %all-to-all-start.5 = ((bf16[32,32,128]{2,1,0:T(8,128)(2,1)}), bf16[32,32,128]{2,1,0:T(8,128)(2,1)S(1)}, u32[]{:S(2)}, u32[]{:S(2)}) async-start(bf16[32,32,128]{2,1,0:T(8,128)(2,1)} %bitcast.32), calls=%async_computation.5 | async-start | bytes 524288 | tf_op jit(solution)/shard_map/all_to_all | solution.py:37
  (4 other events, 2.7 us)

commit v5 on v2

--- a/solution.py
+++ b/solution.py
@@ -444,15 +444,18 @@
     hidden_ref[...] = (gate_pre / (1.0 + jnp.exp(-gate_pre)) * up_sum[...]).astype(bf16)
     copies[2].wait()
 
-    def outward(j):
-        put_rows(wide_ref, j, dot(hidden_ref[...], down_ref[:, columns(j, 256)]))
-
-    loop(8, outward)
+    def outward(c):
+        for part in range(2):
+            made = dot(hidden_ref[...], down_ref[:, columns(part * 4 + c, 256)])
+            for i in range(2):
+                wide_ref[part, pl.ds(2 * c + i, count, stride=8), :] = made[:, i * 128 : i * 128 + 128]
+
+    loop(4, outward)
 
     def put(d, rows):
-        for lane in range(2):
-            first_ref[d, :, LANES[lane]] = wide_ref[lane, area_rows(d, 1), :].astype(bf16)
-            second_ref[d, :, LANES[lane]] = wide_ref[lane, area_rows(d, 0), :].astype(bf16)
+        for half in range(2):
+            first_ref[d, pl.ds(half * ROWS, ROWS), :] = wide_ref[0, area_rows(d, half), :].astype(bf16)
+            second_ref[d, pl.ds(half * ROWS, ROWS), :] = wide_ref[1, area_rows(d, half), :].astype(bf16)
 
     each_peer(put)
 
@@ -460,7 +463,7 @@
 def run_ahead_experts(*args):
     return call(
         ahead_experts,
-        (shape((PEERS, ROWS, 256)), shape((PEERS, ROWS, 256))),
+        (shape((PEERS, 2 * ROWS, 128)), shape((PEERS, 2 * ROWS, 128))),
         [VMEM] * 2 + [HBM] * 3,
         [pltpu.VMEM((2, 2 * AREA, 128), f32)]
         + WEIGHTS
@@ -636,30 +639,46 @@
     return call(share_parts, (shape((D // 2, 128)),), [SMEM] + [VMEM] * 9, [], args, 10**9, 3)[0]
 
 
-def ahead_sums(home_ref, mix_ref, wide_ref):
+def ahead_end(home_ref, near_mix_ref, far_mix_ref, resid_ref, near_ref, far_ref, wide_ref):
     def take(d, rows):
-        for lane in range(2):
-            wide_ref[lane, rows, :] = home_ref[d, :, LANES[lane]].astype(f32)
+        for half in range(2):
+            wide_ref[0, area_rows(d, half), :] = home_ref[d, pl.ds(half * ROWS, ROWS), :].astype(f32)
 
     each_peer(take)
-    for j in range(8):
-        yield pl.ds(j * 256, 256), dot(mix_ref[...], get_rows(wide_ref, j, SLOTS), DOWN)
-
-
-def ahead_far(home_ref, mix_ref, out_ref, wide_ref):
-    for cols, sums in ahead_sums(home_ref, mix_ref, wide_ref):
-        out_ref[:, cols] = sums.astype(bf16)
-
-
-def ahead_near(home_ref, mix_ref, resid_ref, out_ref, wide_ref):
-    for cols, sums in ahead_sums(home_ref, mix_ref, wide_ref):
-        out_ref[:, cols] = (resid_ref[:, cols].astype(f32) + sums).astype(bf16)
-
-
-def run_ahead_end(kernel, *args):
-    return call(
-        kernel, (shape((TOK, D)),), [VMEM] * len(args), [pltpu.VMEM((2, AREA, 128), f32)], args, 10**9, 3
-    )[0]
+    for c in range(4):
+        cols = pl.ds(c * 256, 256)
+        for half, (mix_ref, out_ref) in enumerate(((near_mix_ref, near_ref), (far_mix_ref, far_ref))):
+            rows = jnp.concatenate([get_rows(wide_ref, 2 * c + i, SLOTS, half * AREA) for i in range(2)], axis=1)
+            sums = dot(mix_ref[...], rows, DOWN)
+            if half == 0:
+                sums = sums + resid_ref[:, cols].astype(f32)
+            out_ref[:, cols] = sums.astype(bf16)
+
+
+def run_ahead_end(home, near_mix, far_mix, resid, part):
+    columns = pl.BlockSpec((TOK, D // 2), lambda i: (0, part))
+    whole = [pl.BlockSpec(a.shape, lambda i, n=a.ndim: (0,) * n) for a in (home, near_mix, far_mix)]
+    half = pl.BlockSpec((TOK, D // 2), lambda i: (0, 0))
+    return pl.pallas_call(
+        ahead_end,
+        grid=(1,),
+        out_shape=(shape((TOK, D // 2)), shape((TOK, D // 2))),
+        in_specs=whole + [columns],
+        out_specs=(half, half),
+        scratch_shapes=[pltpu.VMEM((1, 2 * AREA, 128), f32)],
+        compiler_params=pltpu.CompilerParams(vmem_limit_bytes=63 * 2**20),
+        cost_estimate=pl.CostEstimate(flops=10**9, transcendentals=0, bytes_accessed=3 * 2**20),
+    )(home, near_mix, far_mix, resid)
+
+
+def final_add(a_ref, b_ref, c_ref, d_ref, out_ref):
+    half = D // 2
+    out_ref[:, pl.ds(0, half)] = (a_ref[...].astype(f32) + b_ref[...].astype(f32)).astype(bf16)
+    out_ref[:, pl.ds(half, half)] = (c_ref[...].astype(f32) + d_ref[...].astype(f32)).astype(bf16)
+
+
+def run_final_add(*args):
+    return call(final_add, (shape((TOK, D)),), [VMEM] * 4, [], args, 10**6, 2)[0]
 
 
 def share_sums(got_ref, router_ref, gain_ref):
@@ -731,6 +750,8 @@
     made_1, made_2 = run_ahead_experts(got_1, got_3, *weights)
     made_1, home_b = lax.optimization_barrier((made_1, home_b))
     home_1 = spread_out(made_1)
+    made_2, home_1 = lax.optimization_barrier((made_2, home_1))
+    home_2 = spread_out(made_2)
     note = run_behind_note(zh, home_b, hot_b, hot_c)
     far_note = swapped(note)
     sums_b, own_c, theirs, mine = run_behind_sums(
@@ -741,21 +762,21 @@
         note, far_note, sums_b, probs_b, probs_c, back_x, back_g, gain, table
     )
     moved_b = moved(own_b, True, -1)
-    made_2, home_1 = lax.optimization_barrier((made_2, home_1))
-    home_2 = spread_out(made_2)
-    own_h = run_ahead_end(ahead_far, home_1, mix_h)
-    moved_h = moved(own_h, False, 1)
+    own_f1, own_h1 = run_ahead_end(home_1, mix_f, mix_h, resid, 0)
+    moved_h1 = moved(own_h1, False, 1)
+    moved_f1 = moved(own_f1, True, 1)
     theirs = swapped(theirs)
     shares = run_share_parts(
         zh, logit_b, logit_c, mine, theirs, normed_b, normed_c, back_x, x_far, table
     )
-    own_f = run_ahead_end(ahead_near, home_2, mix_f, resid)
-    moved_f = moved(own_f, True, 1)
-    shares, own_f = lax.optimization_barrier((shares, own_f))
+    own_f2, own_h2 = run_ahead_end(home_2, mix_f, mix_h, resid, 1)
+    moved_h2 = moved(own_h2, False, 1)
+    moved_f2 = moved(own_f2, True, 1)
+    shares, own_f2 = lax.optimization_barrier((shares, own_f2))
     got_s = spread_out(shares.reshape(PEERS, PEERS, 128))
     router_grad, gain_grad = run_share_sums(got_s)
     input_grad = (moved_b.astype(f32) + moved_c.astype(f32)).astype(bf16)
-    forward_output = (moved_f.astype(f32) + moved_h.astype(f32)).astype(bf16)
+    forward_output = run_final_add(moved_f1, moved_h1, moved_f2, moved_h2)
     return forward_output[None], input_grad[None], router_grad[None], gain_grad
 
 

time: 314 us -> 337 us (1.073)
  waiting for transfers between devices: 95.2 us -> 113 us
  starting transfers between devices: 96.3 us -> 103 us
    ppermute x4 -> x6, waiting for transfers between devices: 0.01 us -> 17.6 us  [moved(): return lax.ppermute(x, ('pipe', 'zh'), pairs)]
    ppermute x4 -> x6, starting transfers between devices: 2.17 us -> 9.91 us  [moved(): return lax.ppermute(x, ('pipe', 'zh'), pairs)]
    all_to_all x6, waiting for transfers between devices: 29.5 us -> 23.4 us  [spread_out(): return lax.all_to_all(x, XY, 0, 0, tiled=True)]
    pallas_call x0 -> x2, Pallas kernels: none -> 5.95 us  [run_ahead_end(): pl.pallas_call(ahead_end, grid=(1,), out_shape=(shape((TOK, D // 2)), sha...]
    ppermute x6, waiting for transfers between devices: 65.8 us -> 71.6 us  [swapped(): return lax.ppermute(x, 'zh', [(0, 1), (1, 0)])]
    pallas_call x13 -> x12, Pallas kernels: 84.3 us -> 79.4 us  [call(): pl.pallas_call(kernel, out_shape=outs, in_specs=ins, out_specs=tuple((VME...]
  transfers between devices with their start and end apart: 16 -> 18, of which waited for: 7 -> 7; matrix products, arithmetic and copies ran while one was open for 1% -> 1% of each run, Pallas kernels for 24% -> 22%
where the time goes in v5:
time: 337 us; the launch traced here: 336 us
  waiting for transfers between devices  113 us (34%)
  starting transfers between devices  103 us (31%)
  Pallas kernels  87.6 us (26%)
  blocking collectives  24.2 us (7%)
  local copies, waits for them, and re-layouts  4.96 us (1%)
    pallas_call x12, Pallas kernels, call(): pl.pallas_call(kernel, out_shape=outs, in_specs=ins, out_specs=tuple((VME...  79.4 us
    ppermute x6, waiting for transfers between devices, swapped(): return lax.ppermute(x, 'zh', [(0, 1), (1, 0)])  71.6 us
    all_to_all x6, starting transfers between devices, spread_out(): return lax.all_to_all(x, XY, 0, 0, tiled=True)  64.1 us
    ppermute x6, starting transfers between devices, swapped(): return lax.ppermute(x, 'zh', [(0, 1), (1, 0)])  29.2 us
    all_to_all x1, blocking collectives, spread_out(): return lax.all_to_all(x, XY, 0, 0, tiled=True)  24.2 us
    all_to_all x6, waiting for transfers between devices, spread_out(): return lax.all_to_all(x, XY, 0, 0, tiled=True)  23.4 us
    ppermute x6, waiting for transfers between devices, moved(): return lax.ppermute(x, ('pipe', 'zh'), pairs)  17.6 us
    ppermute x6, starting transfers between devices, moved(): return lax.ppermute(x, ('pipe', 'zh'), pairs)  9.91 us
  transfers between devices with their start and end apart: 18, of which 7 were waited for; matrix products, arithmetic and copies ran while one was open for 1% of the time, Pallas kernels for 22%

profile of v5, /device:TPU:1, one launch (start us, length us, event | category | flops | bytes accessed | tf_op | source)
XLA Modules:
  0.0 335.9 jit_solution(147541440641917577)
XLA Ops:
  4.9 6.6 %shard_map.184 = (bf16[32,216,256]{2,1,0:T(8,128)(2,1)}, bf16[128,2048]{1,0:T(8,128)(2,1)}, bf16[288,128]{1,0:T(8,128)(2,1)}, f32[64,128]{1,0:T(8,128)}, bf16[288,128]{1,0:T(8,128)(2,1)}) custom-call(s32[1]{0:T(128)} %bitcast.zh_ref, s32[4,128]{1,0:T(4,128)} %bitcast.33, s32[4,128]{1,0:T(4,128)} %bitcast.35, bf16[128,2048]{1,0:T(8,128)(2,1)} %bitcast.27, ...), custom_call_target="tpu_custom_call" | custom-call | flops 2000000000 | bytes 8388608 | tf_op jit(solution)/shard_map/pallas_call | solution.py:58
  11.6 8.8 %all-to-all-start = ((bf16[32,216,256]{2,1,0:T(8,128)(2,1)}), bf16[32,216,256]{2,1,0:T(8,128)(2,1)}, u32[]{:S(2)}, u32[]{:S(2)}) async-start(bf16[32,216,256]{2,1,0:T(8,128)(2,1)} %get-tuple-element.42), calls=%async_computation | async-start | bytes 7077888 | tf_op jit(solution)/shard_map/all_to_all | solution.py:37
  20.3 7.0 %collective-permute-start.2 = (bf16[128,2048]{1,0:T(8,128)(2,1)S(1)}, bf16[128,2048]{1,0:T(8,128)(2,1)S(1)}, u32[]{:S(2)}, u32[]{:S(2)}) collective-permute-start(bf16[128,2048]{1,0:T(8,128)(2,1)S(1)} %bitcast.31), channel_id=1, source_target_pairs={{0,8},{8,0},{1,9},{9,1},{2,10},{10,2},{3,11},{11,3},{4,12},{12,4},... | collective-permute-start | bytes 1572872 | tf_op jit(solution)/shard_map/ppermute | solution.py:41
  27.5 5.4 %collective-permute-start = (s32[8,128]{1,0:T(8,128)S(1)}, s32[8,128]{1,0:T(8,128)S(1)}, u32[]{:S(2)}, u32[]{:S(2)}) collective-permute-start(s32[8,128]{1,0:T(8,128)S(1)} %pad_add_fusion), channel_id=1, source_target_pairs={{0,8},{8,0},{1,9},{9,1},{2,10},{10,2},{3,11},{11,3},{4,12},{12,4},... | collective-permute-start | bytes 12296 | tf_op jit(solution)/shard_map/ppermute | solution.py:41
  32.8 23.8 %collective-permute-done = s32[8,128]{1,0:T(8,128)S(1)} collective-permute-done((s32[8,128]{1,0:T(8,128)S(1)}, s32[8,128]{1,0:T(8,128)S(1)}, u32[]{:S(2)}, u32[]{:S(2)}) %collective-permute-start) | collective-permute-done | bytes 4128 | tf_op jit(solution)/shard_map/ppermute | solution.py:41
  58.8 5.2 %shard_map.186 = (bf16[32,144,256]{2,1,0:T(8,128)(2,1)}, bf16[128,2048]{1,0:T(8,128)(2,1)}, bf16[288,128]{1,0:T(8,128)(2,1)}, f32[64,128]{1,0:T(8,128)}) custom-call(s32[1]{0:T(128)} %bitcast.zh_ref, s32[4,128]{1,0:T(4,128)} %get-tuple-element.80.ids_ref, bf16[128,2048]{1,0:T(8,128)(2,1)} %copy-done.2, bf16[128,2048]{1,0:T(8,128)(2,1)} %copy-done.7, ...), custom_call_target="tpu_custom_call" | custom-call | flops 1000000000 | bytes 6291456 | tf_op jit(solution)/shard_map/pallas_call | solution.py:58
  64.3 23.2 %all-to-all-start.1 = ((bf16[32,144,256]{2,1,0:T(8,128)(2,1)}), bf16[32,144,256]{2,1,0:T(8,128)(2,1)}, u32[]{:S(2)}, u32[]{:S(2)}) async-start(bf16[32,144,256]{2,1,0:T(8,128)(2,1)} %get-tuple-element.45), calls=%async_computation.1 | async-start | bytes 4718592 | tf_op jit(solution)/shard_map/all_to_all | solution.py:37
  87.5 6.2 %collective-permute-start.1 = (bf16[128,2048]{1,0:T(8,128)(2,1)S(1)}, bf16[128,2048]{1,0:T(8,128)(2,1)S(1)}, u32[]{:S(2)}, u32[]{:S(2)}) collective-permute-start(bf16[128,2048]{1,0:T(8,128)(2,1)S(1)} %copy-done.6), channel_id=1, source_target_pairs={{0,8},{8,0},{1,9},{9,1},{2,10},{10,2},{3,11},{11,3},{4,12},{12,4},... | collective-permute-start | bytes 1572872 | tf_op jit(solution)/shard_map/ppermute | solution.py:41
  93.7 13.8 %collective-permute-done.1.x_ref = bf16[128,2048]{1,0:T(8,128)(2,1)S(1)} collective-permute-done((bf16[128,2048]{1,0:T(8,128)(2,1)S(1)}, bf16[128,2048]{1,0:T(8,128)(2,1)S(1)}, u32[]{:S(2)}, u32[]{:S(2)}) %collective-permute-start.1) | collective-permute-done | bytes 524320 | tf_op jit(solution)/shard_map/ppermute | solution.py:41
  108.3 5.0 %shard_map.185 = (bf16[32,72,256]{2,1,0:T(8,128)(2,1)}, bf16[288,128]{1,0:T(8,128)(2,1)}) custom-call(s32[1]{0:T(128)} %bitcast.zh_ref, s32[4,128]{1,0:T(4,128)} %get-tuple-element.81.ids_ref, bf16[128,2048]{1,0:T(8,128)(2,1)} %copy-done.8, f32[1,2048]{1,0:T(1,128)} %gain_ref.9, bf16[64,2048]{1,0:T(8,128)(2,1)} %bitcast.53), custom_call_target="tpu_custom_call" | custom-call | flops 1000000000 | bytes 4194304 | tf_op jit(solution)/shard_map/pallas_call | solution.py:58
  113.2 5.5 %all-to-all-done.1.got_ref = bf16[32,144,256]{2,1,0:T(8,128)(2,1)} async-done(((bf16[32,144,256]{2,1,0:T(8,128)(2,1)}), bf16[32,144,256]{2,1,0:T(8,128)(2,1)}, u32[]{:S(2)}, u32[]{:S(2)}) %all-to-all-start.1) | async-done | bytes 2359328 | tf_op jit(solution)/shard_map/all_to_all | solution.py:37
  118.7 11.2 %all-to-all-start.2 = ((bf16[32,72,256]{2,1,0:T(8,128)(2,1)}), bf16[32,72,256]{2,1,0:T(8,128)(2,1)}, u32[]{:S(2)}, u32[]{:S(2)}) async-start(bf16[32,72,256]{2,1,0:T(8,128)(2,1)} %get-tuple-element.49), calls=%async_computation.2 | async-start | bytes 2359296 | tf_op jit(solution)/shard_map/all_to_all | solution.py:37
  129.9 15.7 %shard_map.187 = (bf16[32,72,256]{2,1,0:T(8,128)(2,1)}, f32[256,128]{1,0:T(8,128)}) custom-call(bf16[32,216,256]{2,1,0:T(8,128)(2,1)} %all-to-all-done.got_ref.near_ref, bf16[2048,768]{1,0:T(8,128)(2,1)} %bitcast.37, bf16[2048,768]{1,0:T(8,128)(2,1)} %bitcast.40, bf16[768,2048]{1,0:T(8,128)(2,1)} %bitcast.43), custom_call_target="tpu_custom_call" | custom-call | flops 5000000000 | bytes 13631488 | tf_op jit(solution)/shard_map/pallas_call | solution.py:58
  145.6 12.7 %shard_map.188 = bf16[32,152,256]{2,1,0:T(8,128)(2,1)} custom-call(bf16[32,144,256]{2,1,0:T(8,128)(2,1)} %all-to-all-done.1.got_ref, bf16[32,72,256]{2,1,0:T(8,128)(2,1)} %get-tuple-element.47.near_ref, f32[256,128]{1,0:T(8,128)} %get-tuple-element.48.near_small_ref, bf16[2048,768]{1,0:T(8,128)(2,1)} %bitcast.38, bf16[2048,768]{1,0:T(8,128)(2,1)} %bitcast.41, ...), custom_call_target="tpu_custom_call" | custom-call | flops 5000000000 | bytes 15728640 | tf_op jit(solution)/shard_map/pallas_call | solution.py:58
  158.4 7.4 %all-to-all-start.3 = ((bf16[32,152,256]{2,1,0:T(8,128)(2,1)}), bf16[32,152,256]{2,1,0:T(8,128)(2,1)}, u32[]{:S(2)}, u32[]{:S(2)}) async-start(bf16[32,152,256]{2,1,0:T(8,128)(2,1)} %shard_map.188), calls=%async_computation.3 | async-start | bytes 4980736 | tf_op jit(solution)/shard_map/all_to_all | solution.py:37
  165.8 14.9 %shard_map.189 = (bf16[32,144,128]{2,1,0:T(8,128)(2,1)}, bf16[32,144,128]{2,1,0:T(8,128)(2,1)}) custom-call(bf16[32,216,256]{2,1,0:T(8,128)(2,1)} %all-to-all-done.got_ref.near_ref, bf16[32,72,256]{2,1,0:T(8,128)(2,1)} %all-to-all-done.2.far_ref, bf16[2048,768]{1,0:T(8,128)(2,1)} %bitcast.39, bf16[2048,768]{1,0:T(8,128)(2,1)} %bitcast.42, ...), custom_call_target="tpu_custom_call" | custom-call | flops 6000000000 | bytes 14680064 | tf_op jit(solution)/shard_map/pallas_call | solution.py:58
  180.8 17.7 %all-to-all-done.3.home_ref = bf16[32,152,256]{2,1,0:T(8,128)(2,1)} async-done(((bf16[32,152,256]{2,1,0:T(8,128)(2,1)}), bf16[32,152,256]{2,1,0:T(8,128)(2,1)}, u32[]{:S(2)}, u32[]{:S(2)}) %all-to-all-start.3) | async-done | bytes 2490400 | tf_op jit(solution)/shard_map/all_to_all | solution.py:37
  198.4 24.2 %all_to_all.35.home_ref = bf16[32,144,128]{2,1,0:T(8,128)(2,1)} all-to-all(bf16[32,144,128]{2,1,0:T(8,128)(2,1)} %get-tuple-element.54), channel_id=1, replica_groups=mesh['pipe'=4,'x'=4,'zh'=2,'y'=4,'core'=2] {'x','y','core'}, dimensions={0} | all-to-all | bytes 2359296 | tf_op jit(solution)/shard_map/all_to_all | solution.py:37
  229.5 6.1 %collective-permute-start.8 = (f32[64,256]{1,0:T(8,128)}, f32[64,256]{1,0:T(8,128)S(1)}, u32[]{:S(2)}, u32[]{:S(2)}) collective-permute-start(f32[64,256]{1,0:T(8,128)} %shard_map.193.near_note_ref), channel_id=1, source_target_pairs={{0,8},{8,0},{1,9},{9,1},{2,10},{10,2},{3,11},{11,3},{4,12},{12,4},... | collective-permute-start | bytes 196616 | tf_op jit(solution)/shard_map/ppermute | solution.py:41
  235.6 5.7 %shard_map.194 = (f32[128,2048]{1,0:T(8,128)}, bf16[128,2048]{1,0:T(8,128)(2,1)}, f32[8,256]{1,0:T(8,128)}, f32[8,256]{1,0:T(8,128)}) custom-call(s32[1]{0:T(128)} %bitcast.zh_ref, bf16[32,152,256]{2,1,0:T(8,128)(2,1)} %all-to-all-done.3.home_ref, bf16[288,128]{1,0:T(8,128)(2,1)} %get-tuple-element.64.near_hot_ref, ...), custom_call_target="tpu_custom_call" | custom-call | flops 1000000000 | bytes 6291456 | tf_op jit(solution)/shard_map/pallas_call | solution.py:58
  251.7 34.0 %collective-permute-done.11.theirs_ref = f32[8,256]{1,0:T(8,128)S(1)} collective-permute-done((f32[8,256]{1,0:T(8,128)S(1)}, f32[8,256]{1,0:T(8,128)S(1)}, u32[]{:S(2)}, u32[]{:S(2)}) %collective-permute-start.11) | collective-permute-done | bytes 8224 | tf_op jit(solution)/shard_map/ppermute | solution.py:41
  295.4 8.8 %all-to-all-start.6 = ((bf16[32,32,128]{2,1,0:T(8,128)(2,1)}), bf16[32,32,128]{2,1,0:T(8,128)(2,1)S(1)}, u32[]{:S(2)}, u32[]{:S(2)}) async-start(bf16[32,32,128]{2,1,0:T(8,128)(2,1)} %bitcast.32), calls=%async_computation.6 | async-start | bytes 524288 | tf_op jit(solution)/shard_map/all_to_all | solution.py:37
  304.2 7.7 %collective-permute-start.7 = (bf16[128,1024]{1,0:T(8,128)(2,1)}, bf16[128,1024]{1,0:T(8,128)(2,1)}, u32[]{:S(2)}, u32[]{:S(2)}) collective-permute-start(bf16[128,1024]{1,0:T(8,128)(2,1)} %get-tuple-element.62), channel_id=1, source_target_pairs={{0,72},{8,64},{64,136},{72,128},{128,200},{136,192},{192,8},{200,0... | collective-permute-start | bytes 786440 | tf_op jit(solution)/shard_map/ppermute | solution.py:50
  316.2 17.6 %collective-permute-done.7.d_ref = bf16[128,1024]{1,0:T(8,128)(2,1)} collective-permute-done((bf16[128,1024]{1,0:T(8,128)(2,1)}, bf16[128,1024]{1,0:T(8,128)(2,1)}, u32[]{:S(2)}, u32[]{:S(2)}) %collective-permute-start.7) | collective-permute-done | bytes 262176 | tf_op jit(solution)/shard_map/ppermute | solution.py:50
  (55 shorter events, 40.2 us)
Async XLA Ops:
  11.5 8.8 %copy-start.1 = (bf16[1,128,2048]{2,1,0:T(8,128)(2,1)S(1)}, bf16[1,128,2048]{2,1,0:T(8,128)(2,1)}, u32[]{:S(2)}) copy-start(bf16[1,128,2048]{2,1,0:T(8,128)(2,1)} %param.29) | copy-start | bytes 1572868
  11.5 15.8 %copy-start.5 = (bf16[1,128,2048]{2,1,0:T(8,128)(2,1)S(1)}, bf16[1,128,2048]{2,1,0:T(8,128)(2,1)}, u32[]{:S(2)}) copy-start(bf16[1,128,2048]{2,1,0:T(8,128)(2,1)} %param.31) | copy-start | bytes 1572868
  11.5 15.9 %copy-start.3 = (s32[1,128,4]{1,2,0:T(4,128)S(1)}, s32[1,128,4]{1,2,0:T(4,128)}, u32[]{:S(2)}) copy-start(s32[1,128,4]{1,2,0:T(4,128)} %param.30) | copy-start | bytes 6148
  11.5 15.9 %copy-start.4 = (s32[1,128,4]{1,2,0:T(4,128)S(1)}, s32[1,128,4]{1,2,0:T(4,128)}, u32[]{:S(2)}) copy-start(s32[1,128,4]{1,2,0:T(4,128)} %param.28) | copy-start | bytes 6148
  11.6 52.7 %all-to-all-start = ((bf16[32,216,256]{2,1,0:T(8,128)(2,1)}), bf16[32,216,256]{2,1,0:T(8,128)(2,1)}, u32[]{:S(2)}, u32[]{:S(2)}) async-start(bf16[32,216,256]{2,1,0:T(8,128)(2,1)} %get-tuple-element.42), calls=%async_computation | async-start | bytes 7077888 | tf_op jit(solution)/shard_map/all_to_all | solution.py:37
  20.3 36.9 %collective-permute-start.2 = (bf16[128,2048]{1,0:T(8,128)(2,1)S(1)}, bf16[128,2048]{1,0:T(8,128)(2,1)S(1)}, u32[]{:S(2)}, u32[]{:S(2)}) collective-permute-start(bf16[128,2048]{1,0:T(8,128)(2,1)S(1)} %bitcast.31), channel_id=1, source_target_pairs={{0,8},{8,0},{1,9},{9,1},{2,10},{10,2},{3,11},{11,3},{4,12},{12,4},... | collective-permute-start | bytes 1572872 | tf_op jit(solution)/shard_map/ppermute | solution.py:41
  27.3 30.7 %collective-permute-start.3 = (bf16[128,2048]{1,0:T(8,128)(2,1)S(1)}, bf16[128,2048]{1,0:T(8,128)(2,1)S(1)}, u32[]{:S(2)}, u32[]{:S(2)}) collective-permute-start(bf16[128,2048]{1,0:T(8,128)(2,1)S(1)} %bitcast.50), channel_id=1, source_target_pairs={{0,8},{8,0},{1,9},{9,1},{2,10},{10,2},{3,11},{11,3},{4,12},{12,4},... | collective-permute-start | bytes 1572872 | tf_op jit(solution)/shard_map/ppermute | solution.py:41
  27.5 29.2 %collective-permute-start = (s32[8,128]{1,0:T(8,128)S(1)}, s32[8,128]{1,0:T(8,128)S(1)}, u32[]{:S(2)}, u32[]{:S(2)}) collective-permute-start(s32[8,128]{1,0:T(8,128)S(1)} %pad_add_fusion), channel_id=1, source_target_pairs={{0,8},{8,0},{1,9},{9,1},{2,10},{10,2},{3,11},{11,3},{4,12},{12,4},... | collective-permute-start | bytes 12296 | tf_op jit(solution)/shard_map/ppermute | solution.py:41
  64.3 23.2 %copy-start.6 = (bf16[128,2048]{1,0:T(8,128)(2,1)S(1)}, bf16[128,2048]{1,0:T(8,128)(2,1)}, u32[]{:S(2)}) copy-start(bf16[128,2048]{1,0:T(8,128)(2,1)} %shard_map.183.resid_ref) | copy-start | bytes 1572868
  64.3 54.4 %all-to-all-start.1 = ((bf16[32,144,256]{2,1,0:T(8,128)(2,1)}), bf16[32,144,256]{2,1,0:T(8,128)(2,1)}, u32[]{:S(2)}, u32[]{:S(2)}) async-start(bf16[32,144,256]{2,1,0:T(8,128)(2,1)} %get-tuple-element.45), calls=%async_computation.1 | async-start | bytes 4718592 | tf_op jit(solution)/shard_map/all_to_all | solution.py:37
  87.5 20.0 %collective-permute-start.1 = (bf16[128,2048]{1,0:T(8,128)(2,1)S(1)}, bf16[128,2048]{1,0:T(8,128)(2,1)S(1)}, u32[]{:S(2)}, u32[]{:S(2)}) collective-permute-start(bf16[128,2048]{1,0:T(8,128)(2,1)S(1)} %copy-done.6), channel_id=1, source_target_pairs={{0,8},{8,0},{1,9},{9,1},{2,10},{10,2},{3,11},{11,3},{4,12},{12,4},... | collective-permute-start | bytes 1572872 | tf_op jit(solution)/shard_map/ppermute | solution.py:41
  118.7 39.7 %all-to-all-start.2 = ((bf16[32,72,256]{2,1,0:T(8,128)(2,1)}), bf16[32,72,256]{2,1,0:T(8,128)(2,1)}, u32[]{:S(2)}, u32[]{:S(2)}) async-start(bf16[32,72,256]{2,1,0:T(8,128)(2,1)} %get-tuple-element.49), calls=%async_computation.2 | async-start | bytes 2359296 | tf_op jit(solution)/shard_map/all_to_all | solution.py:37
  158.4 40.1 %all-to-all-start.3 = ((bf16[32,152,256]{2,1,0:T(8,128)(2,1)}), bf16[32,152,256]{2,1,0:T(8,128)(2,1)}, u32[]{:S(2)}, u32[]{:S(2)}) async-start(bf16[32,152,256]{2,1,0:T(8,128)(2,1)} %shard_map.188), calls=%async_computation.3 | async-start | bytes 4980736 | tf_op jit(solution)/shard_map/all_to_all | solution.py:37
  222.6 69.7 %all-to-all-start.5 = ((bf16[32,144,128]{2,1,0:T(8,128)(2,1)}), bf16[32,144,128]{2,1,0:T(8,128)(2,1)}, u32[]{:S(2)}, u32[]{:S(2)}) async-start(bf16[32,144,128]{2,1,0:T(8,128)(2,1)} %get-tuple-element.60), calls=%async_computation.5 | async-start | bytes 2359296 | tf_op jit(solution)/shard_map/all_to_all | solution.py:37
  229.5 11.9 %collective-permute-start.8 = (f32[64,256]{1,0:T(8,128)}, f32[64,256]{1,0:T(8,128)S(1)}, u32[]{:S(2)}, u32[]{:S(2)}) collective-permute-start(f32[64,256]{1,0:T(8,128)} %shard_map.193.near_note_ref), channel_id=1, source_target_pairs={{0,8},{8,0},{1,9},{9,1},{2,10},{10,2},{3,11},{11,3},{4,12},{12,4},... | collective-permute-start | bytes 196616 | tf_op jit(solution)/shard_map/ppermute | solution.py:41
  241.3 6.0 %copy-start.10 = (f32[8,256]{1,0:T(8,128)S(1)}, f32[8,256]{1,0:T(8,128)}, u32[]{:S(2)}) copy-start(f32[8,256]{1,0:T(8,128)} %get-tuple-element.74) | copy-start | bytes 24580
  241.3 62.8 %collective-permute-start.10 = (bf16[128,2048]{1,0:T(8,128)(2,1)}, bf16[128,2048]{1,0:T(8,128)(2,1)S(1)}, u32[]{:S(2)}, u32[]{:S(2)}) collective-permute-start(bf16[128,2048]{1,0:T(8,128)(2,1)} %get-tuple-element.70), channel_id=1, source_target_pairs={{0,200},{8,192},{64,8},{72,0},{128,72},{136,64},{192,136},{200,128... | collective-permute-start | bytes 1572872 | tf_op jit(solution)/shard_map/ppermute | solution.py:50
  245.1 66.8 %collective-permute-start.9 = (bf16[128,2048]{1,0:T(8,128)(2,1)}, bf16[128,2048]{1,0:T(8,128)(2,1)}, u32[]{:S(2)}, u32[]{:S(2)}) collective-permute-start(bf16[128,2048]{1,0:T(8,128)(2,1)} %get-tuple-element.69), channel_id=1, source_target_pairs={{0,192},{8,200},{64,0},{72,8},{128,64},{136,72},{192,128},{200,136... | collective-permute-start | bytes 1572872 | tf_op jit(solution)/shard_map/ppermute | solution.py:50
  247.3 38.4 %collective-permute-start.11 = (f32[8,256]{1,0:T(8,128)S(1)}, f32[8,256]{1,0:T(8,128)S(1)}, u32[]{:S(2)}, u32[]{:S(2)}) collective-permute-start(f32[8,256]{1,0:T(8,128)S(1)} %copy-done.10), channel_id=1, source_target_pairs={{0,8},{8,0},{1,9},{9,1},{2,10},{10,2},{3,11},{11,3},{4,12},{12,4},... | collective-permute-start | bytes 24584 | tf_op jit(solution)/shard_map/ppermute | solution.py:41
  292.3 23.9 %collective-permute-start.4 = (bf16[128,1024]{1,0:T(8,128)(2,1)}, bf16[128,1024]{1,0:T(8,128)(2,1)}, u32[]{:S(2)}, u32[]{:S(2)}) collective-permute-start(bf16[128,1024]{1,0:T(8,128)(2,1)} %get-tuple-element.58), channel_id=1, source_target_pairs={{0,64},{8,72},{64,128},{72,136},{128,192},{136,200},{192,0},{200,8... | collective-permute-start | bytes 786440 | tf_op jit(solution)/shard_map/ppermute | solution.py:50
  292.3 23.9 %collective-permute-start.5 = (bf16[128,1024]{1,0:T(8,128)(2,1)}, bf16[128,1024]{1,0:T(8,128)(2,1)}, u32[]{:S(2)}, u32[]{:S(2)}) collective-permute-start(bf16[128,1024]{1,0:T(8,128)(2,1)} %get-tuple-element.59), channel_id=1, source_target_pairs={{0,72},{8,64},{64,136},{72,128},{128,200},{136,192},{192,8},{200,0... | collective-permute-start | bytes 786440 | tf_op jit(solution)/shard_map/ppermute | solution.py:50
  295.4 38.4 %collective-permute-start.6 = (bf16[128,1024]{1,0:T(8,128)(2,1)}, bf16[128,1024]{1,0:T(8,128)(2,1)}, u32[]{:S(2)}, u32[]{:S(2)}) collective-permute-start(bf16[128,1024]{1,0:T(8,128)(2,1)} %get-tuple-element.61), channel_id=1, source_target_pairs={{0,64},{8,72},{64,128},{72,136},{128,192},{136,200},{192,0},{200,8... | collective-permute-start | bytes 786440 | tf_op jit(solution)/shard_map/ppermute | solution.py:50
  295.4 18.5 %all-to-all-start.6 = ((bf16[32,32,128]{2,1,0:T(8,128)(2,1)}), bf16[32,32,128]{2,1,0:T(8,128)(2,1)S(1)}, u32[]{:S(2)}, u32[]{:S(2)}) async-start(bf16[32,32,128]{2,1,0:T(8,128)(2,1)} %bitcast.32), calls=%async_computation.6 | async-start | bytes 524288 | tf_op jit(solution)/shard_map/all_to_all | solution.py:37
  304.2 29.6 %collective-permute-start.7 = (bf16[128,1024]{1,0:T(8,128)(2,1)}, bf16[128,1024]{1,0:T(8,128)(2,1)}, u32[]{:S(2)}, u32[]{:S(2)}) collective-permute-start(bf16[128,1024]{1,0:T(8,128)(2,1)} %get-tuple-element.62), channel_id=1, source_target_pairs={{0,72},{8,64},{64,136},{72,128},{128,200},{136,192},{192,8},{200,0... | collective-permute-start | bytes 786440 | tf_op jit(solution)/shard_map/ppermute | solution.py:50
  (6 other events, 4.4 us)
